TPU v7x, 32 devices: a whole 2x2x4 slice. The times are simulated.
32 devices in a mesh: snap: 2 (over x), dom: 16 (over z, y, core).
Axes of the slice: x: 2, y: 2, z: 4, core: 2. Of those that a mesh axis runs over, the one named last changes fastest.
Arguments:
- features: bfloat16 [4, 18432, 128], P('snap', 'dom'), may hold values from -6 to 6
- adjacency: bfloat16 [4, 18432, 4, 128], P('snap', 'dom'), may hold values from -0.25 to 0.25
- block_cols: int32 [4, 144, 4], P('snap', 'dom'), may hold values from 0 to 24, as said below
- send_lists: int32 [4, 16, 16], P('snap', 'dom'), may hold values from -1 to 8, as said below
- receive_lists: int32 [4, 16, 16], P('snap', 'dom'), may hold values from -1 to 8, as said below
- spatial_weight: bfloat16 [128, 128], replicated, may hold values from -0.5 to 0.5
- temporal_weight: bfloat16 [3, 128, 256], replicated, may hold values from -0.3125 to 0.3125
- temporal_bias: float32 [256], replicated, may hold values from -3 to 3
- cotangent: bfloat16 [4, 18432, 128], P('snap', 'dom'), may hold values from -6 to 6
Outputs:
- output: bfloat16 [4, 18432, 128], P('snap', 'dom')
- input_grad: bfloat16 [4, 18432, 128], P('snap', 'dom')
Inputs may be any that keep to these rules, and one draw needn't show every extreme that they name: receive_lists[s, d, p] is the local index, within partition p, of the one block of 128 items that partition d receives from p in snapshot s, or -1 if none; each partition receives from exactly 15 other partitions and never from itself. send_lists[s, p, d] = receive_lists[s, d, p]: at most one block goes from one partition to another in a snapshot. `block_cols`: for row block r, slot 0 holds r mod 9, its own block; every other slot holds 9 + p for a partition p from which r's partition receives a block in that snapshot, and each such block is named by some slot of the partition.
All inputs are finite; a program needn't handle non-finite values.
Results may differ from a plain program's by a relative error of at most 0.012.
Values may be sent and summed in bfloat16 or wider, within the bound.
No kernel may reach another device: no remote copies, remote signals or barrier semaphores. Data moves between devices by JAX's collectives and lax.ppermute only.
A program may use at most 64 MiB of HBM per device.

v0:
```python
import jax
import jax.numpy as jnp
from jax import lax
from jax.sharding import PartitionSpec as P


def pad_time(values):
    return jnp.pad(values, ((1, 1), (0, 0), (0, 0)))


def to_items(values):
    return lax.all_to_all(values, "snap", split_axis=1, concat_axis=0, tiled=True)


def to_snaps(values):
    return lax.all_to_all(values, "snap", split_axis=0, concat_axis=1, tiled=True)


def gate_terms(padded, temporal_weight, temporal_bias):
    length = padded.shape[0] - 2
    row_count = padded.shape[1]
    channels = padded.shape[2]
    running = jnp.zeros((length * row_count, temporal_weight.shape[2]), jnp.float32)
    for offset in range(temporal_weight.shape[0]):
        window = padded[offset : offset + length].reshape(length * row_count, channels)
        running = running + jnp.dot(
            window, temporal_weight[offset], preferred_element_type=jnp.float32
        )
    return (running + temporal_bias).reshape(length, row_count, -1)


def gate_forward(mixture, channels):
    linear = mixture[..., :channels]
    gate_value = jax.nn.sigmoid(mixture[..., channels:])
    return ((linear * gate_value).astype(jnp.bfloat16), linear, gate_value)


def gate_backward(upstream, linear, gate_value):
    upstream_f = upstream.astype(jnp.float32)
    return jnp.concatenate(
        [upstream_f * gate_value, upstream_f * linear * gate_value * (1.0 - gate_value)], axis=-1
    ).astype(jnp.bfloat16)


def spread_back(padded_grad, temporal_weight):
    length = padded_grad.shape[0] - 2
    row_count = padded_grad.shape[1]
    doubled = padded_grad.shape[2]
    channels = temporal_weight.shape[1]
    taps_count = temporal_weight.shape[0]
    running = jnp.zeros((length * row_count, channels), jnp.float32)
    for offset in range(taps_count):
        start = taps_count - 1 - offset
        window = padded_grad[start : start + length].reshape(length * row_count, doubled)
        running = running + lax.dot_general(
            window,
            temporal_weight[offset],
            (((1,), (1,)), ((), ())),
            preferred_element_type=jnp.float32,
        )
    return running.reshape(length, row_count, channels).astype(jnp.bfloat16)


def local(
    features,
    adjacency,
    block_cols,
    send_lists,
    receive_lists,
    spatial_weight,
    temporal_weight,
    temporal_bias,
    cotangent,
):
    domains = lax.axis_size("dom")
    snaps_here, items_here, channels = features.shape
    slot_count = adjacency.shape[2]
    block_size = adjacency.shape[3]
    blocks_here = items_here // block_size
    frame_size = blocks_here + domains
    own_blocks = features.reshape(snaps_here, blocks_here, block_size, channels)
    adjacency_tiles = adjacency.reshape(snaps_here, blocks_here, block_size, slot_count, block_size)
    wanted = send_lists[:, 0, :]
    selector = (wanted[:, :, None] == jnp.arange(blocks_here)[None, None, :]).astype(jnp.bfloat16)
    outgoing = jnp.einsum(
        "sqn,snbc->sqbc", selector, own_blocks, preferred_element_type=jnp.float32
    ).astype(jnp.bfloat16)
    arrived = lax.all_to_all(outgoing, "dom", split_axis=1, concat_axis=1, tiled=True)
    snap_rows = jnp.arange(snaps_here)[:, None, None]
    extended = jnp.concatenate([own_blocks, arrived], axis=1)
    neighbours = extended[snap_rows, block_cols]
    aggregated = jnp.einsum(
        "sjrkc,sjkcd->sjrd", adjacency_tiles, neighbours, preferred_element_type=jnp.float32
    )
    aggregated = aggregated.astype(jnp.bfloat16).reshape(snaps_here * items_here, channels)
    hidden = jnp.dot(aggregated, spatial_weight, preferred_element_type=jnp.float32).astype(
        jnp.bfloat16
    )
    hidden = hidden.reshape(snaps_here, items_here, channels)
    hidden_items = to_items(hidden)
    mixture = gate_terms(pad_time(hidden_items), temporal_weight, temporal_bias)
    output_items, linear, gate_value = gate_forward(mixture, channels)
    output = to_snaps(output_items)
    gate_grad = gate_backward(to_items(cotangent), linear, gate_value)
    hidden_grad = to_snaps(spread_back(pad_time(gate_grad), temporal_weight))
    aggregate_grad = lax.dot_general(
        hidden_grad.reshape(snaps_here * items_here, channels),
        spatial_weight,
        (((1,), (1,)), ((), ())),
        preferred_element_type=jnp.float32,
    ).astype(jnp.bfloat16)
    aggregate_grad = aggregate_grad.reshape(snaps_here, blocks_here, block_size, channels)
    contribution = jnp.einsum(
        "sjrkc,sjrd->sjkcd", adjacency_tiles, aggregate_grad, preferred_element_type=jnp.float32
    )
    placing = (block_cols[..., None] == jnp.arange(frame_size)[None, None, None, :]).astype(
        jnp.float32
    )
    framed = jnp.einsum(
        "sjkf,sjkcd->sfcd",
        placing,
        contribution,
        precision=lax.Precision.HIGHEST,
        preferred_element_type=jnp.float32,
    )
    returned = lax.all_to_all(
        framed[:, blocks_here:].astype(jnp.bfloat16), "dom", split_axis=1, concat_axis=1, tiled=True
    )
    input_grad = framed[:, :blocks_here] + jnp.einsum(
        "sqn,sqbc->snbc", selector, returned, preferred_element_type=jnp.float32
    )
    return (output, input_grad.reshape(snaps_here, items_here, channels).astype(jnp.bfloat16))


def solution(mesh):
    return jax.shard_map(
        local,
        mesh=mesh,
        in_specs=(
            P("snap", "dom", None),
            P("snap", "dom", None, None),
            P("snap", "dom", None),
            P("snap", "dom", None),
            P("snap", "dom", None),
            P(),
            P(),
            P(),
            P("snap", "dom", None),
        ),
        out_specs=(P("snap", "dom", None), P("snap", "dom", None)),
        check_vma=False,
    )
```

profile of v0, /device:TPU:0, one launch (start us, length us, event | category | flops | bytes accessed | tf_op | source)
XLA Modules:
  0.0 139.7 jit_solution(9423234578631463373)
XLA Ops:
  0.6 0.0 copy-start
  0.6 1.7 %convolution_convert_fusion.2 = bf16[2,16,128,128]{3,1,2,0:T(8,128)(2,1)S(1)} fusion(bf16[2,9,128,128]{3,2,1,0:T(8,128)(2,1)} %bitcast.114, s32[2,16]{1,0:T(2,128)} %bitcast.131), kind=kOutput, calls=%fused_computation.24 | convolution fusion | flops 9961760 | bytes 1638528 | tf_op jit(solution)/shard_map/sqn,snbc->sqbc/dot_general | solution.py:85
  2.3 0.0 copy-start.6
  2.3 0.0 copy-start.5
  2.3 1.3 copy.42
  3.6 0.0 copy-start.2
  3.6 7.5 %all-to-all-start = ((bf16[2,16,128,128]{3,2,0,1:T(8,128)(2,1)}), bf16[2,16,128,128]{3,2,0,1:T(8,128)(2,1)S(1)}, u32[]{:S(2)}, u32[]{:S(2)}) async-start(bf16[2,16,128,128]{3,2,0,1:T(8,128)(2,1)} %copy.42), calls=%async_computation | async-start | bytes 2097152 | tf_op jit(solution)/shard_map/all_to_all | solution.py:88
  11.1 0.0 copy-done.6
  11.2 0.1 copy.44
  11.3 0.1 reshape.75
  11.3 0.0 copy-done.5
  11.4 5.6 %copy.51 = bf16[2,1152,128]{2,0,1:T(2,128)(2,1)} copy(bf16[2,1152,128]{2,1,0:T(8,128)(2,1)S(1)} %copy-done.5) | data formatting | bytes 1179648 | tf_op args[8]
  17.0 17.1 %all-to-all-done = bf16[2,16,128,128]{3,2,0,1:T(8,128)(2,1)S(1)} async-done(((bf16[2,16,128,128]{3,2,0,1:T(8,128)(2,1)}), bf16[2,16,128,128]{3,2,0,1:T(8,128)(2,1)S(1)}, u32[]{:S(2)}, u32[]{:S(2)}) %all-to-all-start) | async-done | bytes 1048608 | tf_op jit(solution)/shard_map/all_to_all | solution.py:88
  34.1 4.2 %all-to-all-start.3 = ((bf16[2,1152,128]{2,0,1:T(2,128)(2,1)}), bf16[2,1152,128]{2,0,1:T(2,128)(2,1)}, u32[]{:S(2)}, u32[]{:S(2)}) async-start(bf16[2,1152,128]{2,0,1:T(2,128)(2,1)} %copy.51), calls=%async_computation.3 | async-start | bytes 1179648 | tf_op jit(solution)/shard_map/all_to_all | solution.py:12
  38.3 0.0 copy-done.2
  38.3 0.2 pad_maximum_fusion
  38.5 2.8 %gather_fusion = bf16[72,128,128]{2,1,0:T(8,128)(2,1)} fusion(bf16[2,25,128,128]{3,2,1,0:T(8,128)(2,1)S(1)} %pad_maximum_fusion, s32[72]{0:T(128)S(1)} %reshape.75), kind=kCustom, calls=%fused_computation | custom fusion | bytes 4719168 | tf_op jit(solution)/shard_map/gather | solution.py:91
  41.4 3.1 %fusion.13 = bf16[2,9,128,128]{2,3,1,0:T(8,128)(2,1)S(1)} fusion(bf16[2,9,4,128,128]{4,3,2,1,0:T(8,128)(2,1)} %bitcast.123, bf16[2,9,128,4,128]{4,3,2,1,0:T(4,128)(2,1)} %bitcast.125), kind=kOutput, calls=%fused_computation.26 | convolution fusion | flops 302284800 | bytes 5308416 | tf_op jit(solution)/shard_map/sjrkc,sjkcd->sjrd/dot_general | solution.py:92
  44.5 0.0 copy-done
  44.5 0.3 convolution_convert_fusion.1
  44.8 5.6 %copy.46 = bf16[2,1152,128]{2,0,1:T(2,128)(2,1)} copy(bf16[2,1152,128]{2,1,0:T(8,128)(2,1)S(1)} %bitcast.120) | data formatting | bytes 1179648 | tf_op jit(solution)/shard_map/reshape | solution.py:99
  50.4 0.0 all-to-all-done.3
  50.4 3.7 %all-to-all-start.1 = ((bf16[2,1152,128]{2,0,1:T(2,128)(2,1)}), bf16[2,1152,128]{2,0,1:T(2,128)(2,1)S(1)}, u32[]{:S(2)}, u32[]{:S(2)}) async-start(bf16[2,1152,128]{2,0,1:T(2,128)(2,1)} %copy.46), calls=%async_computation.1 | async-start | bytes 1179648 | tf_op jit(solution)/shard_map/all_to_all | solution.py:12
  54.1 1.5 %convert_bitcast_fusion = f32[2,2,576,128]{3,1,2,0:T(2,128)S(1)} fusion(bf16[2,2,576,128]{3,0,2,1:T(2,128)(2,1)} %bitcast.50), kind=kLoop, calls=%fused_computation.34 | loop fusion | flops 294912 | bytes 1769472 | tf_op jit(solution)/shard_map/convert_element_type | solution.py:39
  55.6 0.1 copy.52
  55.7 8.1 %all-to-all-done.1 = bf16[2,1152,128]{2,0,1:T(2,128)(2,1)S(1)} async-done(((bf16[2,1152,128]{2,0,1:T(2,128)(2,1)}), bf16[2,1152,128]{2,0,1:T(2,128)(2,1)S(1)}, u32[]{:S(2)}, u32[]{:S(2)}) %all-to-all-start.1) | async-done | bytes 589856 | tf_op jit(solution)/shard_map/all_to_all | solution.py:12
  63.8 0.1 copy.47
  63.9 0.0 copy-start.4
  63.9 0.1 pad_slice_fusion
  64.1 0.7 copy-done.4
  64.8 0.4 fusion.34
  65.3 0.0 copy-start.8
  65.3 0.4 convolution_add_fusion.1
  65.7 0.2 copy-done.8
  65.9 0.4 fusion
  66.4 1.4 %fusion.22 = (bf16[4,576,128]{2,1,0:T(8,128)(2,1)S(1)}, bf16[4,576,128]{2,1,0:T(8,128)(2,1)S(1)}, bf16[4,576,128]{2,1,0:T(8,128)(2,1)}) fusion(f32[2,2,576,128]{3,2,1,0:T(8,128)S(1)} %copy.52, f32[4,576,256]{2,1,0:T(8,128)S(1)} %bitcast.107), kind=kLoop, calls=%fused_computation.37 | loop fusion | flops 3538944 | bytes 5308416 | tf_op jit(solution)/shard_map/convert.8
  67.8 0.2 fusion.9
  68.0 0.2 fusion.55
  68.2 0.5 fusion.32
  68.6 0.5 convolution_add_fusion.3
  69.1 0.5 fusion.1
  69.6 11.4 %all_to_all.70 = bf16[4,576,128]{2,1,0:T(8,128)(2,1)S(1)} all-to-all(bf16[4,576,128]{2,1,0:T(8,128)(2,1)S(1)} %bitcast.124), channel_id=1, replica_groups=mesh['snap'=2,'dom'=16] {'snap'}, dimensions={0} | all-to-all | bytes 1179648 | tf_op jit(solution)/shard_map/all_to_all | solution.py:16
  81.0 3.5 %all-to-all-start.2 = ((bf16[4,576,128]{2,1,0:T(8,128)(2,1)}), bf16[4,576,128]{2,1,0:T(8,128)(2,1)S(1)}, u32[]{:S(2)}, u32[]{:S(2)}) async-start(bf16[4,576,128]{2,1,0:T(8,128)(2,1)} %get-tuple-element.4), calls=%async_computation.2 | async-start | bytes 1179648 | tf_op jit(solution)/shard_map/all_to_all | solution.py:16
  84.5 0.0 copy-start.3
  84.6 0.3 convolution_convert_fusion
  84.9 1.3 copy-done.3
  86.2 3.0 %convolution_bitcast_fusion = f32[2,9,4,128,128]{3,4,2,1,0:T(8,128)} fusion(bf16[2,9,128,128,1]{3,2,4,1,0:T(8,128)(2,1)S(1)} %bitcast.127, bf16[2,9,128,4,128]{4,3,2,1,0:T(4,128)(2,1)S(1)} %bitcast.126), kind=kOutput, calls=%fused_computation.14 | convolution fusion | flops 301989888 | bytes 7667712 | tf_op jit(solution)/shard_map/sjrkc,sjrd->sjkcd/dot_general | solution.py:113
  89.2 8.8 %copy.56 = f32[2,9,4,128,128]{4,1,2,3,0:T(8,128)} copy(f32[2,9,4,128,128]{3,4,2,1,0:T(8,128)} %convolution_bitcast_fusion) | data formatting | bytes 9437184 | tf_op jit(solution)/shard_map/sjrkc,sjrd->sjkcd/dot_general | solution.py:113
  98.1 5.5 %convolution_bitcast_fusion.1 = f32[2,25,128,128]{3,1,2,0:T(8,128)S(1)} fusion(f32[2,9,4,128,128]{4,1,2,3,0:T(8,128)} %copy.56, s32[2,9,4]{1,2,0:T(4,128)S(1)} %copy-done.6), kind=kOutput, calls=%fused_computation.15 | convolution fusion | flops 353896192 | bytes 7995680 | tf_op jit(solution)/shard_map/sjkf,sjkcd->sfcd/dot_general | solution.py:119
  103.6 0.0 copy-start.1
  103.6 1.9 %copy-done.1 = f32[2,25,128,128]{3,1,2,0:T(8,128)} copy-done((f32[2,25,128,128]{3,1,2,0:T(8,128)}, f32[2,25,128,128]{3,1,2,0:T(8,128)S(1)}, u32[]{:S(2)}) %copy-start.1) | copy-done | bytes 3276824
  105.5 0.3 slice.103
  105.8 1.2 copy.57
  107.1 0.0 copy-start.7
  107.1 0.0 all-to-all-done.2
  107.1 6.3 %all-to-all-start.5 = ((bf16[2,16,128,128]{3,2,0,1:T(8,128)(2,1)}), bf16[2,16,128,128]{3,2,0,1:T(8,128)(2,1)S(1)}, u32[]{:S(2)}, u32[]{:S(2)}) async-start(bf16[2,16,128,128]{3,2,0,1:T(8,128)(2,1)} %copy.57), calls=%async_computation.5 | async-start | bytes 2097152 | tf_op jit(solution)/shard_map/all_to_all | solution.py:126
  113.4 0.9 copy.50
  114.3 22.1 %all-to-all-done.5 = bf16[2,16,128,128]{3,2,0,1:T(8,128)(2,1)S(1)} async-done(((bf16[2,16,128,128]{3,2,0,1:T(8,128)(2,1)}), bf16[2,16,128,128]{3,2,0,1:T(8,128)(2,1)S(1)}, u32[]{:S(2)}, u32[]{:S(2)}) %all-to-all-start.5) | async-done | bytes 1048608 | tf_op jit(solution)/shard_map/all_to_all | solution.py:126
  136.3 0.0 copy-done.7
  136.4 2.4 %fusion.5 = bf16[2,9,128,128]{3,1,2,0:T(8,128)(2,1)S(1)} fusion(f32[2,25,128,128]{3,1,2,0:T(8,128)} %copy-done.1, bf16[2,16,128,128]{3,2,0,1:T(8,128)(2,1)S(1)} %all-to-all-done.5, s32[2,16]{1,0:T(2,128)S(1)} %bitcast.132), kind=kOutput, calls=%fused_computation.18 | convolution fusion | flops 10027296 | bytes 2818176 | tf_op jit(solution)/shard_map/sqn,sqbc->snbc/dot_general | solution.py:129
  138.8 1.0 copy.59
  (3 shorter events, 0.1 us)
Async XLA Ops:
  0.6 43.9 %copy-start = (bf16[128,128]{1,0:T(8,128)(2,1)S(1)}, bf16[128,128]{1,0:T(8,128)(2,1)}, u32[]{:S(2)}) copy-start(bf16[128,128]{1,0:T(8,128)(2,1)} %param.13) | copy-start | bytes 98308
  2.3 8.8 %copy-start.6 = (s32[2,9,4]{1,2,0:T(4,128)S(1)}, s32[2,9,4]{1,2,0:T(4,128)}, u32[]{:S(2)}) copy-start(s32[2,9,4]{1,2,0:T(4,128)} %param.11) | copy-start | bytes 868
  2.3 9.0 %copy-start.5 = (bf16[2,1152,128]{2,1,0:T(8,128)(2,1)S(1)}, bf16[2,1152,128]{2,1,0:T(8,128)(2,1)}, u32[]{:S(2)}) copy-start(bf16[2,1152,128]{2,1,0:T(8,128)(2,1)} %param.16) | copy-start | bytes 1769476
  3.6 34.7 %copy-start.2 = (bf16[2,1152,128]{2,1,0:T(8,128)(2,1)S(1)}, bf16[2,1152,128]{2,1,0:T(8,128)(2,1)}, u32[]{:S(2)}) copy-start(bf16[2,1152,128]{2,1,0:T(8,128)(2,1)} %param.9) | copy-start | bytes 1769476
  3.6 30.5 %all-to-all-start = ((bf16[2,16,128,128]{3,2,0,1:T(8,128)(2,1)}), bf16[2,16,128,128]{3,2,0,1:T(8,128)(2,1)S(1)}, u32[]{:S(2)}, u32[]{:S(2)}) async-start(bf16[2,16,128,128]{3,2,0,1:T(8,128)(2,1)} %copy.42), calls=%async_computation | async-start | bytes 2097152 | tf_op jit(solution)/shard_map/all_to_all | solution.py:88
  34.1 16.4 %all-to-all-start.3 = ((bf16[2,1152,128]{2,0,1:T(2,128)(2,1)}), bf16[2,1152,128]{2,0,1:T(2,128)(2,1)}, u32[]{:S(2)}, u32[]{:S(2)}) async-start(bf16[2,1152,128]{2,0,1:T(2,128)(2,1)} %copy.51), calls=%async_computation.3 | async-start | bytes 1179648 | tf_op jit(solution)/shard_map/all_to_all | solution.py:12
  50.4 13.4 %all-to-all-start.1 = ((bf16[2,1152,128]{2,0,1:T(2,128)(2,1)}), bf16[2,1152,128]{2,0,1:T(2,128)(2,1)S(1)}, u32[]{:S(2)}, u32[]{:S(2)}) async-start(bf16[2,1152,128]{2,0,1:T(2,128)(2,1)} %copy.46), calls=%async_computation.1 | async-start | bytes 1179648 | tf_op jit(solution)/shard_map/all_to_all | solution.py:12
  63.9 0.9 copy-start.4
  65.3 0.7 copy-start.8
  81.0 26.1 %all-to-all-start.2 = ((bf16[4,576,128]{2,1,0:T(8,128)(2,1)}), bf16[4,576,128]{2,1,0:T(8,128)(2,1)S(1)}, u32[]{:S(2)}, u32[]{:S(2)}) async-start(bf16[4,576,128]{2,1,0:T(8,128)(2,1)} %get-tuple-element.4), calls=%async_computation.2 | async-start | bytes 1179648 | tf_op jit(solution)/shard_map/all_to_all | solution.py:16
  84.5 1.7 %copy-start.3 = (bf16[2,1152,4,128]{3,2,1,0:T(4,128)(2,1)S(1)}, bf16[2,1152,4,128]{3,2,1,0:T(4,128)(2,1)}, u32[]{:S(2)}) copy-start(bf16[2,1152,4,128]{3,2,1,0:T(4,128)(2,1)} %param.10) | copy-start | bytes 7077892
  103.6 1.9 %copy-start.1 = (f32[2,25,128,128]{3,1,2,0:T(8,128)}, f32[2,25,128,128]{3,1,2,0:T(8,128)S(1)}, u32[]{:S(2)}) copy-start(f32[2,25,128,128]{3,1,2,0:T(8,128)S(1)} %convolution_bitcast_fusion.1) | copy-start | bytes 9830404
  107.1 29.3 %copy-start.7 = (s32[2,1,16]{2,1,0:T(1,128)S(1)}, s32[2,1,16]{2,1,0:T(1,128)}, u32[]{:S(2)}) copy-start(s32[2,1,16]{2,1,0:T(1,128)} %param.12) | copy-start | bytes 388
  107.1 29.3 %all-to-all-start.5 = ((bf16[2,16,128,128]{3,2,0,1:T(8,128)(2,1)}), bf16[2,16,128,128]{3,2,0,1:T(8,128)(2,1)S(1)}, u32[]{:S(2)}, u32[]{:S(2)}) async-start(bf16[2,16,128,128]{3,2,0,1:T(8,128)(2,1)} %copy.57), calls=%async_computation.5 | async-start | bytes 2097152 | tf_op jit(solution)/shard_map/all_to_all | solution.py:126
where the time goes:
time: 142 us; the launch traced here: 140 us
  waiting for transfers between devices  47.3 us (33%)
  local copies, waits for them, and re-layouts  32.4 us (23%)
  starting transfers between devices  25.3 us (18%)
  matrix products  19.1 us (13%)
  blocking collectives  11.4 us (8%)
  other arithmetic  3.27 us (2%)
    all_to_all x1, waiting for transfers between devices, local(): lax.all_to_all(framed[:, blocks_here:].astype(jnp.bfloat16), 'dom', split...  22.1 us
    all_to_all x1, waiting for transfers between devices, local(): lax.all_to_all(outgoing, 'dom', split_axis=1, concat_axis=1, tiled=True)  17.1 us
    all_to_all x1, blocking collectives, to_snaps(): lax.all_to_all(values, 'snap', split_axis=0, concat_axis=1, tiled=True)  11.4 us
    unnamed x19, local copies, waits for them, and re-layouts  9.82 us
    dot_general x1, local copies, waits for them, and re-layouts, local(): jnp.einsum('sjrkc,sjrd->sjkcd', adjacency_tiles, aggregate_grad, preferre...  8.84 us
    all_to_all x2, waiting for transfers between devices, to_items(): lax.all_to_all(values, 'snap', split_axis=1, concat_axis=0, tiled=True)  8.12 us
    all_to_all x2, starting transfers between devices, to_items(): lax.all_to_all(values, 'snap', split_axis=1, concat_axis=0, tiled=True)  7.92 us
    all_to_all x1, starting transfers between devices, local(): lax.all_to_all(outgoing, 'dom', split_axis=1, concat_axis=1, tiled=True)  7.52 us
  transfers between devices with their start and end apart: 5, of which 3 were waited for; matrix products, arithmetic and copies ran while one was open for 28% of the time, Pallas kernels for 0%

commit v1 on v0

--- a/solution.py
+++ b/solution.py
@@ -1,7 +1,394 @@
+import functools
+
 import jax
 import jax.numpy as jnp
 from jax import lax
+from jax.experimental import pallas as pl
+from jax.experimental.pallas import tpu as pltpu
 from jax.sharding import PartitionSpec as P
+
+F32 = jnp.float32
+BF16 = jnp.bfloat16
+VMEM = pl.BlockSpec(memory_space=pltpu.VMEM)
+SMEM = pl.BlockSpec(memory_space=pltpu.SMEM)
+ANY = pl.BlockSpec(memory_space=pl.ANY)
+VMEM_LIMIT = 48 * 1024 * 1024
+
+
+def dot(a, b):
+    return jnp.dot(a, b, preferred_element_type=F32)
+
+
+def shape(dims, dtype=BF16):
+    return jax.ShapeDtypeStruct(dims, dtype)
+
+
+def call(body, outs, in_specs, out_specs, scratch=(), flops=0, moved=0):
+    return pl.pallas_call(
+        body,
+        out_shape=outs,
+        in_specs=in_specs,
+        out_specs=out_specs,
+        scratch_shapes=list(scratch),
+        compiler_params=pltpu.CompilerParams(vmem_limit_bytes=VMEM_LIMIT),
+        cost_estimate=pl.CostEstimate(flops=flops, bytes_accessed=moved, transcendentals=0),
+    )
+
+
+def inner_index():
+    return 1 - lax.axis_index("snap")
+
+
+def split_index():
+    me = lax.axis_index("dom")
+    return me // 2, lax.rem(me, 2)
+
+
+def pack_body(inner, chips, block, send, partner_send, feats, partner_feats, *rest):
+    outs, sem = rest[:chips], rest[chips]
+    chip, core = split_index()
+    snap = inner_index() if inner else 1 - inner_index()
+    copies = []
+    for offset in range(chips):
+        target = 2 * jnp.bitwise_xor(chip, offset) + core
+        for which, (lists, source) in enumerate(((send, feats), (partner_send, partner_feats))):
+            start = pl.multiple_of(jnp.maximum(lists[snap, 0, target], 0) * block, block)
+            copies.append(
+                pltpu.make_async_copy(
+                    source.at[snap, pl.ds(start, block)],
+                    outs[offset].at[which],
+                    sem.at[2 * offset + which],
+                )
+            )
+    for copy in copies:
+        copy.start()
+    for copy in copies:
+        copy.wait()
+
+
+def prep_body(slots, adj, tw, sw, rows_out, cols_out, twt, swt, wide):
+    block = adj.shape[2]
+
+    @pl.when(pl.program_id(0) == 0)
+    def _():
+        for tap in range(tw.shape[0]):
+            twt[tap] = tw[tap].astype(F32).T.astype(BF16)
+        swt[...] = sw[...].astype(F32).T.astype(BF16)
+
+    wide[...] = adj[0].astype(F32)
+    for slot in range(slots):
+        tile = wide[pl.ds(slot, block, stride=slots), :]
+        rows_out[0, 0, :, slot * block : (slot + 1) * block] = tile.astype(BF16)
+        cols_out[0, 0, slot * block : (slot + 1) * block, :] = tile.T.astype(BF16)
+
+
+def position(column, blocks_here):
+    chip, core = split_index()
+    part = jnp.clip(column - blocks_here, 0, lax.axis_size("dom") - 1)
+    return 2 * jnp.bitwise_xor(part // 2, chip) + jnp.bitwise_xor(lax.rem(part, 2), core)
+
+
+def hidden_body(inner, chips, blocks_here, slots, cols, feats, tiles, sw, *rest):
+    arrived = rest[:chips]
+    hidden, own, adj, halo, sem = rest[chips:]
+    snap = inner_index() if inner else 1 - inner_index()
+    copies = [
+        pltpu.make_async_copy(feats.at[snap], own, sem.at[chips]),
+        pltpu.make_async_copy(tiles.at[snap], adj, sem.at[chips + 1]),
+    ]
+    for offset in range(chips):
+        copies.append(
+            pltpu.make_async_copy(arrived[offset], halo.at[pl.ds(2 * offset, 2)], sem.at[offset])
+        )
+    for copy in copies:
+        copy.start()
+    for copy in copies:
+        copy.wait()
+    block = halo.shape[1]
+    for j in range(blocks_here):
+        pieces = [own[j * block : (j + 1) * block, :]]
+        for slot in range(1, slots):
+            pieces.append(halo[position(cols[snap, j, slot], blocks_here)])
+        total = dot(adj[j], jnp.concatenate(pieces, axis=0))
+        hidden[j * block : (j + 1) * block, :] = dot(total.astype(BF16), sw[...]).astype(BF16)
+
+
+def spread(snap, j, grad, cols, tiles_t, swt, local, acc, blocks_here, slots):
+    block = grad.shape[0]
+    agg = dot(grad, swt[...]).astype(BF16)
+    parts = dot(tiles_t[j], agg)
+    local[j * block : (j + 1) * block, :] = parts[:block]
+    for slot in range(1, slots):
+        at = position(cols[snap, j, slot], blocks_here)
+        acc[at] = acc[at] + parts[slot * block : (slot + 1) * block]
+
+
+def temporal_body(
+    chips, blocks_here, slots, cols, ha, hb, hn, cot, tw, twt, bias, swt, tiles_t, *rest
+):
+    shares = rest[:chips]
+    out, partial, rest_a, local, acc, adj, sem = rest[chips:]
+    ia = inner_index()
+    ib = 1 - ia
+    fetch = pltpu.make_async_copy(tiles_t.at[ib], adj, sem)
+    fetch.start()
+    flip = lax.axis_index("snap")
+    lo, hi = 2 * flip, 2 - 2 * flip
+    channels = ha.shape[1]
+    block = acc.shape[1]
+    acc[...] = jnp.zeros_like(acc)
+    fetch.wait()
+    for j in range(blocks_here):
+        rows = pl.ds(j * block, block)
+        xa, xb, xn = ha[rows, :], hb[rows, :], hn[rows, :]
+        mix_a = bias[...] + dot(xb, tw[lo]) + dot(xa, tw[1]) + dot(xn, tw[hi])
+        mix_b = bias[...] + dot(xb, tw[1]) + dot(xa, tw[hi])
+        grads = []
+        for index, mix in ((ia, mix_a), (ib, mix_b)):
+            linear = mix[:, :channels]
+            gate = jax.nn.sigmoid(mix[:, channels:])
+            out[index, rows, :] = (linear * gate).astype(BF16)
+            up = cot[index, rows, :].astype(F32)
+            first = (up * gate).astype(BF16)
+            second = (up * linear * gate * (1.0 - gate)).astype(BF16)
+            grads.append(jnp.concatenate([first, second], axis=1))
+        ga, gb = grads
+        partial[rows, :] = dot(ga, twt[hi]).astype(BF16)
+        rest_a[rows, :] = dot(ga, twt[1]) + dot(gb, twt[hi])
+        grad_b = (dot(ga, twt[lo]) + dot(gb, twt[1])).astype(BF16)
+        spread(ib, j, grad_b, cols, adj, swt, local, acc, blocks_here, slots)
+    for offset in range(chips):
+        shares[offset][...] = acc[2 * offset : 2 * offset + 2].astype(BF16)
+
+
+def inner_body(chips, blocks_here, slots, cols, rest_a, partial, swt, tiles_t, *rest):
+    shares = rest[:chips]
+    local, acc, adj, sem = rest[chips:]
+    ia = inner_index()
+    fetch = pltpu.make_async_copy(tiles_t.at[ia], adj, sem)
+    fetch.start()
+    block = acc.shape[1]
+    acc[...] = jnp.zeros_like(acc)
+    fetch.wait()
+    for j in range(blocks_here):
+        rows = pl.ds(j * block, block)
+        grad = (rest_a[rows, :] + partial[rows, :].astype(F32)).astype(BF16)
+        spread(ia, j, grad, cols, adj, swt, local, acc, blocks_here, slots)
+    for offset in range(chips):
+        shares[offset][...] = acc[2 * offset : 2 * offset + 2].astype(BF16)
+
+
+def collect_body(chips, *refs):
+    sources, out, sem = refs[:chips], refs[chips], refs[chips + 1]
+    copies = [
+        pltpu.make_async_copy(sources[offset].at[1], out.at[offset], sem.at[offset])
+        for offset in range(chips)
+    ]
+    for copy in copies:
+        copy.start()
+    for copy in copies:
+        copy.wait()
+
+
+def final_body(chips, send, local_a, local_b, swap_a, swap_b, *rest):
+    back_a, back_b = rest[:chips], rest[chips : 2 * chips]
+    out, acc = rest[2 * chips :]
+    chip, core = split_index()
+    blocks_here, block = acc.shape[0], acc.shape[1]
+    ia = inner_index()
+    for snap, local, back, swap in (
+        (ia, local_a, back_a, swap_a),
+        (1 - ia, local_b, back_b, swap_b),
+    ):
+        for n in range(blocks_here):
+            acc[n] = local[n * block : (n + 1) * block, :]
+        for offset in range(chips):
+            base = 2 * jnp.bitwise_xor(chip, offset)
+            for which in range(2):
+                if offset == 0 and which == 0:
+                    continue
+                source = base + jnp.bitwise_xor(core, which)
+                at = send[snap, 0, source]
+                value = back[offset][0] if which == 0 else swap[offset]
+
+                @pl.when(at >= 0)
+                def _():
+                    acc[at] = acc[at] + value.astype(F32)
+
+        for n in range(blocks_here):
+            out[snap, n * block : (n + 1) * block, :] = acc[n].astype(BF16)
+
+
+def local_pair(
+    features,
+    adjacency,
+    block_cols,
+    send_lists,
+    receive_lists,
+    spatial_weight,
+    temporal_weight,
+    temporal_bias,
+    cotangent,
+):
+    domains = lax.axis_size("dom")
+    chips = domains // 2
+    snaps_here, items_here, channels = features.shape
+    slots, block = adjacency.shape[2:]
+    blocks_here = items_here // block
+    taps, _, doubled = temporal_weight.shape
+    flip_core = [(i, i ^ 1) for i in range(domains)]
+    other_snap = [(0, 1), (1, 0)]
+
+    def to_chip(values, offset):
+        return lax.ppermute(values, "dom", [(i, i ^ (2 * offset)) for i in range(domains)])
+
+    partner_send = lax.ppermute(send_lists, "dom", flip_core)
+    partner_feats = lax.ppermute(features, "dom", flip_core)
+
+    pair = shape((2, block, channels))
+
+    def pack(inner):
+        return call(
+            functools.partial(pack_body, inner, chips, block),
+            [pair] * chips,
+            [SMEM, SMEM, ANY, ANY],
+            [ANY] * chips,
+            [pltpu.SemaphoreType.DMA((2 * chips,))],
+            moved=4 * chips * block * channels * 2,
+        )(send_lists, partner_send, features, partner_feats)
+
+    def exchange(payload):
+        order = sorted(range(1, chips), key=lambda o: -o)
+        got = {0: payload[0]}
+        for offset in order:
+            got[offset] = to_chip(payload[offset], offset)
+        return [got[o] for o in range(chips)]
+
+    adj_flat = adjacency.reshape(snaps_here, items_here * slots, block)
+    steps = snaps_here * blocks_here
+    tile_rows = block * slots
+    tiles, tiles_t, twt, swt = pl.pallas_call(
+        functools.partial(prep_body, slots),
+        grid=(steps,),
+        in_specs=[
+            pl.BlockSpec((1, tile_rows, block), lambda i: (i // blocks_here, i % blocks_here, 0)),
+            pl.BlockSpec((taps, channels, doubled), lambda i: (0, 0, 0)),
+            pl.BlockSpec((channels, channels), lambda i: (0, 0)),
+        ],
+        out_specs=[
+            pl.BlockSpec(
+                (1, 1, block, tile_rows), lambda i: (i // blocks_here, i % blocks_here, 0, 0)
+            ),
+            pl.BlockSpec(
+                (1, 1, tile_rows, block), lambda i: (i // blocks_here, i % blocks_here, 0, 0)
+            ),
+            pl.BlockSpec((taps, doubled, channels), lambda i: (0, 0, 0)),
+            pl.BlockSpec((channels, channels), lambda i: (0, 0)),
+        ],
+        out_shape=[
+            shape((snaps_here, blocks_here, block, tile_rows)),
+            shape((snaps_here, blocks_here, tile_rows, block)),
+            shape((taps, doubled, channels)),
+            shape((channels, channels)),
+        ],
+        scratch_shapes=[pltpu.VMEM((tile_rows, block), F32)],
+        compiler_params=pltpu.CompilerParams(vmem_limit_bytes=VMEM_LIMIT),
+        cost_estimate=pl.CostEstimate(
+            flops=0, bytes_accessed=3 * adj_flat.size * 2, transcendentals=0
+        ),
+    )(adj_flat, temporal_weight, spatial_weight)
+
+    arrived_a = exchange(pack(True))
+    arrived_b = exchange(pack(False))
+
+    def hidden_of(inner, arrived):
+        return call(
+            functools.partial(hidden_body, inner, chips, blocks_here, slots),
+            shape((items_here, channels)),
+            [SMEM, ANY, ANY, VMEM] + [ANY] * chips,
+            VMEM,
+            [
+                pltpu.VMEM((items_here, channels), BF16),
+                pltpu.VMEM((blocks_here, block, tile_rows), BF16),
+                pltpu.VMEM((domains, block, channels), BF16),
+                pltpu.SemaphoreType.DMA((chips + 2,)),
+            ],
+            flops=2 * items_here * channels * (tile_rows + channels),
+            moved=items_here * tile_rows * 2 + 2 * items_here * channels * 2,
+        )(block_cols, features, tiles, spatial_weight, *arrived)
+
+    hidden_a = hidden_of(True, arrived_a)
+    hidden_n = lax.ppermute(hidden_a, "snap", other_snap)
+    hidden_b = hidden_of(False, arrived_b)
+
+    acc_scratch = [
+        pltpu.VMEM((domains, block, channels), F32),
+        pltpu.VMEM((blocks_here, tile_rows, block), BF16),
+        pltpu.SemaphoreType.DMA,
+    ]
+    results = call(
+        functools.partial(temporal_body, chips, blocks_here, slots),
+        [pair] * chips
+        + [
+            shape((snaps_here, items_here, channels)),
+            shape((items_here, channels)),
+            shape((items_here, channels), F32),
+            shape((items_here, channels), F32),
+        ],
+        [SMEM] + [VMEM] * 8 + [ANY],
+        [VMEM] * (chips + 4),
+        acc_scratch,
+        flops=30 * items_here * channels * channels,
+        moved=20 * items_here * channels * 2,
+    )(
+        block_cols,
+        hidden_a,
+        hidden_b,
+        hidden_n,
+        cotangent,
+        temporal_weight,
+        twt,
+        temporal_bias.reshape(1, doubled),
+        swt,
+        tiles_t,
+    )
+    shares_b, (output, partial, rest_a, local_b) = results[:chips], results[chips:]
+    partial_n = lax.ppermute(partial, "snap", other_snap)
+    back_b = exchange(shares_b)
+
+    results = call(
+        functools.partial(inner_body, chips, blocks_here, slots),
+        [pair] * chips + [shape((items_here, channels), F32)],
+        [SMEM] + [VMEM] * 3 + [ANY],
+        [VMEM] * (chips + 1),
+        acc_scratch,
+        flops=10 * items_here * channels * channels,
+        moved=12 * items_here * channels * 2,
+    )(block_cols, rest_a, partial_n, swt, tiles_t)
+    shares_a, local_a = results[:chips], results[chips]
+    back_a = exchange(shares_a)
+
+    def swap(back):
+        mine = call(
+            functools.partial(collect_body, chips),
+            shape((chips, block, channels)),
+            [ANY] * chips,
+            ANY,
+            [pltpu.SemaphoreType.DMA((chips,))],
+            moved=2 * chips * block * channels * 2,
+        )(*back)
+        return lax.ppermute(mine, "dom", flip_core)
+
+    input_grad = call(
+        functools.partial(final_body, chips),
+        shape((snaps_here, items_here, channels)),
+        [SMEM] + [VMEM] * (4 + 2 * chips),
+        VMEM,
+        [pltpu.VMEM((blocks_here, block, channels), F32)],
+        flops=40 * block * channels,
+        moved=12 * items_here * channels * 2,
+    )(send_lists, local_a, local_b, swap(back_a), swap(back_b), *back_a, *back_b)
+    return output, input_grad
 
 
 def pad_time(values):
@@ -61,7 +448,7 @@
     return running.reshape(length, row_count, channels).astype(jnp.bfloat16)
 
 
-def local(
+def local_any(
     features,
     adjacency,
     block_cols,
@@ -133,8 +520,9 @@
 
 
 def solution(mesh):
+    paired = mesh.shape["snap"] == 2 and mesh.shape["dom"] == 16
     return jax.shard_map(
-        local,
+        local_pair if paired else local_any,
         mesh=mesh,
         in_specs=(
             P("snap", "dom", None),

time: 142 us -> 104 us (0.73); the launches traced: 140 us -> 103 us
  Pallas kernels: 0 us -> 32.9 us
  waiting for transfers between devices: 47.3 us -> 16.5 us
  local copies, waits for them, and re-layouts: 32.4 us -> 5.65 us
  starting transfers between devices: 25.3 us -> 47.3 us
  matrix products: 19.1 us -> 0 us
  blocking collectives: 11.4 us -> 0 us
  other arithmetic: 3.27 us -> 0 us
    all_to_all x5 -> x0, waiting for transfers between devices: 47.3 us -> none  [the longest x1 22.1 us: local(): lax.all_to_all(framed[:, blocks_here:].astype(jnp.bfloat16), 'dom', split...]
    ppermute x0 -> x34, starting transfers between devices: none -> 47.3 us  [the longest x28 44.2 us: to_chip(): lax.ppermute(values, 'dom', [(i, i ^ 2 * offset) for i in range(domains)])]
    pallas_call x0 -> x10, Pallas kernels: none -> 32.9 us  [the longest x1 9.79 us: local_pair(): pl.pallas_call(functools.partial(prep_body, slots), grid=(steps,), in_spe...]
    all_to_all x5 -> x0, starting transfers between devices: 25.3 us -> none  [the longest x2 7.92 us: to_items(): lax.all_to_all(values, 'snap', split_axis=1, concat_axis=0, tiled=True)]
    dot_general x13 -> x0, matrix products: 19.1 us -> none  [the longest x1 5.51 us: local(): jnp.einsum('sjkf,sjkcd->sfcd', placing, contribution, precision=lax.Preci...]
    ppermute x0 -> x34, waiting for transfers between devices: none -> 16.5 us  [the longest x28 11.2 us: to_chip(): lax.ppermute(values, 'dom', [(i, i ^ 2 * offset) for i in range(domains)])]
    all_to_all x1 -> x0, blocking collectives: 11.4 us -> none  [to_snaps(): lax.all_to_all(values, 'snap', split_axis=0, concat_axis=1, tiled=True)]
    dot_general x1 -> x0, local copies, waits for them, and re-layouts: 8.84 us -> none  [local(): jnp.einsum('sjrkc,sjrd->sjkcd', adjacency_tiles, aggregate_grad, preferre...]
  transfers between devices with their start and end apart: 5 -> 34, of which waited for: 3 -> 9; matrix products, arithmetic and copies ran while one was open for 28% -> 1% of each run, Pallas kernels for 0% -> 17%
where the time goes in v1:
time: 104 us; the launch traced here: 103 us
  starting transfers between devices  47.3 us (45%)
  Pallas kernels  32.9 us (32%)
  waiting for transfers between devices  16.5 us (16%)
  local copies, waits for them, and re-layouts  5.65 us (5%)
    ppermute x28, starting transfers between devices, to_chip(): lax.ppermute(values, 'dom', [(i, i ^ 2 * offset) for i in range(domains)])  44.2 us
    ppermute x28, waiting for transfers between devices, to_chip(): lax.ppermute(values, 'dom', [(i, i ^ 2 * offset) for i in range(domains)])  11.2 us
    pallas_call x1, Pallas kernels, local_pair(): pl.pallas_call(functools.partial(prep_body, slots), grid=(steps,), in_spe...  9.79 us
    pallas_call x1, Pallas kernels, local_pair(): call(functools.partial(temporal_body, chips, blocks_here, slots), [pair]...  8.01 us
    pallas_call x2, Pallas kernels, hidden_of(): call(functools.partial(hidden_body, inner, chips, blocks_here, slots), sh...  6.84 us
    unnamed x23, local copies, waits for them, and re-layouts  5.65 us
    pallas_call x2, Pallas kernels, pack(): call(functools.partial(pack_body, inner, chips, block), [pair] * chips, [...  3.21 us
    pallas_call x1, Pallas kernels, local_pair(): call(functools.partial(inner_body, chips, blocks_here, slots), [pair] * c...  2.35 us
  transfers between devices with their start and end apart: 34, of which 9 were waited for; matrix products, arithmetic and copies ran while one was open for 1% of the time, Pallas kernels for 17%

profile of v1, /device:TPU:0, one launch (start us, length us, event | category | flops | bytes accessed | tf_op | source)
XLA Modules:
  0.0 103.2 jit_solution(16800189315995710669)
XLA Ops:
  0.6 0.5 collective-permute-start.1
  1.1 0.1 collective-permute-start
  1.2 1.8 %collective-permute-done.partner_send = s32[2,1,16]{2,1,0:T(1,128)S(1)} collective-permute-done((s32[2,1,16]{2,1,0:T(1,128)}, s32[2,1,16]{2,1,0:T(1,128)S(1)}, u32[]{:S(2)}, u32[]{:S(2)}) %collective-permute-start) | collective-permute-done | bytes 160 | tf_op jit(solution)/shard_map/ppermute | solution.py:245
  3.0 1.1 %copy-done.2 = bf16[2,1152,128]{2,1,0:T(8,128)(2,1)S(1)} copy-done((bf16[2,1152,128]{2,1,0:T(8,128)(2,1)S(1)}, bf16[2,1152,128]{2,1,0:T(8,128)(2,1)}, u32[]{:S(2)}) %copy-start.2) | copy-done | bytes 589848
  4.1 0.7 copy-done.8
  4.7 1.6 %shard_map.96 = (bf16[2,128,128]{2,1,0:T(8,128)(2,1)S(1)}, bf16[2,128,128]{2,1,0:T(8,128)(2,1)S(1)}, bf16[2,128,128]{2,1,0:T(8,128)(2,1)S(1)}, bf16[2,128,128]{2...) custom-call(s32[2,1,16]{2,1,0:T(1,128)S(1)} %copy-done.8, ...), custom_call_target="tpu_custom_call" | custom-call | bytes 1048576 | tf_op jit(solution)/shard_map/pallas_call | solution.py:251
  6.4 3.0 %collective-permute-start.2 = (bf16[2,128,128]{2,1,0:T(8,128)(2,1)S(1)}, bf16[2,128,128]{2,1,0:T(8,128)(2,1)S(1)}, u32[]{:S(2)}, u32[]{:S(2)}) collective-permute-start(bf16[2,128,128]{2,1,0:T(8,128)(2,1)S(1)} %get-tuple-element.45), channel_id=1, source_target_pairs={{0,2},{1,3},{2,0},{3,1},{4,6},{5,7},{6,4},{7,5},{8,10},{9,11},{10,... | collective-permute-start | bytes 196616 | tf_op jit(solution)/shard_map/ppermute | solution.py:243
  9.3 1.6 %collective-permute-start.3 = (bf16[2,128,128]{2,1,0:T(8,128)(2,1)S(1)}, bf16[2,128,128]{2,1,0:T(8,128)(2,1)S(1)}, u32[]{:S(2)}, u32[]{:S(2)}) collective-permute-start(bf16[2,128,128]{2,1,0:T(8,128)(2,1)S(1)} %get-tuple-element.46), channel_id=1, source_target_pairs={{0,4},{1,5},{2,6},{3,7},{4,0},{5,1},{6,2},{7,3},{8,12},{9,13},{10,... | collective-permute-start | bytes 196616 | tf_op jit(solution)/shard_map/ppermute | solution.py:243
  10.9 0.0 collective-permute-start.4
  10.9 3.0 %collective-permute-start.5 = (bf16[2,128,128]{2,1,0:T(8,128)(2,1)S(1)}, bf16[2,128,128]{2,1,0:T(8,128)(2,1)S(1)}, u32[]{:S(2)}, u32[]{:S(2)}) collective-permute-start(bf16[2,128,128]{2,1,0:T(8,128)(2,1)S(1)} %get-tuple-element.48), channel_id=1, source_target_pairs={{0,8},{1,9},{2,10},{3,11},{4,12},{5,13},{6,14},{7,15},{8,0},{9,1},... | collective-permute-start | bytes 196616 | tf_op jit(solution)/shard_map/ppermute | solution.py:243
  13.9 1.3 %collective-permute-start.6 = (bf16[2,128,128]{2,1,0:T(8,128)(2,1)S(1)}, bf16[2,128,128]{2,1,0:T(8,128)(2,1)S(1)}, u32[]{:S(2)}, u32[]{:S(2)}) collective-permute-start(bf16[2,128,128]{2,1,0:T(8,128)(2,1)S(1)} %get-tuple-element.49), channel_id=1, source_target_pairs={{0,10},{1,11},{2,8},{3,9},{4,14},{5,15},{6,12},{7,13},{8,2},{9,3},... | collective-permute-start | bytes 196616 | tf_op jit(solution)/shard_map/ppermute | solution.py:243
  15.2 3.6 %collective-permute-start.7 = (bf16[2,128,128]{2,1,0:T(8,128)(2,1)S(1)}, bf16[2,128,128]{2,1,0:T(8,128)(2,1)S(1)}, u32[]{:S(2)}, u32[]{:S(2)}) collective-permute-start(bf16[2,128,128]{2,1,0:T(8,128)(2,1)S(1)} %get-tuple-element.50), channel_id=1, source_target_pairs={{0,12},{1,13},{2,14},{3,15},{4,8},{5,9},{6,10},{7,11},{8,4},{9,5},... | collective-permute-start | bytes 196616 | tf_op jit(solution)/shard_map/ppermute | solution.py:243
  18.8 0.0 collective-permute-done.3.rest_2_
  18.8 0.0 collective-permute-start.8
  18.8 0.8 copy.12.cols
  19.6 0.9 copy-done.4
  20.5 0.8 copy-done.7
  21.2 9.8 %shard_map.95 = (bf16[2,9,128,512]{3,2,1,0:T(8,128)(2,1)S(1)}, bf16[2,9,512,128]{3,2,1,0:T(8,128)(2,1)S(1)}, bf16[3,256,128]{2,1,0:T(8,128)(2,1)S(1)}, bf16[128,128]{1,0:T(8,128)(2,1)S(1)}) custom-call(bf16[2,4608,128]{2,1,0:T(8,128)(2,1)} %bitcast.3, bf16[3,128,256]{2,1,0:T(8,128)(2,1)S(1)} %copy-done.4, bf16[128,128]{1,0:T(8,128)(2,1)S(1)} %copy-done.7), custom_call_target="tpu_custom_call" | custom-call | bytes 7077888 | tf_op jit(solution)/shard_map/pallas_call | solution.py:270
  31.0 1.4 %copy-done = bf16[2,9,512,128]{3,2,1,0:T(8,128)(2,1)} copy-done((bf16[2,9,512,128]{3,2,1,0:T(8,128)(2,1)}, bf16[2,9,512,128]{3,2,1,0:T(8,128)(2,1)S(1)}, u32[]{:S(2)}) %copy-start) | copy-done | bytes 2359320
  32.5 0.0 collective-permute-done.4.rest_3_
  32.5 0.0 collective-permute-done.5.rest_4_
  32.5 0.0 collective-permute-done.8.rest_7_
  32.5 3.4 %shard_map.97.ha = bf16[1152,128]{1,0:T(8,128)(2,1)S(1)} custom-call(s32[2,9,4]{2,1,0:T(8,128)S(1)} %copy.12.cols, bf16[2,1152,128]{2,1,0:T(8,128)(2,1)S(1)} %copy-done.3, bf16[2,9,128,512]{3,2,1,0:T(8,128)(2,1)S(1)} %get-tuple-element.43.tiles, bf16[128,128]{1,0:T(8,128)(2,1)S(1)} %copy-done.7, bf16[2,128,128]{2,1,0:T(8,128)(2,1)S(1)} %get-tuple-element.44.rest_0_, ...), custom_call_target="tpu_custom_call" | custom-call | flops 188743680 | bytes 1769472 | tf_op jit(solution)/shard_map/pallas_call | solution.py:305
  35.9 0.0 copy-start.5
  36.0 0.0 copy-start.6
  36.0 0.0 copy-start.10
  36.0 1.7 %collective-permute-start.16 = (bf16[1152,128]{1,0:T(8,128)(2,1)S(1)}, bf16[1152,128]{1,0:T(8,128)(2,1)S(1)}, u32[]{:S(2)}, u32[]{:S(2)}) collective-permute-start(bf16[1152,128]{1,0:T(8,128)(2,1)S(1)} %shard_map.97.ha), channel_id=1, source_target_pairs={{0,16},{16,0},{1,17},{17,1},{2,18},{18,2},{3,19},{19,3},{4,20},{20... | collective-permute-start | bytes 884744 | tf_op jit(solution)/shard_map/ppermute | solution.py:321
  37.7 1.6 %shard_map.98 = (bf16[2,128,128]{2,1,0:T(8,128)(2,1)S(1)}, bf16[2,128,128]{2,1,0:T(8,128)(2,1)S(1)}, bf16[2,128,128]{2,1,0:T(8,128)(2,1)S(1)}, bf16[2,128,128]{2...) custom-call(s32[2,1,16]{2,1,0:T(1,128)S(1)} %copy-done.9, ...), custom_call_target="tpu_custom_call" | custom-call | bytes 1048576 | tf_op jit(solution)/shard_map/pallas_call | solution.py:251
  39.3 1.6 %collective-permute-start.9 = (bf16[2,128,128]{2,1,0:T(8,128)(2,1)S(1)}, bf16[2,128,128]{2,1,0:T(8,128)(2,1)S(1)}, u32[]{:S(2)}, u32[]{:S(2)}) collective-permute-start(bf16[2,128,128]{2,1,0:T(8,128)(2,1)S(1)} %get-tuple-element.53), channel_id=1, source_target_pairs={{0,2},{1,3},{2,0},{3,1},{4,6},{5,7},{6,4},{7,5},{8,10},{9,11},{10,... | collective-permute-start | bytes 196616 | tf_op jit(solution)/shard_map/ppermute | solution.py:243
  40.9 2.0 %collective-permute-start.11 = (bf16[2,128,128]{2,1,0:T(8,128)(2,1)S(1)}, bf16[2,128,128]{2,1,0:T(8,128)(2,1)S(1)}, u32[]{:S(2)}, u32[]{:S(2)}) collective-permute-start(bf16[2,128,128]{2,1,0:T(8,128)(2,1)S(1)} %get-tuple-element.55), channel_id=1, source_target_pairs={{0,6},{1,7},{2,4},{3,5},{4,2},{5,3},{6,0},{7,1},{8,14},{9,15},{10,... | collective-permute-start | bytes 196616 | tf_op jit(solution)/shard_map/ppermute | solution.py:243
  42.9 2.2 %collective-permute-start.12 = (bf16[2,128,128]{2,1,0:T(8,128)(2,1)S(1)}, bf16[2,128,128]{2,1,0:T(8,128)(2,1)S(1)}, u32[]{:S(2)}, u32[]{:S(2)}) collective-permute-start(bf16[2,128,128]{2,1,0:T(8,128)(2,1)S(1)} %get-tuple-element.56), channel_id=1, source_target_pairs={{0,8},{1,9},{2,10},{3,11},{4,12},{5,13},{6,14},{7,15},{8,0},{9,1},... | collective-permute-start | bytes 196616 | tf_op jit(solution)/shard_map/ppermute | solution.py:243
  45.1 0.0 collective-permute-done.9.rest_1_
  45.1 1.7 %collective-permute-start.13 = (bf16[2,128,128]{2,1,0:T(8,128)(2,1)S(1)}, bf16[2,128,128]{2,1,0:T(8,128)(2,1)S(1)}, u32[]{:S(2)}, u32[]{:S(2)}) collective-permute-start(bf16[2,128,128]{2,1,0:T(8,128)(2,1)S(1)} %get-tuple-element.57), channel_id=1, source_target_pairs={{0,10},{1,11},{2,8},{3,9},{4,14},{5,15},{6,12},{7,13},{8,2},{9,3},... | collective-permute-start | bytes 196616 | tf_op jit(solution)/shard_map/ppermute | solution.py:243
  46.8 3.6 %collective-permute-start.14 = (bf16[2,128,128]{2,1,0:T(8,128)(2,1)S(1)}, bf16[2,128,128]{2,1,0:T(8,128)(2,1)S(1)}, u32[]{:S(2)}, u32[]{:S(2)}) collective-permute-start(bf16[2,128,128]{2,1,0:T(8,128)(2,1)S(1)} %get-tuple-element.58), channel_id=1, source_target_pairs={{0,12},{1,13},{2,14},{3,15},{4,8},{5,9},{6,10},{7,11},{8,4},{9,5},... | collective-permute-start | bytes 196616 | tf_op jit(solution)/shard_map/ppermute | solution.py:243
  50.4 0.9 collective-permute-start.15
  51.3 3.4 %collective-permute-done.13.rest_5_ = bf16[2,128,128]{2,1,0:T(8,128)(2,1)S(1)} collective-permute-done((bf16[2,128,128]{2,1,0:T(8,128)(2,1)S(1)}, bf16[2,128,128]{2,1,0:T(8,128)(2,1)S(1)}, u32[]{:S(2)}, u32[]{:S(2)}) %collective-permute-start.13) | collective-permute-done | bytes 65568 | tf_op jit(solution)/shard_map/ppermute | solution.py:243
  54.7 2.6 %collective-permute-done.15.rest_7_ = bf16[2,128,128]{2,1,0:T(8,128)(2,1)S(1)} collective-permute-done((bf16[2,128,128]{2,1,0:T(8,128)(2,1)S(1)}, bf16[2,128,128]{2,1,0:T(8,128)(2,1)S(1)}, u32[]{:S(2)}, u32[]{:S(2)}) %collective-permute-start.15) | collective-permute-done | bytes 65568 | tf_op jit(solution)/shard_map/ppermute | solution.py:243
  57.3 3.4 %shard_map.99.hb = bf16[1152,128]{1,0:T(8,128)(2,1)S(1)} custom-call(s32[2,9,4]{2,1,0:T(8,128)S(1)} %copy.12.cols, bf16[2,1152,128]{2,1,0:T(8,128)(2,1)S(1)} %copy-done.3, bf16[2,9,128,512]{3,2,1,0:T(8,128)(2,1)S(1)} %get-tuple-element.43.tiles, bf16[128,128]{1,0:T(8,128)(2,1)S(1)} %copy-done.7, bf16[2,128,128]{2,1,0:T(8,128)(2,1)S(1)} %get-tuple-element.52.rest_0_, ...), custom_call_target="tpu_custom_call" | custom-call | flops 188743680 | bytes 1769472 | tf_op jit(solution)/shard_map/pallas_call | solution.py:305
  60.8 8.0 %shard_map.100 = (bf16[2,128,128]{2,1,0:T(8,128)(2,1)S(1)}, bf16[2,128,128]{2,1,0:T(8,128)(2,1)S(1)}, bf16[2,128,128]{2,1,0:T(8,128)(2,1)S(1)}, bf16[2,128,128]{...) custom-call(s32[2,9,4]{2,1,0:T(8,128)S(1)} %copy.12.cols, ...), custom_call_target="tpu_custom_call" | custom-call | flops 566231040 | bytes 5898240 | tf_op jit(solution)/shard_map/pallas_call | solution.py:329
  68.8 0.6 collective-permute-start.17
  69.4 0.5 collective-permute-start.26
  69.9 3.0 %collective-permute-start.28 = (bf16[2,128,128]{2,1,0:T(8,128)(2,1)S(1)}, bf16[2,128,128]{2,1,0:T(8,128)(2,1)S(1)}, u32[]{:S(2)}, u32[]{:S(2)}) collective-permute-start(bf16[2,128,128]{2,1,0:T(8,128)(2,1)S(1)} %get-tuple-element.79), channel_id=1, source_target_pairs={{0,6},{1,7},{2,4},{3,5},{4,2},{5,3},{6,0},{7,1},{8,14},{9,15},{10,... | collective-permute-start | bytes 196616 | tf_op jit(solution)/shard_map/ppermute | solution.py:243
  72.9 0.7 collective-permute-start.29
  73.7 1.9 %collective-permute-done.17.partial = bf16[1152,128]{1,0:T(8,128)(2,1)S(1)} collective-permute-done((bf16[1152,128]{1,0:T(8,128)(2,1)S(1)}, bf16[1152,128]{1,0:T(8,128)(2,1)S(1)}, u32[]{:S(2)}, u32[]{:S(2)}) %collective-permute-start.17) | collective-permute-done | bytes 294944 | tf_op jit(solution)/shard_map/ppermute | solution.py:356
  75.6 0.8 collective-permute-start.30
  76.4 2.4 %shard_map.101 = (bf16[2,128,128]{2,1,0:T(8,128)(2,1)S(1)}, bf16[2,128,128]{2,1,0:T(8,128)(2,1)S(1)}, bf16[2,128,128]{2,1,0:T(8,128)(2,1)S(1)}, bf16[2,128,128]{...) custom-call(s32[2,9,4]{2,1,0:T(8,128)S(1)} %copy.12.cols, ...), custom_call_target="tpu_custom_call" | custom-call | flops 188743680 | bytes 3538944 | tf_op jit(solution)/shard_map/pallas_call | solution.py:359
  78.8 2.3 %collective-permute-start.31 = (bf16[2,128,128]{2,1,0:T(8,128)(2,1)S(1)}, bf16[2,128,128]{2,1,0:T(8,128)(2,1)S(1)}, u32[]{:S(2)}, u32[]{:S(2)}) collective-permute-start(bf16[2,128,128]{2,1,0:T(8,128)(2,1)S(1)} %get-tuple-element.82), channel_id=1, source_target_pairs={{0,12},{1,13},{2,14},{3,15},{4,8},{5,9},{6,10},{7,11},{8,4},{9,5},... | collective-permute-start | bytes 196616 | tf_op jit(solution)/shard_map/ppermute | solution.py:243
  81.1 2.4 %collective-permute-start.32 = (bf16[2,128,128]{2,1,0:T(8,128)(2,1)S(1)}, bf16[2,128,128]{2,1,0:T(8,128)(2,1)S(1)}, u32[]{:S(2)}, u32[]{:S(2)}) collective-permute-start(bf16[2,128,128]{2,1,0:T(8,128)(2,1)S(1)} %get-tuple-element.83), channel_id=1, source_target_pairs={{0,14},{1,15},{2,12},{3,13},{4,10},{5,11},{6,8},{7,9},{8,6},{9,7},... | collective-permute-start | bytes 196616 | tf_op jit(solution)/shard_map/ppermute | solution.py:243
  83.5 0.6 collective-permute-start.18
  84.2 2.9 %collective-permute-start.20 = (bf16[2,128,128]{2,1,0:T(8,128)(2,1)S(1)}, bf16[2,128,128]{2,1,0:T(8,128)(2,1)S(1)}, u32[]{:S(2)}, u32[]{:S(2)}) collective-permute-start(bf16[2,128,128]{2,1,0:T(8,128)(2,1)S(1)} %get-tuple-element.71), channel_id=1, source_target_pairs={{0,6},{1,7},{2,4},{3,5},{4,2},{5,3},{6,0},{7,1},{8,14},{9,15},{10,... | collective-permute-start | bytes 196616 | tf_op jit(solution)/shard_map/ppermute | solution.py:243
  87.0 0.4 collective-permute-start.21
  87.4 1.1 %collective-permute-done.32.refs_7_.rest_15_ = bf16[2,128,128]{2,1,0:T(8,128)(2,1)S(1)} collective-permute-done((bf16[2,128,128]{2,1,0:T(8,128)(2,1)S(1)}, bf16[2,128,128]{2,1,0:T(8,128)(2,1)S(1)}, u32[]{:S(2)}, u32[]{:S(2)}) %collective-permute-start.32) | collective-permute-done | bytes 65568 | tf_op jit(solution)/shard_map/ppermute | solution.py:243
  88.5 1.5 %collective-permute-start.22 = (bf16[2,128,128]{2,1,0:T(8,128)(2,1)S(1)}, bf16[2,128,128]{2,1,0:T(8,128)(2,1)S(1)}, u32[]{:S(2)}, u32[]{:S(2)}) collective-permute-start(bf16[2,128,128]{2,1,0:T(8,128)(2,1)S(1)} %get-tuple-element.73), channel_id=1, source_target_pairs={{0,10},{1,11},{2,8},{3,9},{4,14},{5,15},{6,12},{7,13},{8,2},{9,3},... | collective-permute-start | bytes 196616 | tf_op jit(solution)/shard_map/ppermute | solution.py:243
  90.0 2.3 %collective-permute-start.23 = (bf16[2,128,128]{2,1,0:T(8,128)(2,1)S(1)}, bf16[2,128,128]{2,1,0:T(8,128)(2,1)S(1)}, u32[]{:S(2)}, u32[]{:S(2)}) collective-permute-start(bf16[2,128,128]{2,1,0:T(8,128)(2,1)S(1)} %get-tuple-element.74), channel_id=1, source_target_pairs={{0,12},{1,13},{2,14},{3,15},{4,8},{5,9},{6,10},{7,11},{8,4},{9,5},... | collective-permute-start | bytes 196616 | tf_op jit(solution)/shard_map/ppermute | solution.py:243
  92.3 2.4 %collective-permute-start.24 = (bf16[2,128,128]{2,1,0:T(8,128)(2,1)S(1)}, bf16[2,128,128]{2,1,0:T(8,128)(2,1)S(1)}, u32[]{:S(2)}, u32[]{:S(2)}) collective-permute-start(bf16[2,128,128]{2,1,0:T(8,128)(2,1)S(1)} %get-tuple-element.75), channel_id=1, source_target_pairs={{0,14},{1,15},{2,12},{3,13},{4,10},{5,11},{6,8},{7,9},{8,6},{9,7},... | collective-permute-start | bytes 196616 | tf_op jit(solution)/shard_map/ppermute | solution.py:243
  94.7 0.4 shard_map.103
  95.1 0.1 collective-permute-start.33
  95.2 0.4 collective-permute-done.22.refs_5_.rest_5_
  95.6 0.6 collective-permute-done.23.refs_6_.rest_6_
  96.2 3.1 %collective-permute-done.24.refs_7_.rest_7_ = bf16[2,128,128]{2,1,0:T(8,128)(2,1)S(1)} collective-permute-done((bf16[2,128,128]{2,1,0:T(8,128)(2,1)S(1)}, bf16[2,128,128]{2,1,0:T(8,128)(2,1)S(1)}, u32[]{:S(2)}, u32[]{:S(2)}) %collective-permute-start.24) | collective-permute-done | bytes 65568 | tf_op jit(solution)/shard_map/ppermute | solution.py:243
  99.3 0.4 shard_map.102
  99.7 0.1 collective-permute-start.25
  99.8 1.5 %collective-permute-done.25.swap_a = bf16[8,128,128]{2,1,0:T(8,128)(2,1)S(1)} collective-permute-done((bf16[8,128,128]{2,1,0:T(8,128)(2,1)S(1)}, bf16[8,128,128]{2,1,0:T(8,128)(2,1)S(1)}, u32[]{:S(2)}, u32[]{:S(2)}) %collective-permute-start.25) | collective-permute-done | bytes 262176 | tf_op jit(solution)/shard_map/ppermute | solution.py:380
  101.3 1.9 %shard_map.104 = bf16[2,1152,128]{2,1,0:T(8,128)(2,1)} custom-call(s32[2,1,16]{2,1,0:T(1,128)S(1)} %copy-done.9, f32[1152,128]{1,0:T(8,128)S(1)} %get-tuple-element.66.local_a, f32[1152,128]{1,0:T(8,128)S(1)} %get-tuple-element.67.local_b, bf16[8,128,128]{2,1,0:T(8,128)(2,1)S(1)} %collective-permute-done.25.swap_a, ...), custom_call_target="tpu_custom_call" | custom-call | flops 655360 | bytes 3538944 | tf_op jit(solution)/shard_map/pallas_call | solution.py:382
  (37 shorter events, 0.1 us)
Async XLA Ops:
  0.6 2.4 %collective-permute-start.1 = (bf16[2,1152,128]{2,1,0:T(8,128)(2,1)}, bf16[2,1152,128]{2,1,0:T(8,128)(2,1)S(1)}, u32[]{:S(2)}, u32[]{:S(2)}) collective-permute-start(bf16[2,1152,128]{2,1,0:T(8,128)(2,1)} %feats.7), channel_id=1, source_target_pairs={{0,1},{1,0},{2,3},{3,2},{4,5},{5,4},{6,7},{7,6},{8,9},{9,8},{10,11... | collective-permute-start | bytes 1769480 | tf_op jit(solution)/shard_map/ppermute | solution.py:246
  1.1 1.8 %collective-permute-start = (s32[2,1,16]{2,1,0:T(1,128)}, s32[2,1,16]{2,1,0:T(1,128)S(1)}, u32[]{:S(2)}, u32[]{:S(2)}) collective-permute-start(s32[2,1,16]{2,1,0:T(1,128)} %send.5), channel_id=1, source_target_pairs={{0,1},{1,0},{2,3},{3,2},{4,5},{5,4},{6,7},{7,6},{8,9},{9,8},{10,11... | collective-permute-start | bytes 392 | tf_op jit(solution)/shard_map/ppermute | solution.py:245
  3.0 1.1 %copy-start.2 = (bf16[2,1152,128]{2,1,0:T(8,128)(2,1)S(1)}, bf16[2,1152,128]{2,1,0:T(8,128)(2,1)}, u32[]{:S(2)}) copy-start(bf16[2,1152,128]{2,1,0:T(8,128)(2,1)} %feats.7) | copy-start | bytes 1769476
  4.1 0.7 copy-start.8
  4.7 27.8 %copy-start.3 = (bf16[2,1152,128]{2,1,0:T(8,128)(2,1)S(1)}, bf16[2,1152,128]{2,1,0:T(8,128)(2,1)}, u32[]{:S(2)}) copy-start(bf16[2,1152,128]{2,1,0:T(8,128)(2,1)} %feats.7) | copy-start | bytes 1769476
  6.4 8.8 %collective-permute-start.2 = (bf16[2,128,128]{2,1,0:T(8,128)(2,1)S(1)}, bf16[2,128,128]{2,1,0:T(8,128)(2,1)S(1)}, u32[]{:S(2)}, u32[]{:S(2)}) collective-permute-start(bf16[2,128,128]{2,1,0:T(8,128)(2,1)S(1)} %get-tuple-element.45), channel_id=1, source_target_pairs={{0,2},{1,3},{2,0},{3,1},{4,6},{5,7},{6,4},{7,5},{8,10},{9,11},{10,... | collective-permute-start | bytes 196616 | tf_op jit(solution)/shard_map/ppermute | solution.py:243
  9.3 9.5 %collective-permute-start.3 = (bf16[2,128,128]{2,1,0:T(8,128)(2,1)S(1)}, bf16[2,128,128]{2,1,0:T(8,128)(2,1)S(1)}, u32[]{:S(2)}, u32[]{:S(2)}) collective-permute-start(bf16[2,128,128]{2,1,0:T(8,128)(2,1)S(1)} %get-tuple-element.46), channel_id=1, source_target_pairs={{0,4},{1,5},{2,6},{3,7},{4,0},{5,1},{6,2},{7,3},{8,12},{9,13},{10,... | collective-permute-start | bytes 196616 | tf_op jit(solution)/shard_map/ppermute | solution.py:243
  10.9 21.6 %collective-permute-start.4 = (bf16[2,128,128]{2,1,0:T(8,128)(2,1)S(1)}, bf16[2,128,128]{2,1,0:T(8,128)(2,1)S(1)}, u32[]{:S(2)}, u32[]{:S(2)}) collective-permute-start(bf16[2,128,128]{2,1,0:T(8,128)(2,1)S(1)} %get-tuple-element.47), channel_id=1, source_target_pairs={{0,6},{1,7},{2,4},{3,5},{4,2},{5,3},{6,0},{7,1},{8,14},{9,15},{10,... | collective-permute-start | bytes 196616 | tf_op jit(solution)/shard_map/ppermute | solution.py:243
  10.9 21.6 %collective-permute-start.5 = (bf16[2,128,128]{2,1,0:T(8,128)(2,1)S(1)}, bf16[2,128,128]{2,1,0:T(8,128)(2,1)S(1)}, u32[]{:S(2)}, u32[]{:S(2)}) collective-permute-start(bf16[2,128,128]{2,1,0:T(8,128)(2,1)S(1)} %get-tuple-element.48), channel_id=1, source_target_pairs={{0,8},{1,9},{2,10},{3,11},{4,12},{5,13},{6,14},{7,15},{8,0},{9,1},... | collective-permute-start | bytes 196616 | tf_op jit(solution)/shard_map/ppermute | solution.py:243
  13.9 18.6 %collective-permute-start.6 = (bf16[2,128,128]{2,1,0:T(8,128)(2,1)S(1)}, bf16[2,128,128]{2,1,0:T(8,128)(2,1)S(1)}, u32[]{:S(2)}, u32[]{:S(2)}) collective-permute-start(bf16[2,128,128]{2,1,0:T(8,128)(2,1)S(1)} %get-tuple-element.49), channel_id=1, source_target_pairs={{0,10},{1,11},{2,8},{3,9},{4,14},{5,15},{6,12},{7,13},{8,2},{9,3},... | collective-permute-start | bytes 196616 | tf_op jit(solution)/shard_map/ppermute | solution.py:243
  15.2 17.3 %collective-permute-start.7 = (bf16[2,128,128]{2,1,0:T(8,128)(2,1)S(1)}, bf16[2,128,128]{2,1,0:T(8,128)(2,1)S(1)}, u32[]{:S(2)}, u32[]{:S(2)}) collective-permute-start(bf16[2,128,128]{2,1,0:T(8,128)(2,1)S(1)} %get-tuple-element.50), channel_id=1, source_target_pairs={{0,12},{1,13},{2,14},{3,15},{4,8},{5,9},{6,10},{7,11},{8,4},{9,5},... | collective-permute-start | bytes 196616 | tf_op jit(solution)/shard_map/ppermute | solution.py:243
  18.8 13.7 %collective-permute-start.8 = (bf16[2,128,128]{2,1,0:T(8,128)(2,1)S(1)}, bf16[2,128,128]{2,1,0:T(8,128)(2,1)S(1)}, u32[]{:S(2)}, u32[]{:S(2)}) collective-permute-start(bf16[2,128,128]{2,1,0:T(8,128)(2,1)S(1)} %get-tuple-element.51), channel_id=1, source_target_pairs={{0,14},{1,15},{2,12},{3,13},{4,10},{5,11},{6,8},{7,9},{8,6},{9,7},... | collective-permute-start | bytes 196616 | tf_op jit(solution)/shard_map/ppermute | solution.py:243
  19.6 0.9 copy-start.4
  20.5 0.8 copy-start.7
  31.0 1.4 %copy-start = (bf16[2,9,512,128]{3,2,1,0:T(8,128)(2,1)}, bf16[2,9,512,128]{3,2,1,0:T(8,128)(2,1)S(1)}, u32[]{:S(2)}) copy-start(bf16[2,9,512,128]{3,2,1,0:T(8,128)(2,1)S(1)} %get-tuple-element.62.tiles_t) | copy-start | bytes 7077892
  32.5 5.2 %copy-start.9 = (s32[2,1,16]{2,1,0:T(1,128)S(1)}, s32[2,1,16]{2,1,0:T(1,128)}, u32[]{:S(2)}) copy-start(s32[2,1,16]{2,1,0:T(1,128)} %send.5) | copy-start | bytes 388
  35.9 24.8 %copy-start.5 = (bf16[3,128,256]{2,1,0:T(8,128)(2,1)S(1)}, bf16[3,128,256]{2,1,0:T(8,128)(2,1)}, u32[]{:S(2)}) copy-start(bf16[3,128,256]{2,1,0:T(8,128)(2,1)} %tw.3) | copy-start | bytes 589828
  36.0 24.8 %copy-start.6 = (bf16[2,1152,128]{2,1,0:T(8,128)(2,1)S(1)}, bf16[2,1152,128]{2,1,0:T(8,128)(2,1)}, u32[]{:S(2)}) copy-start(bf16[2,1152,128]{2,1,0:T(8,128)(2,1)} %cot.1) | copy-start | bytes 1769476
  36.0 24.8 %copy-start.10 = (f32[256]{0:T(256)S(1)}, f32[256]{0:T(256)}, u32[]{:S(2)}) copy-start(f32[256]{0:T(256)} %param.15) | copy-start | bytes 3076
  36.0 24.8 %collective-permute-start.16 = (bf16[1152,128]{1,0:T(8,128)(2,1)S(1)}, bf16[1152,128]{1,0:T(8,128)(2,1)S(1)}, u32[]{:S(2)}, u32[]{:S(2)}) collective-permute-start(bf16[1152,128]{1,0:T(8,128)(2,1)S(1)} %shard_map.97.ha), channel_id=1, source_target_pairs={{0,16},{16,0},{1,17},{17,1},{2,18},{18,2},{3,19},{19,3},{4,20},{20... | collective-permute-start | bytes 884744 | tf_op jit(solution)/shard_map/ppermute | solution.py:321
  39.3 5.8 %collective-permute-start.9 = (bf16[2,128,128]{2,1,0:T(8,128)(2,1)S(1)}, bf16[2,128,128]{2,1,0:T(8,128)(2,1)S(1)}, u32[]{:S(2)}, u32[]{:S(2)}) collective-permute-start(bf16[2,128,128]{2,1,0:T(8,128)(2,1)S(1)} %get-tuple-element.53), channel_id=1, source_target_pairs={{0,2},{1,3},{2,0},{3,1},{4,6},{5,7},{6,4},{7,5},{8,10},{9,11},{10,... | collective-permute-start | bytes 196616 | tf_op jit(solution)/shard_map/ppermute | solution.py:243
  40.9 5.9 %collective-permute-start.10 = (bf16[2,128,128]{2,1,0:T(8,128)(2,1)S(1)}, bf16[2,128,128]{2,1,0:T(8,128)(2,1)S(1)}, u32[]{:S(2)}, u32[]{:S(2)}) collective-permute-start(bf16[2,128,128]{2,1,0:T(8,128)(2,1)S(1)} %get-tuple-element.54), channel_id=1, source_target_pairs={{0,4},{1,5},{2,6},{3,7},{4,0},{5,1},{6,2},{7,3},{8,12},{9,13},{10,... | collective-permute-start | bytes 196616 | tf_op jit(solution)/shard_map/ppermute | solution.py:243
  40.9 9.5 %collective-permute-start.11 = (bf16[2,128,128]{2,1,0:T(8,128)(2,1)S(1)}, bf16[2,128,128]{2,1,0:T(8,128)(2,1)S(1)}, u32[]{:S(2)}, u32[]{:S(2)}) collective-permute-start(bf16[2,128,128]{2,1,0:T(8,128)(2,1)S(1)} %get-tuple-element.55), channel_id=1, source_target_pairs={{0,6},{1,7},{2,4},{3,5},{4,2},{5,3},{6,0},{7,1},{8,14},{9,15},{10,... | collective-permute-start | bytes 196616 | tf_op jit(solution)/shard_map/ppermute | solution.py:243
  42.9 8.4 %collective-permute-start.12 = (bf16[2,128,128]{2,1,0:T(8,128)(2,1)S(1)}, bf16[2,128,128]{2,1,0:T(8,128)(2,1)S(1)}, u32[]{:S(2)}, u32[]{:S(2)}) collective-permute-start(bf16[2,128,128]{2,1,0:T(8,128)(2,1)S(1)} %get-tuple-element.56), channel_id=1, source_target_pairs={{0,8},{1,9},{2,10},{3,11},{4,12},{5,13},{6,14},{7,15},{8,0},{9,1},... | collective-permute-start | bytes 196616 | tf_op jit(solution)/shard_map/ppermute | solution.py:243
  45.1 9.7 %collective-permute-start.13 = (bf16[2,128,128]{2,1,0:T(8,128)(2,1)S(1)}, bf16[2,128,128]{2,1,0:T(8,128)(2,1)S(1)}, u32[]{:S(2)}, u32[]{:S(2)}) collective-permute-start(bf16[2,128,128]{2,1,0:T(8,128)(2,1)S(1)} %get-tuple-element.57), channel_id=1, source_target_pairs={{0,10},{1,11},{2,8},{3,9},{4,14},{5,15},{6,12},{7,13},{8,2},{9,3},... | collective-permute-start | bytes 196616 | tf_op jit(solution)/shard_map/ppermute | solution.py:243
  46.8 8.0 %collective-permute-start.14 = (bf16[2,128,128]{2,1,0:T(8,128)(2,1)S(1)}, bf16[2,128,128]{2,1,0:T(8,128)(2,1)S(1)}, u32[]{:S(2)}, u32[]{:S(2)}) collective-permute-start(bf16[2,128,128]{2,1,0:T(8,128)(2,1)S(1)} %get-tuple-element.58), channel_id=1, source_target_pairs={{0,12},{1,13},{2,14},{3,15},{4,8},{5,9},{6,10},{7,11},{8,4},{9,5},... | collective-permute-start | bytes 196616 | tf_op jit(solution)/shard_map/ppermute | solution.py:243
  50.4 7.0 %collective-permute-start.15 = (bf16[2,128,128]{2,1,0:T(8,128)(2,1)S(1)}, bf16[2,128,128]{2,1,0:T(8,128)(2,1)S(1)}, u32[]{:S(2)}, u32[]{:S(2)}) collective-permute-start(bf16[2,128,128]{2,1,0:T(8,128)(2,1)S(1)} %get-tuple-element.59), channel_id=1, source_target_pairs={{0,14},{1,15},{2,12},{3,13},{4,10},{5,11},{6,8},{7,9},{8,6},{9,7},... | collective-permute-start | bytes 196616 | tf_op jit(solution)/shard_map/ppermute | solution.py:243
  60.7 15.7 %copy-start.1 = (bf16[2,9,512,128]{3,2,1,0:T(8,128)(2,1)S(1)}, bf16[2,9,512,128]{3,2,1,0:T(8,128)(2,1)}, u32[]{:S(2)}) copy-start(bf16[2,9,512,128]{3,2,1,0:T(8,128)(2,1)} %copy-done) | copy-start | bytes 7077892
  68.8 6.8 %collective-permute-start.17 = (bf16[1152,128]{1,0:T(8,128)(2,1)S(1)}, bf16[1152,128]{1,0:T(8,128)(2,1)S(1)}, u32[]{:S(2)}, u32[]{:S(2)}) collective-permute-start(bf16[1152,128]{1,0:T(8,128)(2,1)S(1)} %get-tuple-element.65), channel_id=1, source_target_pairs={{0,16},{16,0},{1,17},{17,1},{2,18},{18,2},{3,19},{19,3},{4,20},{20... | collective-permute-start | bytes 884744 | tf_op jit(solution)/shard_map/ppermute | solution.py:356
  69.4 9.4 %collective-permute-start.26 = (bf16[2,128,128]{2,1,0:T(8,128)(2,1)S(1)}, bf16[2,128,128]{2,1,0:T(8,128)(2,1)S(1)}, u32[]{:S(2)}, u32[]{:S(2)}) collective-permute-start(bf16[2,128,128]{2,1,0:T(8,128)(2,1)S(1)} %get-tuple-element.77), channel_id=1, source_target_pairs={{0,2},{1,3},{2,0},{3,1},{4,6},{5,7},{6,4},{7,5},{8,10},{9,11},{10,... | collective-permute-start | bytes 196616 | tf_op jit(solution)/shard_map/ppermute | solution.py:243
  69.9 11.2 %collective-permute-start.27 = (bf16[2,128,128]{2,1,0:T(8,128)(2,1)S(1)}, bf16[2,128,128]{2,1,0:T(8,128)(2,1)S(1)}, u32[]{:S(2)}, u32[]{:S(2)}) collective-permute-start(bf16[2,128,128]{2,1,0:T(8,128)(2,1)S(1)} %get-tuple-element.78), channel_id=1, source_target_pairs={{0,4},{1,5},{2,6},{3,7},{4,0},{5,1},{6,2},{7,3},{8,12},{9,13},{10,... | collective-permute-start | bytes 196616 | tf_op jit(solution)/shard_map/ppermute | solution.py:243
  69.9 13.6 %collective-permute-start.28 = (bf16[2,128,128]{2,1,0:T(8,128)(2,1)S(1)}, bf16[2,128,128]{2,1,0:T(8,128)(2,1)S(1)}, u32[]{:S(2)}, u32[]{:S(2)}) collective-permute-start(bf16[2,128,128]{2,1,0:T(8,128)(2,1)S(1)} %get-tuple-element.79), channel_id=1, source_target_pairs={{0,6},{1,7},{2,4},{3,5},{4,2},{5,3},{6,0},{7,1},{8,14},{9,15},{10,... | collective-permute-start | bytes 196616 | tf_op jit(solution)/shard_map/ppermute | solution.py:243
  72.9 11.2 %collective-permute-start.29 = (bf16[2,128,128]{2,1,0:T(8,128)(2,1)S(1)}, bf16[2,128,128]{2,1,0:T(8,128)(2,1)S(1)}, u32[]{:S(2)}, u32[]{:S(2)}) collective-permute-start(bf16[2,128,128]{2,1,0:T(8,128)(2,1)S(1)} %get-tuple-element.80), channel_id=1, source_target_pairs={{0,8},{1,9},{2,10},{3,11},{4,12},{5,13},{6,14},{7,15},{8,0},{9,1},... | collective-permute-start | bytes 196616 | tf_op jit(solution)/shard_map/ppermute | solution.py:243
  75.6 8.6 %collective-permute-start.30 = (bf16[2,128,128]{2,1,0:T(8,128)(2,1)S(1)}, bf16[2,128,128]{2,1,0:T(8,128)(2,1)S(1)}, u32[]{:S(2)}, u32[]{:S(2)}) collective-permute-start(bf16[2,128,128]{2,1,0:T(8,128)(2,1)S(1)} %get-tuple-element.81), channel_id=1, source_target_pairs={{0,10},{1,11},{2,8},{3,9},{4,14},{5,15},{6,12},{7,13},{8,2},{9,3},... | collective-permute-start | bytes 196616 | tf_op jit(solution)/shard_map/ppermute | solution.py:243
  78.8 8.2 %collective-permute-start.31 = (bf16[2,128,128]{2,1,0:T(8,128)(2,1)S(1)}, bf16[2,128,128]{2,1,0:T(8,128)(2,1)S(1)}, u32[]{:S(2)}, u32[]{:S(2)}) collective-permute-start(bf16[2,128,128]{2,1,0:T(8,128)(2,1)S(1)} %get-tuple-element.82), channel_id=1, source_target_pairs={{0,12},{1,13},{2,14},{3,15},{4,8},{5,9},{6,10},{7,11},{8,4},{9,5},... | collective-permute-start | bytes 196616 | tf_op jit(solution)/shard_map/ppermute | solution.py:243
  81.1 7.4 %collective-permute-start.32 = (bf16[2,128,128]{2,1,0:T(8,128)(2,1)S(1)}, bf16[2,128,128]{2,1,0:T(8,128)(2,1)S(1)}, u32[]{:S(2)}, u32[]{:S(2)}) collective-permute-start(bf16[2,128,128]{2,1,0:T(8,128)(2,1)S(1)} %get-tuple-element.83), channel_id=1, source_target_pairs={{0,14},{1,15},{2,12},{3,13},{4,10},{5,11},{6,8},{7,9},{8,6},{9,7},... | collective-permute-start | bytes 196616 | tf_op jit(solution)/shard_map/ppermute | solution.py:243
  83.5 6.5 %collective-permute-start.18 = (bf16[2,128,128]{2,1,0:T(8,128)(2,1)S(1)}, bf16[2,128,128]{2,1,0:T(8,128)(2,1)S(1)}, u32[]{:S(2)}, u32[]{:S(2)}) collective-permute-start(bf16[2,128,128]{2,1,0:T(8,128)(2,1)S(1)} %get-tuple-element.69), channel_id=1, source_target_pairs={{0,2},{1,3},{2,0},{3,1},{4,6},{5,7},{6,4},{7,5},{8,10},{9,11},{10,... | collective-permute-start | bytes 196616 | tf_op jit(solution)/shard_map/ppermute | solution.py:243
  84.1 8.1 %collective-permute-start.19 = (bf16[2,128,128]{2,1,0:T(8,128)(2,1)S(1)}, bf16[2,128,128]{2,1,0:T(8,128)(2,1)S(1)}, u32[]{:S(2)}, u32[]{:S(2)}) collective-permute-start(bf16[2,128,128]{2,1,0:T(8,128)(2,1)S(1)} %get-tuple-element.70), channel_id=1, source_target_pairs={{0,4},{1,5},{2,6},{3,7},{4,0},{5,1},{6,2},{7,3},{8,12},{9,13},{10,... | collective-permute-start | bytes 196616 | tf_op jit(solution)/shard_map/ppermute | solution.py:243
  84.2 10.9 %collective-permute-start.20 = (bf16[2,128,128]{2,1,0:T(8,128)(2,1)S(1)}, bf16[2,128,128]{2,1,0:T(8,128)(2,1)S(1)}, u32[]{:S(2)}, u32[]{:S(2)}) collective-permute-start(bf16[2,128,128]{2,1,0:T(8,128)(2,1)S(1)} %get-tuple-element.71), channel_id=1, source_target_pairs={{0,6},{1,7},{2,4},{3,5},{4,2},{5,3},{6,0},{7,1},{8,14},{9,15},{10,... | collective-permute-start | bytes 196616 | tf_op jit(solution)/shard_map/ppermute | solution.py:243
  87.0 8.2 %collective-permute-start.21 = (bf16[2,128,128]{2,1,0:T(8,128)(2,1)S(1)}, bf16[2,128,128]{2,1,0:T(8,128)(2,1)S(1)}, u32[]{:S(2)}, u32[]{:S(2)}) collective-permute-start(bf16[2,128,128]{2,1,0:T(8,128)(2,1)S(1)} %get-tuple-element.72), channel_id=1, source_target_pairs={{0,8},{1,9},{2,10},{3,11},{4,12},{5,13},{6,14},{7,15},{8,0},{9,1},... | collective-permute-start | bytes 196616 | tf_op jit(solution)/shard_map/ppermute | solution.py:243
  88.5 7.1 %collective-permute-start.22 = (bf16[2,128,128]{2,1,0:T(8,128)(2,1)S(1)}, bf16[2,128,128]{2,1,0:T(8,128)(2,1)S(1)}, u32[]{:S(2)}, u32[]{:S(2)}) collective-permute-start(bf16[2,128,128]{2,1,0:T(8,128)(2,1)S(1)} %get-tuple-element.73), channel_id=1, source_target_pairs={{0,10},{1,11},{2,8},{3,9},{4,14},{5,15},{6,12},{7,13},{8,2},{9,3},... | collective-permute-start | bytes 196616 | tf_op jit(solution)/shard_map/ppermute | solution.py:243
  90.0 6.2 %collective-permute-start.23 = (bf16[2,128,128]{2,1,0:T(8,128)(2,1)S(1)}, bf16[2,128,128]{2,1,0:T(8,128)(2,1)S(1)}, u32[]{:S(2)}, u32[]{:S(2)}) collective-permute-start(bf16[2,128,128]{2,1,0:T(8,128)(2,1)S(1)} %get-tuple-element.74), channel_id=1, source_target_pairs={{0,12},{1,13},{2,14},{3,15},{4,8},{5,9},{6,10},{7,11},{8,4},{9,5},... | collective-permute-start | bytes 196616 | tf_op jit(solution)/shard_map/ppermute | solution.py:243
  92.3 7.0 %collective-permute-start.24 = (bf16[2,128,128]{2,1,0:T(8,128)(2,1)S(1)}, bf16[2,128,128]{2,1,0:T(8,128)(2,1)S(1)}, u32[]{:S(2)}, u32[]{:S(2)}) collective-permute-start(bf16[2,128,128]{2,1,0:T(8,128)(2,1)S(1)} %get-tuple-element.75), channel_id=1, source_target_pairs={{0,14},{1,15},{2,12},{3,13},{4,10},{5,11},{6,8},{7,9},{8,6},{9,7},... | collective-permute-start | bytes 196616 | tf_op jit(solution)/shard_map/ppermute | solution.py:243
  95.1 4.7 %collective-permute-start.33 = (bf16[8,128,128]{2,1,0:T(8,128)(2,1)S(1)}, bf16[8,128,128]{2,1,0:T(8,128)(2,1)S(1)}, u32[]{:S(2)}, u32[]{:S(2)}) collective-permute-start(bf16[8,128,128]{2,1,0:T(8,128)(2,1)S(1)} %shard_map.103), channel_id=1, source_target_pairs={{0,1},{1,0},{2,3},{3,2},{4,5},{5,4},{6,7},{7,6},{8,9},{9,8},{10,11... | collective-permute-start | bytes 786440 | tf_op jit(solution)/shard_map/ppermute | solution.py:380
  99.7 1.6 %collective-permute-start.25 = (bf16[8,128,128]{2,1,0:T(8,128)(2,1)S(1)}, bf16[8,128,128]{2,1,0:T(8,128)(2,1)S(1)}, u32[]{:S(2)}, u32[]{:S(2)}) collective-permute-start(bf16[8,128,128]{2,1,0:T(8,128)(2,1)S(1)} %shard_map.102), channel_id=1, source_target_pairs={{0,1},{1,0},{2,3},{3,2},{4,5},{5,4},{6,7},{7,6},{8,9},{9,8},{10,11... | collective-permute-start | bytes 786440 | tf_op jit(solution)/shard_map/ppermute | solution.py:380

commit v2 on v0

--- a/solution.py
+++ b/solution.py
@@ -1,7 +1,464 @@
+import functools
+
 import jax
 import jax.numpy as jnp
 from jax import lax
+from jax.experimental import pallas as pl
+from jax.experimental.pallas import tpu as pltpu
 from jax.sharding import PartitionSpec as P
+
+F32 = jnp.float32
+BF16 = jnp.bfloat16
+VMEM = pl.BlockSpec(memory_space=pltpu.VMEM)
+SMEM = pl.BlockSpec(memory_space=pltpu.SMEM)
+HBM = pl.BlockSpec(memory_space=pltpu.MemorySpace.HBM)
+VMEM_LIMIT = 16 * 1024 * 1024
+DMA = pltpu.SemaphoreType.DMA
+FORWARD = (1, 2, 3, 4, 5, 6, 7)
+BACKWARD = (2, 7, 6, 5, 4, 3, 1)
+COST = 100
+
+
+def dot(a, b):
+    return jnp.dot(a, b, preferred_element_type=F32)
+
+
+def dot_t(a, b):
+    return lax.dot_general(a, b, (((1,), (1,)), ((), ())), preferred_element_type=F32)
+
+
+def shape(dims, dtype=BF16):
+    return jax.ShapeDtypeStruct(dims, dtype)
+
+
+def call(body, outs, in_specs, out_specs, scratch=(), flops=0, moved=0):
+    return pl.pallas_call(
+        body,
+        out_shape=outs,
+        in_specs=in_specs,
+        out_specs=out_specs,
+        scratch_shapes=list(scratch),
+        compiler_params=pltpu.CompilerParams(vmem_limit_bytes=VMEM_LIMIT),
+        cost_estimate=pl.CostEstimate(flops=COST * flops, bytes_accessed=COST * moved, transcendentals=0),
+    )
+
+
+def inner_index():
+    return 1 - lax.axis_index("snap")
+
+
+def split_index():
+    me = lax.axis_index("dom")
+    return me // 2, lax.rem(me, 2)
+
+
+def run_copies(pairs, sem):
+    copies = [
+        pltpu.make_async_copy(source, target, sem.at[i]) for i, (source, target) in enumerate(pairs)
+    ]
+    for copy in copies:
+        copy.start()
+    for copy in copies:
+        copy.wait()
+
+
+def wanted(lists, feats, snap, target, block):
+    start = pl.multiple_of(jnp.maximum(lists[snap, 0, target], 0) * block, block)
+    return feats.at[snap, pl.ds(start, block)]
+
+
+def pack_inner_body(domains, block, lists, feats, out, send, sem):
+    run_copies([(lists, send)], sem)
+    ia = inner_index()
+    run_copies([(wanted(send, feats, ia, d, block), out.at[d]) for d in range(domains)], sem)
+
+
+def pack_outer_body(chips, block, send, partner_send, feats, partner_feats, *rest):
+    outs, (lists, sem) = rest[:-2], rest[-2:]
+    run_copies([(send, lists.at[0]), (partner_send, lists.at[1])], sem)
+    send, partner_send = lists.at[0], lists.at[1]
+    chip, core = split_index()
+    ib = 1 - inner_index()
+    pairs = []
+    for offset in range(chips):
+        target = 2 * jnp.bitwise_xor(chip, offset) + core
+        pairs.append((wanted(send, feats, ib, target, block), outs[offset].at[0]))
+        pairs.append((wanted(partner_send, partner_feats, ib, target, block), outs[offset].at[1]))
+    run_copies(pairs, sem)
+
+
+def collect_body(picks, *refs):
+    sources, out, sem = refs[:-2], refs[-2], refs[-1]
+    run_copies([(sources[i].at[j], out.at[n]) for n, (i, j) in enumerate(picks)], sem)
+
+
+def prep_body(slots, per_step, adj, tw, sw, rows_out, twt, wide):
+    block = adj.shape[2]
+
+    @pl.when(pl.program_id(0) == 0)
+    def _():
+        for tap in range(tw.shape[0]):
+            twt[tap] = tw[tap].astype(F32).T.astype(BF16)
+
+    wide[...] = adj[0].astype(F32)
+    for n in range(per_step):
+        for slot in range(slots):
+            tile = wide[pl.ds(n * slots * block + slot, block, stride=slots), :]
+            rows_out[0, n, :, slot * block : (slot + 1) * block] = tile.astype(BF16)
+
+
+def position(column, chips, blocks_here, plain):
+    chip, core = split_index()
+    part = jnp.clip(column - blocks_here, 0, 2 * chips - 1)
+    if plain:
+        return part
+    which = jnp.bitwise_xor(lax.rem(part, 2), core)
+    return which * chips + jnp.bitwise_xor(part // 2, chip)
+
+
+def aggregate(plain, snap, chips, blocks_here, slots, cols, own, adj, halo, agg, sw, hidden):
+    block = halo.shape[1]
+    for j in range(blocks_here):
+        rows = slice(j * block, (j + 1) * block)
+        pieces = [own[rows, :]]
+        for slot in range(1, slots):
+            pieces.append(halo[position(cols[snap, slot, j], chips, blocks_here, plain)])
+        agg[rows, :] = dot(adj[j], jnp.concatenate(pieces, axis=0)).astype(BF16)
+    hidden[...] = dot(agg[...], sw[...]).astype(BF16)
+
+
+def hidden_inner_body(chips, blocks_here, slots, cols, feats, tiles, sw, arrived, *rest):
+    hidden, own, adj, halo, agg, sem = rest
+    ia = inner_index()
+    run_copies([(feats.at[ia], own), (tiles.at[ia], adj), (arrived, halo)], sem)
+    aggregate(True, ia, chips, blocks_here, slots, cols, own, adj, halo, agg, sw, hidden)
+
+
+def hidden_outer_body(chips, blocks_here, slots, cols, feats, tiles, sw, *rest):
+    arrived = rest[:chips]
+    hidden, own, adj, halo, agg, sem = rest[chips:]
+    ib = 1 - inner_index()
+    pairs = [(feats.at[ib], own), (tiles.at[ib], adj)]
+    for offset in range(chips):
+        for which in range(2):
+            pairs.append((arrived[offset].at[which], halo.at[which * chips + offset]))
+    run_copies(pairs, sem)
+    aggregate(False, ib, chips, blocks_here, slots, cols, own, adj, halo, agg, sw, hidden)
+
+
+def spread(plain, snap, chips, blocks_here, slots, cols, grad, sw, adj, local, acc):
+    block = acc.shape[1]
+    agg_t = dot_t(sw[...], grad[...]).astype(BF16)
+    acc[...] = jnp.zeros_like(acc)
+    for j in range(blocks_here):
+        parts = dot(agg_t[:, j * block : (j + 1) * block], adj[j])
+        local[j] = parts[:, :block]
+        for slot in range(1, slots):
+            at = position(cols[snap, slot, j], chips, blocks_here, plain)
+            acc[at] = acc[at] + parts[:, slot * block : (slot + 1) * block]
+
+
+def temporal_body(
+    chips, blocks_here, slots, tile, cols, ha, hb, hn, cot, tw, twt, bias, sw, tiles, *rest
+):
+    shares, out, partial, rest_a, local, grad, acc, adj, sem = rest
+    ia = inner_index()
+    ib = 1 - ia
+    fetch = pltpu.make_async_copy(tiles.at[ib], adj, sem)
+    fetch.start()
+    flip = lax.axis_index("snap")
+    lo, hi = 2 * flip, 2 - 2 * flip
+    items, channels = ha.shape
+    both = jnp.concatenate(
+        [
+            jnp.concatenate([tw[lo], tw[1]], axis=0),
+            jnp.concatenate([tw[1], tw[hi]], axis=0),
+        ],
+        axis=1,
+    )
+    back = jnp.concatenate([twt[hi], twt[1]], axis=1)
+    for start in range(0, items, tile):
+        rows = slice(start, start + tile)
+        pair = jnp.concatenate([hb[rows, :], ha[rows, :]], axis=1)
+        mixes = dot(pair, both)
+        mix_a = mixes[:, : 2 * channels] + dot(hn[rows, :], tw[hi]) + bias[...]
+        mix_b = mixes[:, 2 * channels :] + bias[...]
+        grads = []
+        for index, mix in ((ia, mix_a), (ib, mix_b)):
+            linear = mix[:, :channels]
+            gate = jax.nn.sigmoid(mix[:, channels:])
+            up = cot[index, rows, :].astype(F32)
+            gated = linear * gate
+            out[index, rows, :] = gated.astype(BF16)
+            first = up * gate
+            second = up * gated * (1.0 - gate)
+            grads.append(jnp.concatenate([first.astype(BF16), second.astype(BF16)], axis=1))
+        ga, gb = grads
+        from_a = dot(ga, back)
+        from_b = dot(gb, back)
+        partial[rows, :] = from_a[:, :channels].astype(BF16)
+        rest_a[rows, :] = from_a[:, channels:] + from_b[:, :channels]
+        grad[rows, :] = (dot(ga, twt[lo]) + from_b[:, channels:]).astype(BF16)
+    fetch.wait()
+    spread(True, ib, chips, blocks_here, slots, cols, grad, sw, adj, local, acc)
+    shares[...] = acc[...].astype(BF16)
+
+
+def inner_body(chips, blocks_here, slots, cols, rest_a, partial, sw, tiles, *rest):
+    outs = rest[:chips]
+    local, grad, acc, adj, sem = rest[chips:]
+    ia = inner_index()
+    fetch = pltpu.make_async_copy(tiles.at[ia], adj, sem)
+    fetch.start()
+    grad[...] = (rest_a[...] + partial[...].astype(F32)).astype(BF16)
+    fetch.wait()
+    spread(False, ia, chips, blocks_here, slots, cols, grad, sw, adj, local, acc)
+    for offset in range(chips):
+        for which in range(2):
+            outs[offset][which] = acc[which * chips + offset].astype(BF16)
+
+
+def add_shares(snap, send, local, terms, acc):
+    acc[...] = local[...]
+    for source, value in terms:
+        at = send[snap, 0, source]
+
+        @pl.when(at >= 0)
+        def _():
+            acc[at] = acc[at] + value[...].astype(F32)
+
+
+def finish_rows(acc, n):
+    return acc[n].T.astype(BF16)
+
+
+def source_of(offset, which):
+    chip, core = split_index()
+    return 2 * jnp.bitwise_xor(chip, offset) + jnp.bitwise_xor(core, which)
+
+
+def final_outer_body(domains, send, local, arrived, out, acc):
+    terms = [(d, arrived.at[d]) for d in range(domains)]
+    add_shares(1 - inner_index(), send, local, terms, acc)
+    block = acc.shape[1]
+    for n in range(acc.shape[0]):
+        out[n * block : (n + 1) * block, :] = finish_rows(acc, n)
+
+
+def final_inner_body(chips, send, local, *rest):
+    arrived, acc = rest[: chips - 1], rest[chips - 1]
+    terms = [(source_of(offset, 0), arrived[offset - 1].at[0]) for offset in range(1, chips)]
+    add_shares(inner_index(), send, local, terms, acc)
+
+
+def last_body(chips, send, part, swapped, outer, out, acc, sem):
+    ia = inner_index()
+    move = pltpu.make_async_copy(outer, out.at[1 - ia], sem.at[0])
+    move.start()
+    terms = [(source_of(offset, 1), swapped.at[offset]) for offset in range(chips)]
+    add_shares(ia, send, part, terms, acc)
+    block = acc.shape[1]
+    for n in range(acc.shape[0]):
+        out[ia, n * block : (n + 1) * block, :] = finish_rows(acc, n)
+    move.wait()
+
+
+def local_pair(
+    features,
+    adjacency,
+    block_cols,
+    send_lists,
+    receive_lists,
+    spatial_weight,
+    temporal_weight,
+    temporal_bias,
+    cotangent,
+):
+    domains = lax.axis_size("dom")
+    chips = domains // 2
+    snaps_here, items_here, channels = features.shape
+    slots, block = adjacency.shape[2:]
+    blocks_here = items_here // block
+    taps, _, doubled = temporal_weight.shape
+    flip_core = [(i, i ^ 1) for i in range(domains)]
+    other_snap = [(0, 1), (1, 0)]
+    two = shape((2, block, channels))
+    block_bytes = block * channels * 2
+    item_flops = 2 * items_here * channels * channels
+
+    def swap_cores(values):
+        return lax.ppermute(values, "dom", flip_core)
+
+    def exchange(values):
+        return lax.all_to_all(values, "dom", split_axis=0, concat_axis=0, tiled=True)
+
+    def to_chips(payloads, order):
+        done = {}
+        for offset in order:
+            pairs = [(i, i ^ (2 * offset)) for i in range(domains)]
+            done[offset] = lax.ppermute(payloads[offset], "dom", pairs)
+        return [done[offset] for offset in sorted(done)]
+
+    cols = jnp.swapaxes(block_cols, 1, 2)
+    partner_send = swap_cores(send_lists)
+    partner_feats = swap_cores(features)
+
+    packed_a = call(
+        functools.partial(pack_inner_body, domains, block),
+        shape((domains, block, channels)),
+        [HBM] * 2,
+        HBM,
+        [pltpu.SMEM(send_lists.shape, jnp.int32), DMA((domains,))],
+        moved=2 * domains * block_bytes,
+    )(send_lists, features)
+    packed_a, partner_send, partner_feats = lax.optimization_barrier(
+        (packed_a, partner_send, partner_feats)
+    )
+    got_a = exchange(packed_a)
+    packed = call(
+        functools.partial(pack_outer_body, chips, block),
+        [two] * chips,
+        [HBM] * 4,
+        [HBM] * chips,
+        [pltpu.SMEM((2, *send_lists.shape), jnp.int32), DMA((domains,))],
+        moved=2 * domains * block_bytes,
+    )(send_lists, partner_send, features, partner_feats)
+    got_b = [packed[0]] + to_chips(packed, FORWARD)
+
+    per_step = 3 if blocks_here % 3 == 0 else 1
+    groups = blocks_here // per_step
+    tile_rows = block * slots
+    adj_flat = adjacency.reshape(snaps_here, items_here * slots, block)
+    tiles, twt = pl.pallas_call(
+        functools.partial(prep_body, slots, per_step),
+        grid=(snaps_here * groups,),
+        in_specs=[
+            pl.BlockSpec((1, per_step * tile_rows, block), lambda i: (i // groups, i % groups, 0)),
+            pl.BlockSpec((taps, channels, doubled), lambda i: (0, 0, 0)),
+            pl.BlockSpec((channels, channels), lambda i: (0, 0)),
+        ],
+        out_specs=[
+            pl.BlockSpec(
+                (1, per_step, block, tile_rows), lambda i: (i // groups, i % groups, 0, 0)
+            ),
+            pl.BlockSpec((taps, doubled, channels), lambda i: (0, 0, 0)),
+        ],
+        out_shape=[
+            shape((snaps_here, blocks_here, block, tile_rows)),
+            shape((taps, doubled, channels)),
+        ],
+        scratch_shapes=[pltpu.VMEM((per_step * tile_rows, block), F32)],
+        compiler_params=pltpu.CompilerParams(vmem_limit_bytes=VMEM_LIMIT),
+        cost_estimate=pl.CostEstimate(
+            flops=0, bytes_accessed=2 * adj_flat.size * 2, transcendentals=0
+        ),
+    )(adj_flat, temporal_weight, spatial_weight)
+
+    def hidden_of(body, arrived):
+        return call(
+            functools.partial(body, chips, blocks_here, slots),
+            shape((items_here, channels)),
+            [SMEM, HBM, HBM, VMEM] + [HBM] * len(arrived),
+            VMEM,
+            [
+                pltpu.VMEM((items_here, channels), BF16),
+                pltpu.VMEM((blocks_here, block, tile_rows), BF16),
+                pltpu.VMEM((domains, block, channels), BF16),
+                pltpu.VMEM((items_here, channels), BF16),
+                DMA((domains + 2,)),
+            ],
+            flops=(slots + 1) * item_flops,
+            moved=(slots + 4) * items_here * channels * 2,
+        )(cols, features, tiles, spatial_weight, *arrived)
+
+    hidden_a = hidden_of(hidden_inner_body, [got_a])
+    hidden_n = lax.ppermute(hidden_a, "snap", other_snap)
+    hidden_b = hidden_of(hidden_outer_body, got_b)
+
+    back_scratch = [
+        pltpu.VMEM((items_here, channels), BF16),
+        pltpu.VMEM((domains, block, channels), F32),
+        pltpu.VMEM((blocks_here, block, tile_rows), BF16),
+        DMA,
+    ]
+    local_shape = shape((blocks_here, block, channels), F32)
+    shares_b, output, partial, rest_a, local_b = call(
+        functools.partial(temporal_body, chips, blocks_here, slots, per_step * block),
+        [
+            shape((domains, block, channels)),
+            shape((snaps_here, items_here, channels)),
+            shape((items_here, channels)),
+            shape((items_here, channels), F32),
+            local_shape,
+        ],
+        [SMEM] + [VMEM] * 8 + [HBM],
+        [VMEM] * 5,
+        back_scratch,
+        flops=26 * item_flops,
+        moved=20 * items_here * channels * 2,
+    )(
+        cols,
+        hidden_a,
+        hidden_b,
+        hidden_n,
+        cotangent,
+        temporal_weight,
+        twt,
+        temporal_bias.reshape(1, doubled),
+        spatial_weight,
+        tiles,
+    )
+    partial_n = lax.ppermute(partial, "snap", other_snap)
+    back_b = exchange(shares_b)
+
+    results = call(
+        functools.partial(inner_body, chips, blocks_here, slots),
+        [two] * chips + [local_shape],
+        [SMEM] + [VMEM] * 3 + [HBM],
+        [VMEM] * (chips + 1),
+        back_scratch,
+        flops=(slots + 1) * item_flops,
+        moved=12 * items_here * channels * 2,
+    )(cols, rest_a, partial_n, spatial_weight, tiles)
+    shares_a, local_a = results[:chips], results[chips]
+    back_a = to_chips(shares_a, BACKWARD)
+    swapped = swap_cores(
+        call(
+            functools.partial(collect_body, [(i, 1) for i in range(chips)]),
+            shape((chips, block, channels)),
+            [HBM] * chips,
+            HBM,
+            [DMA((chips,))],
+            moved=2 * chips * block_bytes,
+        )(shares_a[0], *back_a)
+    )
+
+    acc = pltpu.VMEM((blocks_here, block, channels), F32)
+    cost = dict(flops=domains * block * channels, moved=8 * items_here * channels * 2)
+    grad_b = call(
+        functools.partial(final_outer_body, domains),
+        shape((items_here, channels)),
+        [SMEM] + [VMEM] * 2,
+        VMEM,
+        [acc],
+        **cost,
+    )(send_lists, local_b, back_b)
+    part = call(
+        functools.partial(final_inner_body, chips),
+        local_shape,
+        [SMEM] + [VMEM] * chips,
+        VMEM,
+        **cost,
+    )(send_lists, local_a, *back_a)
+    input_grad = call(
+        functools.partial(last_body, chips),
+        shape((snaps_here, items_here, channels)),
+        [SMEM] + [VMEM] * 3,
+        VMEM,
+        [acc, DMA((1,))],
+        **cost,
+    )(send_lists, part, swapped, grad_b)
+    return output, input_grad
 
 
 def pad_time(values):
@@ -61,7 +518,7 @@
     return running.reshape(length, row_count, channels).astype(jnp.bfloat16)
 
 
-def local(
+def local_any(
     features,
     adjacency,
     block_cols,
@@ -133,8 +590,9 @@
 
 
 def solution(mesh):
+    paired = mesh.shape["snap"] == 2 and mesh.shape["dom"] == 16
     return jax.shard_map(
-        local,
+        local_pair if paired else local_any,
         mesh=mesh,
         in_specs=(
             P("snap", "dom", None),

time: 142 us -> 83.4 us (0.59)
  waiting for transfers between devices: 47.3 us -> 12.1 us
  local copies, waits for them, and re-layouts: 32.4 us -> 9.51 us
  matrix products: 19.1 us -> 0 us
  Pallas kernels: 0 us -> 19.1 us
  starting transfers between devices: 25.3 us -> 40.6 us
  blocking collectives: 11.4 us -> 0 us
  other arithmetic: 3.27 us -> 0 us
    all_to_all x5 -> x2, waiting for transfers between devices: 47.3 us -> 0.01 us  [exchange(): lax.all_to_all(values, 'dom', split_axis=0, concat_axis=0, tiled=True)]
    ppermute x0 -> x19, starting transfers between devices: none -> 27.4 us  [the longest x14 23.6 us: to_chips(): done[offset] = lax.ppermute(payloads[offset], 'dom', pairs)]
    pallas_call x0 -> x11, Pallas kernels: none -> 19.1 us  [the longest x2 5.77 us: hidden_of(): call(functools.partial(body, chips, blocks_here, slots), shape((items_her...]
    dot_general x13 -> x0, matrix products: 19.1 us -> none  [the longest x1 5.51 us: local(): jnp.einsum('sjkf,sjkcd->sfcd', placing, contribution, precision=lax.Preci...]
    all_to_all x5 -> x2, starting transfers between devices: 25.3 us -> 13.2 us  [exchange(): lax.all_to_all(values, 'dom', split_axis=0, concat_axis=0, tiled=True)]
    ppermute x0 -> x19, waiting for transfers between devices: none -> 12.1 us  [the longest x14 10.5 us: to_chips(): done[offset] = lax.ppermute(payloads[offset], 'dom', pairs)]
    all_to_all x1 -> x0, blocking collectives: 11.4 us -> none  [to_snaps(): lax.all_to_all(values, 'snap', split_axis=0, concat_axis=1, tiled=True)]
    dot_general x1 -> x0, local copies, waits for them, and re-layouts: 8.84 us -> none  [local(): jnp.einsum('sjrkc,sjrd->sjkcd', adjacency_tiles, aggregate_grad, preferre...]
  transfers between devices with their start and end apart: 5 -> 21, of which waited for: 3 -> 4; matrix products, arithmetic and copies ran while one was open for 28% -> 0% of each run, Pallas kernels for 0% -> 16%
where the time goes in v2:
time: 83.4 us; the launch traced here: 82.2 us
  starting transfers between devices  40.6 us (49%)
  Pallas kernels  19.1 us (23%)
  waiting for transfers between devices  12.1 us (15%)
  local copies, waits for them, and re-layouts  9.51 us (11%)
  between operations  0.88 us (1%)
    ppermute x14, starting transfers between devices, to_chips(): done[offset] = lax.ppermute(payloads[offset], 'dom', pairs)  23.6 us
    all_to_all x2, starting transfers between devices, exchange(): lax.all_to_all(values, 'dom', split_axis=0, concat_axis=0, tiled=True)  13.2 us
    ppermute x14, waiting for transfers between devices, to_chips(): done[offset] = lax.ppermute(payloads[offset], 'dom', pairs)  10.5 us
    unnamed x38, local copies, waits for them, and re-layouts  9.51 us
    pallas_call x2, Pallas kernels, hidden_of(): call(functools.partial(body, chips, blocks_here, slots), shape((items_her...  5.77 us
    pallas_call x1, Pallas kernels, local_pair(): call(functools.partial(temporal_body, chips, blocks_here, slots, per_step...  3.82 us
    pallas_call x1, Pallas kernels, local_pair(): call(functools.partial(last_body, chips), shape((snaps_here, items_here,...  1.76 us
    pallas_call x1, Pallas kernels, local_pair(): call(functools.partial(pack_outer_body, chips, block), [two] * chips, [HB...  1.75 us
  transfers between devices with their start and end apart: 21, of which 4 were waited for; matrix products, arithmetic and copies ran while one was open for 0% of the time, Pallas kernels for 16%

profile of v2, /device:TPU:0, one launch (start us, length us, event | category | flops | bytes accessed | tf_op | source)
XLA Modules:
  0.0 82.2 jit_solution(1349326997070276246)
XLA Ops:
  0.6 0.5 collective-permute-start.1
  1.1 0.1 collective-permute-start
  1.2 1.1 %copy-done = bf16[2,1152,128]{2,1,0:T(8,128)(2,1)S(1)} copy-done((bf16[2,1152,128]{2,1,0:T(8,128)(2,1)S(1)}, bf16[2,1152,128]{2,1,0:T(8,128)(2,1)}, u32[]{:S(2)}) %copy-start) | copy-done | bytes 589848
  2.3 0.7 copy-done.7
  3.0 1.5 %shard_map.96 = bf16[16,128,128]{2,1,0:T(8,128)(2,1)} custom-call(s32[2,1,16]{2,1,0:T(1,128)S(1)} %copy-done.7, bf16[2,1152,128]{2,1,0:T(8,128)(2,1)S(1)} %copy-done), custom_call_target="tpu_custom_call" | custom-call | bytes 104857600 | tf_op jit(solution)/shard_map/pallas_call | solution.py:306
  4.5 0.0 collective-permute-done.partner_send
  4.5 0.0 collective-permute-done.1.partner_feats
  4.5 7.4 %all-to-all-start = ((bf16[16,128,128]{2,1,0:T(8,128)(2,1)}), bf16[16,128,128]{2,1,0:T(8,128)(2,1)}, u32[]{:S(2)}, u32[]{:S(2)}) async-start(bf16[16,128,128]{2,1,0:T(8,128)(2,1)} %shard_map.96), calls=%async_computation | async-start | bytes 1048576 | tf_op jit(solution)/shard_map/all_to_all | solution.py:293
  11.9 0.0 copy-start.8
  11.9 0.7 copy-done.8
  12.6 1.7 %shard_map.98 = (bf16[2,128,128]{2,1,0:T(8,128)(2,1)S(1)}, bf16[2,128,128]{2,1,0:T(8,128)(2,1)S(1)}, bf16[2,128,128]{2,1,0:T(8,128)(2,1)S(1)}, bf16[2,128,128]{2...) custom-call(s32[2,1,16]{2,1,0:T(1,128)S(1)} %copy-done.8, ...), custom_call_target="tpu_custom_call" | custom-call | bytes 104857600 | tf_op jit(solution)/shard_map/pallas_call | solution.py:318
  14.4 0.6 copy-done.15
  15.0 1.9 %collective-permute-start.2 = (bf16[2,128,128]{2,1,0:T(8,128)(2,1)S(1)}, bf16[2,128,128]{2,1,0:T(8,128)(2,1)S(1)}, u32[]{:S(2)}, u32[]{:S(2)}) collective-permute-start(bf16[2,128,128]{2,1,0:T(8,128)(2,1)S(1)} %get-tuple-element.34), channel_id=1, source_target_pairs={{0,2},{1,3},{2,0},{3,1},{4,6},{5,7},{6,4},{7,5},{8,10},{9,11},{10,... | collective-permute-start | bytes 196616 | tf_op jit(solution)/shard_map/ppermute | solution.py:299
  16.9 1.5 %collective-permute-start.3 = (bf16[2,128,128]{2,1,0:T(8,128)(2,1)S(1)}, bf16[2,128,128]{2,1,0:T(8,128)(2,1)S(1)}, u32[]{:S(2)}, u32[]{:S(2)}) collective-permute-start(bf16[2,128,128]{2,1,0:T(8,128)(2,1)S(1)} %get-tuple-element.35), channel_id=1, source_target_pairs={{0,4},{1,5},{2,6},{3,7},{4,0},{5,1},{6,2},{7,3},{8,12},{9,13},{10,... | collective-permute-start | bytes 196616 | tf_op jit(solution)/shard_map/ppermute | solution.py:299
  18.3 0.9 %copy-done.3 = bf16[3,128,256]{2,1,0:T(8,128)(2,1)S(1)} copy-done((bf16[3,128,256]{2,1,0:T(8,128)(2,1)S(1)}, bf16[3,128,256]{2,1,0:T(8,128)(2,1)}, u32[]{:S(2)}) %copy-start.3) | copy-done | bytes 196632
  19.3 0.8 copy-done.5
  20.0 0.9 %shard_map.95 = (bf16[2,9,128,512]{3,2,1,0:T(8,128)(2,1)S(1)}, bf16[3,256,128]{2,1,0:T(8,128)(2,1)S(1)}) custom-call(bf16[2,4608,128]{2,1,0:T(8,128)(2,1)S(1)} %bitcast.3, bf16[3,128,256]{2,1,0:T(8,128)(2,1)S(1)} %copy-done.3, bf16[128,128]{1,0:T(8,128)(2,1)S(1)} %copy-done.5), custom_call_target="tpu_custom_call" | custom-call | bytes 4718592 | tf_op jit(solution)/shard_map/pallas_call | solution.py:332
  21.0 1.4 %copy-done.10 = bf16[2,9,128,512]{3,2,1,0:T(8,128)(2,1)} copy-done((bf16[2,9,128,512]{3,2,1,0:T(8,128)(2,1)}, bf16[2,9,128,512]{3,2,1,0:T(8,128)(2,1)S(1)}, u32[]{:S(2)}) %copy-start.10) | copy-done | bytes 2359320
  22.4 0.2 collective-permute-start.4
  22.6 2.8 %collective-permute-start.5 = (bf16[2,128,128]{2,1,0:T(8,128)(2,1)}, bf16[2,128,128]{2,1,0:T(8,128)(2,1)S(1)}, u32[]{:S(2)}, u32[]{:S(2)}) collective-permute-start(bf16[2,128,128]{2,1,0:T(8,128)(2,1)} %get-tuple-element.37), channel_id=1, source_target_pairs={{0,8},{1,9},{2,10},{3,11},{4,12},{5,13},{6,14},{7,15},{8,0},{9,1},... | collective-permute-start | bytes 196616 | tf_op jit(solution)/shard_map/ppermute | solution.py:299
  25.3 1.5 %collective-permute-start.6 = (bf16[2,128,128]{2,1,0:T(8,128)(2,1)}, bf16[2,128,128]{2,1,0:T(8,128)(2,1)S(1)}, u32[]{:S(2)}, u32[]{:S(2)}) collective-permute-start(bf16[2,128,128]{2,1,0:T(8,128)(2,1)} %get-tuple-element.38), channel_id=1, source_target_pairs={{0,10},{1,11},{2,8},{3,9},{4,14},{5,15},{6,12},{7,13},{8,2},{9,3},... | collective-permute-start | bytes 196616 | tf_op jit(solution)/shard_map/ppermute | solution.py:299
  26.8 0.0 collective-permute-done.2.rest_1_
  26.8 3.3 %collective-permute-start.7 = (bf16[2,128,128]{2,1,0:T(8,128)(2,1)}, bf16[2,128,128]{2,1,0:T(8,128)(2,1)}, u32[]{:S(2)}, u32[]{:S(2)}) collective-permute-start(bf16[2,128,128]{2,1,0:T(8,128)(2,1)} %get-tuple-element.39), channel_id=1, source_target_pairs={{0,12},{1,13},{2,14},{3,15},{4,8},{5,9},{6,10},{7,11},{8,4},{9,5},... | collective-permute-start | bytes 196616 | tf_op jit(solution)/shard_map/ppermute | solution.py:299
  30.1 0.0 collective-permute-done.3.rest_2_
  30.1 0.1 collective-permute-start.8
  30.2 0.0 all-to-all-done.arrived
  30.2 1.7 %copy-done.11 = bf16[2,9,128,512]{3,2,1,0:T(8,128)(2,1)S(1)} copy-done((bf16[2,9,128,512]{3,2,1,0:T(8,128)(2,1)S(1)}, bf16[2,9,128,512]{3,2,1,0:T(8,128)(2,1)}, u32[]{:S(2)}) %copy-start.11) | copy-done | bytes 2359320
  31.9 2.7 %shard_map.97.ha = bf16[1152,128]{1,0:T(8,128)(2,1)S(1)} custom-call(s32[2,4,9]{2,1,0:T(4,128)S(1)} %bitcast.4, bf16[2,1152,128]{2,1,0:T(8,128)(2,1)S(1)} %copy-done.1, bf16[2,9,128,512]{3,2,1,0:T(8,128)(2,1)S(1)} %copy-done.11, bf16[128,128]{1,0:T(8,128)(2,1)S(1)} %copy-done.6, bf16[16,128,128]{2,1,0:T(8,128)(2,1)} %all-to-all-done.arrived), custom_call_target="tpu_custom_call" | custom-call | flops 18874368000 | bytes 235929600 | tf_op jit(solution)/shard_map/pallas_call | solution.py:358
  34.6 0.0 collective-permute-done.4.rest_3_
  34.7 1.6 %collective-permute-start.9 = (bf16[1152,128]{1,0:T(8,128)(2,1)S(1)}, bf16[1152,128]{1,0:T(8,128)(2,1)S(1)}, u32[]{:S(2)}, u32[]{:S(2)}) collective-permute-start(bf16[1152,128]{1,0:T(8,128)(2,1)S(1)} %shard_map.97.ha), channel_id=1, source_target_pairs={{0,16},{16,0},{1,17},{17,1},{2,18},{18,2},{3,19},{19,3},{4,20},{20... | collective-permute-start | bytes 884744 | tf_op jit(solution)/shard_map/ppermute | solution.py:375
  36.2 0.0 collective-permute-done.5.rest_4_
  36.2 0.0 collective-permute-done.6.rest_5_
  36.2 0.0 collective-permute-done.7.rest_6_
  36.3 1.2 %collective-permute-done.8.rest_7_ = bf16[2,128,128]{2,1,0:T(8,128)(2,1)} collective-permute-done((bf16[2,128,128]{2,1,0:T(8,128)(2,1)}, bf16[2,128,128]{2,1,0:T(8,128)(2,1)}, u32[]{:S(2)}, u32[]{:S(2)}) %collective-permute-start.8) | collective-permute-done | bytes 65568 | tf_op jit(solution)/shard_map/ppermute | solution.py:299
  37.5 0.0 copy-start.18
  37.5 3.0 %shard_map.99.hb = bf16[1152,128]{1,0:T(8,128)(2,1)S(1)} custom-call(s32[2,4,9]{2,1,0:T(4,128)S(1)} %bitcast.5, bf16[2,1152,128]{2,1,0:T(8,128)(2,1)S(1)} %copy-done.1, bf16[2,9,128,512]{3,2,1,0:T(8,128)(2,1)S(1)} %copy-done.12, bf16[128,128]{1,0:T(8,128)(2,1)S(1)} %copy-done.6, bf16[2,128,128]{2,1,0:T(8,128)(2,1)S(1)} %copy-done.16, ...), custom_call_target="tpu_custom_call" | custom-call | flops 18874368000 | bytes 235929600 | tf_op jit(solution)/shard_map/pallas_call | solution.py:358
  40.5 1.5 %collective-permute-done.9.hn = bf16[1152,128]{1,0:T(8,128)(2,1)S(1)} collective-permute-done((bf16[1152,128]{1,0:T(8,128)(2,1)S(1)}, bf16[1152,128]{1,0:T(8,128)(2,1)S(1)}, u32[]{:S(2)}, u32[]{:S(2)}) %collective-permute-start.9) | collective-permute-done | bytes 294944 | tf_op jit(solution)/shard_map/ppermute | solution.py:375
  42.0 3.8 %shard_map.100 = (bf16[16,128,128]{2,1,0:T(8,128)(2,1)}, bf16[2,1152,128]{2,1,0:T(8,128)(2,1)}, bf16[1152,128]{1,0:T(8,128)(2,1)S(1)}, f32[1152,128]{1,0:T(8,128)S(1)}, f32[9,128,128]{2,1,0:T(8,128)S(1)}) custom-call(s32[2,4,9]{2,1,0:T(4,128)S(1)} %bitcast.6, bf16[1152,128]{1,0:T(8,128)(2,1)S(1)} %shard_map.97.ha, bf16[1152,128]{1,0:T(8,128)(2,1)S(1)} %shard_map.99.hb, ...), custom_call_target="tpu_custom_call" | custom-call | flops 98146713600 | bytes 589824000 | tf_op jit(solution)/shard_map/pallas_call | solution.py:385
  45.9 1.6 %collective-permute-start.10 = (bf16[1152,128]{1,0:T(8,128)(2,1)S(1)}, bf16[1152,128]{1,0:T(8,128)(2,1)S(1)}, u32[]{:S(2)}, u32[]{:S(2)}) collective-permute-start(bf16[1152,128]{1,0:T(8,128)(2,1)S(1)} %get-tuple-element.44), channel_id=1, source_target_pairs={{0,16},{16,0},{1,17},{17,1},{2,18},{18,2},{3,19},{19,3},{4,20},{20... | collective-permute-start | bytes 884744 | tf_op jit(solution)/shard_map/ppermute | solution.py:411
  47.4 5.7 %all-to-all-start.1 = ((bf16[16,128,128]{2,1,0:T(8,128)(2,1)}), bf16[16,128,128]{2,1,0:T(8,128)(2,1)S(1)}, u32[]{:S(2)}, u32[]{:S(2)}) async-start(bf16[16,128,128]{2,1,0:T(8,128)(2,1)} %get-tuple-element.55), calls=%async_computation.1 | async-start | bytes 1048576 | tf_op jit(solution)/shard_map/all_to_all | solution.py:293
  53.2 0.0 collective-permute-done.10.partial
  53.2 1.7 %copy-done.13 = bf16[2,9,128,512]{3,2,1,0:T(8,128)(2,1)S(1)} copy-done((bf16[2,9,128,512]{3,2,1,0:T(8,128)(2,1)S(1)}, bf16[2,9,128,512]{3,2,1,0:T(8,128)(2,1)}, u32[]{:S(2)}) %copy-start.13) | copy-done | bytes 2359320
  54.9 1.6 %shard_map.101 = (bf16[2,128,128]{2,1,0:T(8,128)(2,1)S(1)}, bf16[2,128,128]{2,1,0:T(8,128)(2,1)S(1)}, bf16[2,128,128]{2,1,0:T(8,128)(2,1)S(1)}, bf16[2,128,128]{...) custom-call(s32[2,4,9]{2,1,0:T(4,128)S(1)} %bitcast.7, ...), custom_call_target="tpu_custom_call" | custom-call | flops 18874368000 | bytes 353894400 | tf_op jit(solution)/shard_map/pallas_call | solution.py:414
  56.5 2.0 %collective-permute-start.11 = (bf16[2,128,128]{2,1,0:T(8,128)(2,1)S(1)}, bf16[2,128,128]{2,1,0:T(8,128)(2,1)S(1)}, u32[]{:S(2)}, u32[]{:S(2)}) collective-permute-start(bf16[2,128,128]{2,1,0:T(8,128)(2,1)S(1)} %get-tuple-element.46), channel_id=1, source_target_pairs={{0,2},{1,3},{2,0},{3,1},{4,6},{5,7},{6,4},{7,5},{8,10},{9,11},{10,... | collective-permute-start | bytes 196616 | tf_op jit(solution)/shard_map/ppermute | solution.py:299
  58.5 1.5 %collective-permute-start.12 = (bf16[2,128,128]{2,1,0:T(8,128)(2,1)S(1)}, bf16[2,128,128]{2,1,0:T(8,128)(2,1)S(1)}, u32[]{:S(2)}, u32[]{:S(2)}) collective-permute-start(bf16[2,128,128]{2,1,0:T(8,128)(2,1)S(1)} %get-tuple-element.47), channel_id=1, source_target_pairs={{0,4},{1,5},{2,6},{3,7},{4,0},{5,1},{6,2},{7,3},{8,12},{9,13},{10,... | collective-permute-start | bytes 196616 | tf_op jit(solution)/shard_map/ppermute | solution.py:299
  59.9 0.4 collective-permute-start.13
  60.3 2.9 %collective-permute-start.14 = (bf16[2,128,128]{2,1,0:T(8,128)(2,1)S(1)}, bf16[2,128,128]{2,1,0:T(8,128)(2,1)S(1)}, u32[]{:S(2)}, u32[]{:S(2)}) collective-permute-start(bf16[2,128,128]{2,1,0:T(8,128)(2,1)S(1)} %get-tuple-element.49), channel_id=1, source_target_pairs={{0,8},{1,9},{2,10},{3,11},{4,12},{5,13},{6,14},{7,15},{8,0},{9,1},... | collective-permute-start | bytes 196616 | tf_op jit(solution)/shard_map/ppermute | solution.py:299
  63.2 1.1 %collective-permute-start.15 = (bf16[2,128,128]{2,1,0:T(8,128)(2,1)S(1)}, bf16[2,128,128]{2,1,0:T(8,128)(2,1)S(1)}, u32[]{:S(2)}, u32[]{:S(2)}) collective-permute-start(bf16[2,128,128]{2,1,0:T(8,128)(2,1)S(1)} %get-tuple-element.50), channel_id=1, source_target_pairs={{0,10},{1,11},{2,8},{3,9},{4,14},{5,15},{6,12},{7,13},{8,2},{9,3},... | collective-permute-start | bytes 196616 | tf_op jit(solution)/shard_map/ppermute | solution.py:299
  64.3 0.0 collective-permute-done.11.rest_0_.refs_1_
  64.3 3.3 %collective-permute-start.16 = (bf16[2,128,128]{2,1,0:T(8,128)(2,1)S(1)}, bf16[2,128,128]{2,1,0:T(8,128)(2,1)S(1)}, u32[]{:S(2)}, u32[]{:S(2)}) collective-permute-start(bf16[2,128,128]{2,1,0:T(8,128)(2,1)S(1)} %get-tuple-element.51), channel_id=1, source_target_pairs={{0,12},{1,13},{2,14},{3,15},{4,8},{5,9},{6,10},{7,11},{8,4},{9,5},... | collective-permute-start | bytes 196616 | tf_op jit(solution)/shard_map/ppermute | solution.py:299
  67.6 0.0 collective-permute-done.12.rest_1_.refs_2_
  67.6 1.4 %collective-permute-start.17 = (bf16[2,128,128]{2,1,0:T(8,128)(2,1)S(1)}, bf16[2,128,128]{2,1,0:T(8,128)(2,1)S(1)}, u32[]{:S(2)}, u32[]{:S(2)}) collective-permute-start(bf16[2,128,128]{2,1,0:T(8,128)(2,1)S(1)} %get-tuple-element.52), channel_id=1, source_target_pairs={{0,14},{1,15},{2,12},{3,13},{4,10},{5,11},{6,8},{7,9},{8,6},{9,7},... | collective-permute-start | bytes 196616 | tf_op jit(solution)/shard_map/ppermute | solution.py:299
  69.0 0.0 collective-permute-done.13.rest_2_.refs_3_
  69.0 7.0 %collective-permute-done.14.rest_3_.refs_4_ = bf16[2,128,128]{2,1,0:T(8,128)(2,1)S(1)} collective-permute-done((bf16[2,128,128]{2,1,0:T(8,128)(2,1)S(1)}, bf16[2,128,128]{2,1,0:T(8,128)(2,1)S(1)}, u32[]{:S(2)}, u32[]{:S(2)}) %collective-permute-start.14) | collective-permute-done | bytes 65568 | tf_op jit(solution)/shard_map/ppermute | solution.py:299
  76.0 2.3 %collective-permute-done.15.rest_4_.refs_5_ = bf16[2,128,128]{2,1,0:T(8,128)(2,1)S(1)} collective-permute-done((bf16[2,128,128]{2,1,0:T(8,128)(2,1)S(1)}, bf16[2,128,128]{2,1,0:T(8,128)(2,1)S(1)}, u32[]{:S(2)}, u32[]{:S(2)}) %collective-permute-start.15) | collective-permute-done | bytes 65568 | tf_op jit(solution)/shard_map/ppermute | solution.py:299
  78.3 0.0 collective-permute-done.16.rest_5_.refs_6_
  78.3 0.0 collective-permute-done.17.rest_6_.refs_7_
  78.3 0.4 shard_map.103
  78.7 0.1 collective-permute-start.18
  78.8 0.7 shard_map.102.part
  79.5 0.0 all-to-all-done.1.arrived
  79.5 0.9 %shard_map.104.outer = bf16[1152,128]{1,0:T(8,128)(2,1)S(1)} custom-call(s32[2,1,16]{2,1,0:T(1,128)S(1)} %copy-done.9, f32[9,128,128]{2,1,0:T(8,128)S(1)} %get-tuple-element.54.local, bf16[16,128,128]{2,1,0:T(8,128)(2,1)S(1)} %all-to-all-done.1.arrived), custom_call_target="tpu_custom_call" | custom-call | flops 26214400 | bytes 235929600 | tf_op jit(solution)/shard_map/pallas_call | solution.py:438
  80.4 0.0 collective-permute-done.18.swapped
  80.4 1.8 %shard_map.105 = bf16[2,1152,128]{2,1,0:T(8,128)(2,1)} custom-call(s32[2,1,16]{2,1,0:T(1,128)S(1)} %copy-done.9, f32[9,128,128]{2,1,0:T(8,128)S(1)} %shard_map.102.part, bf16[8,128,128]{2,1,0:T(8,128)(2,1)S(1)} %collective-permute-done.18.swapped, bf16[1152,128]{1,0:T(8,128)(2,1)S(1)} %shard_map.104.outer), custom_call_target="tpu_custom_call" | custom-call | flops 26214400 | bytes 235929600 | tf_op jit(solution)/shard_map/pallas_call | solution.py:453
  (27 shorter events, 0.1 us)
Async XLA Ops:
  0.6 3.8 %collective-permute-start.1 = (bf16[2,1152,128]{2,1,0:T(8,128)(2,1)}, bf16[2,1152,128]{2,1,0:T(8,128)(2,1)S(1)}, u32[]{:S(2)}, u32[]{:S(2)}) collective-permute-start(bf16[2,1152,128]{2,1,0:T(8,128)(2,1)} %feats.7), channel_id=1, source_target_pairs={{0,1},{1,0},{2,3},{3,2},{4,5},{5,4},{6,7},{7,6},{8,9},{9,8},{10,11... | collective-permute-start | bytes 1769480 | tf_op jit(solution)/shard_map/ppermute | solution.py:290
  1.1 3.3 %collective-permute-start = (s32[2,1,16]{2,1,0:T(1,128)}, s32[2,1,16]{2,1,0:T(1,128)S(1)}, u32[]{:S(2)}, u32[]{:S(2)}) collective-permute-start(s32[2,1,16]{2,1,0:T(1,128)} %send.7), channel_id=1, source_target_pairs={{0,1},{1,0},{2,3},{3,2},{4,5},{5,4},{6,7},{7,6},{8,9},{9,8},{10,11... | collective-permute-start | bytes 392 | tf_op jit(solution)/shard_map/ppermute | solution.py:290
  1.2 1.1 %copy-start = (bf16[2,1152,128]{2,1,0:T(8,128)(2,1)S(1)}, bf16[2,1152,128]{2,1,0:T(8,128)(2,1)}, u32[]{:S(2)}) copy-start(bf16[2,1152,128]{2,1,0:T(8,128)(2,1)} %feats.7) | copy-start | bytes 1769476
  2.3 0.7 copy-start.7
  3.0 9.0 %copy-start.1 = (bf16[2,1152,128]{2,1,0:T(8,128)(2,1)S(1)}, bf16[2,1152,128]{2,1,0:T(8,128)(2,1)}, u32[]{:S(2)}) copy-start(bf16[2,1152,128]{2,1,0:T(8,128)(2,1)} %feats.7) | copy-start | bytes 1769476
  3.0 15.4 %copy-start.2 = (bf16[2,1152,4,128]{3,2,1,0:T(4,128)(2,1)S(1)}, bf16[2,1152,4,128]{3,2,1,0:T(4,128)(2,1)}, u32[]{:S(2)}) copy-start(bf16[2,1152,4,128]{3,2,1,0:T(4,128)(2,1)} %param.10) | copy-start | bytes 7077892
  4.5 25.7 %all-to-all-start = ((bf16[16,128,128]{2,1,0:T(8,128)(2,1)}), bf16[16,128,128]{2,1,0:T(8,128)(2,1)}, u32[]{:S(2)}, u32[]{:S(2)}) async-start(bf16[16,128,128]{2,1,0:T(8,128)(2,1)} %shard_map.96), calls=%async_computation | async-start | bytes 1048576 | tf_op jit(solution)/shard_map/all_to_all | solution.py:293
  11.9 0.7 copy-start.8
  12.6 17.6 %copy-start.17 = (s32[2,9,4]{1,2,0:T(4,128)S(1)}, s32[2,9,4]{1,2,0:T(4,128)}, u32[]{:S(2)}) copy-start(s32[2,9,4]{1,2,0:T(4,128)} %param.11) | copy-start | bytes 868
  14.4 0.6 copy-start.15
  15.0 11.8 %collective-permute-start.2 = (bf16[2,128,128]{2,1,0:T(8,128)(2,1)S(1)}, bf16[2,128,128]{2,1,0:T(8,128)(2,1)S(1)}, u32[]{:S(2)}, u32[]{:S(2)}) collective-permute-start(bf16[2,128,128]{2,1,0:T(8,128)(2,1)S(1)} %get-tuple-element.34), channel_id=1, source_target_pairs={{0,2},{1,3},{2,0},{3,1},{4,6},{5,7},{6,4},{7,5},{8,10},{9,11},{10,... | collective-permute-start | bytes 196616 | tf_op jit(solution)/shard_map/ppermute | solution.py:299
  16.9 13.2 %collective-permute-start.3 = (bf16[2,128,128]{2,1,0:T(8,128)(2,1)S(1)}, bf16[2,128,128]{2,1,0:T(8,128)(2,1)S(1)}, u32[]{:S(2)}, u32[]{:S(2)}) collective-permute-start(bf16[2,128,128]{2,1,0:T(8,128)(2,1)S(1)} %get-tuple-element.35), channel_id=1, source_target_pairs={{0,4},{1,5},{2,6},{3,7},{4,0},{5,1},{6,2},{7,3},{8,12},{9,13},{10,... | collective-permute-start | bytes 196616 | tf_op jit(solution)/shard_map/ppermute | solution.py:299
  18.3 0.9 %copy-start.3 = (bf16[3,128,256]{2,1,0:T(8,128)(2,1)S(1)}, bf16[3,128,256]{2,1,0:T(8,128)(2,1)}, u32[]{:S(2)}) copy-start(bf16[3,128,256]{2,1,0:T(8,128)(2,1)} %tw.3) | copy-start | bytes 589828
  19.3 0.8 copy-start.5
  20.0 10.2 %copy-start.6 = (bf16[128,128]{1,0:T(8,128)(2,1)S(1)}, bf16[128,128]{1,0:T(8,128)(2,1)}, u32[]{:S(2)}) copy-start(bf16[128,128]{1,0:T(8,128)(2,1)} %sw.9) | copy-start | bytes 98308
  21.0 1.4 %copy-start.10 = (bf16[2,9,128,512]{3,2,1,0:T(8,128)(2,1)}, bf16[2,9,128,512]{3,2,1,0:T(8,128)(2,1)S(1)}, u32[]{:S(2)}) copy-start(bf16[2,9,128,512]{3,2,1,0:T(8,128)(2,1)S(1)} %get-tuple-element.29.tiles) | copy-start | bytes 7077892
  22.4 12.2 %collective-permute-start.4 = (bf16[2,128,128]{2,1,0:T(8,128)(2,1)}, bf16[2,128,128]{2,1,0:T(8,128)(2,1)S(1)}, u32[]{:S(2)}, u32[]{:S(2)}) collective-permute-start(bf16[2,128,128]{2,1,0:T(8,128)(2,1)} %get-tuple-element.36), channel_id=1, source_target_pairs={{0,6},{1,7},{2,4},{3,5},{4,2},{5,3},{6,0},{7,1},{8,14},{9,15},{10,... | collective-permute-start | bytes 196616 | tf_op jit(solution)/shard_map/ppermute | solution.py:299
  22.6 13.7 %collective-permute-start.5 = (bf16[2,128,128]{2,1,0:T(8,128)(2,1)}, bf16[2,128,128]{2,1,0:T(8,128)(2,1)S(1)}, u32[]{:S(2)}, u32[]{:S(2)}) collective-permute-start(bf16[2,128,128]{2,1,0:T(8,128)(2,1)} %get-tuple-element.37), channel_id=1, source_target_pairs={{0,8},{1,9},{2,10},{3,11},{4,12},{5,13},{6,14},{7,15},{8,0},{9,1},... | collective-permute-start | bytes 196616 | tf_op jit(solution)/shard_map/ppermute | solution.py:299
  25.3 10.9 %collective-permute-start.6 = (bf16[2,128,128]{2,1,0:T(8,128)(2,1)}, bf16[2,128,128]{2,1,0:T(8,128)(2,1)S(1)}, u32[]{:S(2)}, u32[]{:S(2)}) collective-permute-start(bf16[2,128,128]{2,1,0:T(8,128)(2,1)} %get-tuple-element.38), channel_id=1, source_target_pairs={{0,10},{1,11},{2,8},{3,9},{4,14},{5,15},{6,12},{7,13},{8,2},{9,3},... | collective-permute-start | bytes 196616 | tf_op jit(solution)/shard_map/ppermute | solution.py:299
  26.8 9.5 %collective-permute-start.7 = (bf16[2,128,128]{2,1,0:T(8,128)(2,1)}, bf16[2,128,128]{2,1,0:T(8,128)(2,1)}, u32[]{:S(2)}, u32[]{:S(2)}) collective-permute-start(bf16[2,128,128]{2,1,0:T(8,128)(2,1)} %get-tuple-element.39), channel_id=1, source_target_pairs={{0,12},{1,13},{2,14},{3,15},{4,8},{5,9},{6,10},{7,11},{8,4},{9,5},... | collective-permute-start | bytes 196616 | tf_op jit(solution)/shard_map/ppermute | solution.py:299
  30.1 7.4 %collective-permute-start.8 = (bf16[2,128,128]{2,1,0:T(8,128)(2,1)}, bf16[2,128,128]{2,1,0:T(8,128)(2,1)}, u32[]{:S(2)}, u32[]{:S(2)}) collective-permute-start(bf16[2,128,128]{2,1,0:T(8,128)(2,1)} %get-tuple-element.40), channel_id=1, source_target_pairs={{0,14},{1,15},{2,12},{3,13},{4,10},{5,11},{6,8},{7,9},{8,6},{9,7},... | collective-permute-start | bytes 196616 | tf_op jit(solution)/shard_map/ppermute | solution.py:299
  30.2 1.7 %copy-start.11 = (bf16[2,9,128,512]{3,2,1,0:T(8,128)(2,1)S(1)}, bf16[2,9,128,512]{3,2,1,0:T(8,128)(2,1)}, u32[]{:S(2)}) copy-start(bf16[2,9,128,512]{3,2,1,0:T(8,128)(2,1)} %copy-done.10) | copy-start | bytes 7077892
  31.9 5.6 %copy-start.12 = (bf16[2,9,128,512]{3,2,1,0:T(8,128)(2,1)S(1)}, bf16[2,9,128,512]{3,2,1,0:T(8,128)(2,1)}, u32[]{:S(2)}) copy-start(bf16[2,9,128,512]{3,2,1,0:T(8,128)(2,1)} %copy-done.10) | copy-start | bytes 7077892
  31.9 5.6 %copy-start.16 = (bf16[2,128,128]{2,1,0:T(8,128)(2,1)S(1)}, bf16[2,128,128]{2,1,0:T(8,128)(2,1)}, u32[]{:S(2)}) copy-start(bf16[2,128,128]{2,1,0:T(8,128)(2,1)} %copy-done.15) | copy-start | bytes 196612
  34.7 7.4 %collective-permute-start.9 = (bf16[1152,128]{1,0:T(8,128)(2,1)S(1)}, bf16[1152,128]{1,0:T(8,128)(2,1)S(1)}, u32[]{:S(2)}, u32[]{:S(2)}) collective-permute-start(bf16[1152,128]{1,0:T(8,128)(2,1)S(1)} %shard_map.97.ha), channel_id=1, source_target_pairs={{0,16},{16,0},{1,17},{17,1},{2,18},{18,2},{3,19},{19,3},{4,20},{20... | collective-permute-start | bytes 884744 | tf_op jit(solution)/shard_map/ppermute | solution.py:375
  37.5 4.6 %copy-start.4 = (bf16[3,128,256]{2,1,0:T(8,128)(2,1)S(1)}, bf16[3,128,256]{2,1,0:T(8,128)(2,1)}, u32[]{:S(2)}) copy-start(bf16[3,128,256]{2,1,0:T(8,128)(2,1)} %tw.3) | copy-start | bytes 589828
  37.5 4.6 %copy-start.14 = (bf16[2,1152,128]{2,1,0:T(8,128)(2,1)S(1)}, bf16[2,1152,128]{2,1,0:T(8,128)(2,1)}, u32[]{:S(2)}) copy-start(bf16[2,1152,128]{2,1,0:T(8,128)(2,1)} %cot.1) | copy-start | bytes 1769476
  37.5 4.6 %copy-start.18 = (f32[256]{0:T(256)S(1)}, f32[256]{0:T(256)}, u32[]{:S(2)}) copy-start(f32[256]{0:T(256)} %param.15) | copy-start | bytes 3076
  45.9 7.3 %collective-permute-start.10 = (bf16[1152,128]{1,0:T(8,128)(2,1)S(1)}, bf16[1152,128]{1,0:T(8,128)(2,1)S(1)}, u32[]{:S(2)}, u32[]{:S(2)}) collective-permute-start(bf16[1152,128]{1,0:T(8,128)(2,1)S(1)} %get-tuple-element.44), channel_id=1, source_target_pairs={{0,16},{16,0},{1,17},{17,1},{2,18},{18,2},{3,19},{19,3},{4,20},{20... | collective-permute-start | bytes 884744 | tf_op jit(solution)/shard_map/ppermute | solution.py:411
  47.4 32.0 %all-to-all-start.1 = ((bf16[16,128,128]{2,1,0:T(8,128)(2,1)}), bf16[16,128,128]{2,1,0:T(8,128)(2,1)S(1)}, u32[]{:S(2)}, u32[]{:S(2)}) async-start(bf16[16,128,128]{2,1,0:T(8,128)(2,1)} %get-tuple-element.55), calls=%async_computation.1 | async-start | bytes 1048576 | tf_op jit(solution)/shard_map/all_to_all | solution.py:293
  53.2 1.7 %copy-start.13 = (bf16[2,9,128,512]{3,2,1,0:T(8,128)(2,1)S(1)}, bf16[2,9,128,512]{3,2,1,0:T(8,128)(2,1)}, u32[]{:S(2)}) copy-start(bf16[2,9,128,512]{3,2,1,0:T(8,128)(2,1)} %copy-done.10) | copy-start | bytes 7077892
  54.9 23.9 %copy-start.9 = (s32[2,1,16]{2,1,0:T(1,128)S(1)}, s32[2,1,16]{2,1,0:T(1,128)}, u32[]{:S(2)}) copy-start(s32[2,1,16]{2,1,0:T(1,128)} %send.7) | copy-start | bytes 388
  56.5 7.8 %collective-permute-start.11 = (bf16[2,128,128]{2,1,0:T(8,128)(2,1)S(1)}, bf16[2,128,128]{2,1,0:T(8,128)(2,1)S(1)}, u32[]{:S(2)}, u32[]{:S(2)}) collective-permute-start(bf16[2,128,128]{2,1,0:T(8,128)(2,1)S(1)} %get-tuple-element.46), channel_id=1, source_target_pairs={{0,2},{1,3},{2,0},{3,1},{4,6},{5,7},{6,4},{7,5},{8,10},{9,11},{10,... | collective-permute-start | bytes 196616 | tf_op jit(solution)/shard_map/ppermute | solution.py:299
  58.5 9.1 %collective-permute-start.12 = (bf16[2,128,128]{2,1,0:T(8,128)(2,1)S(1)}, bf16[2,128,128]{2,1,0:T(8,128)(2,1)S(1)}, u32[]{:S(2)}, u32[]{:S(2)}) collective-permute-start(bf16[2,128,128]{2,1,0:T(8,128)(2,1)S(1)} %get-tuple-element.47), channel_id=1, source_target_pairs={{0,4},{1,5},{2,6},{3,7},{4,0},{5,1},{6,2},{7,3},{8,12},{9,13},{10,... | collective-permute-start | bytes 196616 | tf_op jit(solution)/shard_map/ppermute | solution.py:299
  59.9 9.1 %collective-permute-start.13 = (bf16[2,128,128]{2,1,0:T(8,128)(2,1)S(1)}, bf16[2,128,128]{2,1,0:T(8,128)(2,1)S(1)}, u32[]{:S(2)}, u32[]{:S(2)}) collective-permute-start(bf16[2,128,128]{2,1,0:T(8,128)(2,1)S(1)} %get-tuple-element.48), channel_id=1, source_target_pairs={{0,6},{1,7},{2,4},{3,5},{4,2},{5,3},{6,0},{7,1},{8,14},{9,15},{10,... | collective-permute-start | bytes 196616 | tf_op jit(solution)/shard_map/ppermute | solution.py:299
  60.3 15.7 %collective-permute-start.14 = (bf16[2,128,128]{2,1,0:T(8,128)(2,1)S(1)}, bf16[2,128,128]{2,1,0:T(8,128)(2,1)S(1)}, u32[]{:S(2)}, u32[]{:S(2)}) collective-permute-start(bf16[2,128,128]{2,1,0:T(8,128)(2,1)S(1)} %get-tuple-element.49), channel_id=1, source_target_pairs={{0,8},{1,9},{2,10},{3,11},{4,12},{5,13},{6,14},{7,15},{8,0},{9,1},... | collective-permute-start | bytes 196616 | tf_op jit(solution)/shard_map/ppermute | solution.py:299
  63.2 15.1 %collective-permute-start.15 = (bf16[2,128,128]{2,1,0:T(8,128)(2,1)S(1)}, bf16[2,128,128]{2,1,0:T(8,128)(2,1)S(1)}, u32[]{:S(2)}, u32[]{:S(2)}) collective-permute-start(bf16[2,128,128]{2,1,0:T(8,128)(2,1)S(1)} %get-tuple-element.50), channel_id=1, source_target_pairs={{0,10},{1,11},{2,8},{3,9},{4,14},{5,15},{6,12},{7,13},{8,2},{9,3},... | collective-permute-start | bytes 196616 | tf_op jit(solution)/shard_map/ppermute | solution.py:299
  64.3 14.0 %collective-permute-start.16 = (bf16[2,128,128]{2,1,0:T(8,128)(2,1)S(1)}, bf16[2,128,128]{2,1,0:T(8,128)(2,1)S(1)}, u32[]{:S(2)}, u32[]{:S(2)}) collective-permute-start(bf16[2,128,128]{2,1,0:T(8,128)(2,1)S(1)} %get-tuple-element.51), channel_id=1, source_target_pairs={{0,12},{1,13},{2,14},{3,15},{4,8},{5,9},{6,10},{7,11},{8,4},{9,5},... | collective-permute-start | bytes 196616 | tf_op jit(solution)/shard_map/ppermute | solution.py:299
  67.6 10.7 %collective-permute-start.17 = (bf16[2,128,128]{2,1,0:T(8,128)(2,1)S(1)}, bf16[2,128,128]{2,1,0:T(8,128)(2,1)S(1)}, u32[]{:S(2)}, u32[]{:S(2)}) collective-permute-start(bf16[2,128,128]{2,1,0:T(8,128)(2,1)S(1)} %get-tuple-element.52), channel_id=1, source_target_pairs={{0,14},{1,15},{2,12},{3,13},{4,10},{5,11},{6,8},{7,9},{8,6},{9,7},... | collective-permute-start | bytes 196616 | tf_op jit(solution)/shard_map/ppermute | solution.py:299
  78.7 1.7 %collective-permute-start.18 = (bf16[8,128,128]{2,1,0:T(8,128)(2,1)S(1)}, bf16[8,128,128]{2,1,0:T(8,128)(2,1)S(1)}, u32[]{:S(2)}, u32[]{:S(2)}) collective-permute-start(bf16[8,128,128]{2,1,0:T(8,128)(2,1)S(1)} %shard_map.103), channel_id=1, source_target_pairs={{0,1},{1,0},{2,3},{3,2},{4,5},{5,4},{6,7},{7,6},{8,9},{9,8},{10,11... | collective-permute-start | bytes 786440 | tf_op jit(solution)/shard_map/ppermute | solution.py:290

commit v3 on v2

--- a/solution.py
+++ b/solution.py
@@ -12,10 +12,11 @@
 VMEM = pl.BlockSpec(memory_space=pltpu.VMEM)
 SMEM = pl.BlockSpec(memory_space=pltpu.SMEM)
 HBM = pl.BlockSpec(memory_space=pltpu.MemorySpace.HBM)
+TILE = 384
 VMEM_LIMIT = 16 * 1024 * 1024
 DMA = pltpu.SemaphoreType.DMA
-FORWARD = (1, 2, 3, 4, 5, 6, 7)
-BACKWARD = (2, 7, 6, 5, 4, 3, 1)
+FORWARD = (1, 2, 3, 5, 4, 7, 6)
+BACKWARD = (1, 2, 3, 5, 4, 7, 6)
 COST = 100
 
 
@@ -29,6 +30,14 @@
 
 def shape(dims, dtype=BF16):
     return jax.ShapeDtypeStruct(dims, dtype)
+
+
+def shape_hbm(dims, dtype=BF16):
+    return pltpu.MemorySpace.HBM(dims, dtype)
+
+
+def in_hbm(values):
+    return pltpu.with_memory_space_constraint(values, pltpu.MemorySpace.HBM)
 
 
 def call(body, outs, in_specs, out_specs, scratch=(), flops=0, moved=0):
@@ -64,27 +73,33 @@
 
 def wanted(lists, feats, snap, target, block):
     start = pl.multiple_of(jnp.maximum(lists[snap, 0, target], 0) * block, block)
-    return feats.at[snap, pl.ds(start, block)]
-
-
-def pack_inner_body(domains, block, lists, feats, out, send, sem):
-    run_copies([(lists, send)], sem)
+    return feats.at[pl.ds(start, block)]
+
+
+def pack_inner_body(domains, block, lists, feats, out, held, send, sem):
     ia = inner_index()
-    run_copies([(wanted(send, feats, ia, d, block), out.at[d]) for d in range(domains)], sem)
-
-
-def pack_outer_body(chips, block, send, partner_send, feats, partner_feats, *rest):
-    outs, (lists, sem) = rest[:-2], rest[-2:]
-    run_copies([(send, lists.at[0]), (partner_send, lists.at[1])], sem)
-    send, partner_send = lists.at[0], lists.at[1]
+    run_copies([(lists, send), (feats.at[ia], held)], sem)
+    pairs = [(wanted(send, held, ia, d, block), out.at[d]) for d in range(domains)]
+    run_copies(pairs, sem)
+
+
+def pack_outer_body(chips, block, lists, partner_lists, feats, partner_feats, *rest):
+    outs, (held, partner_held, send, partner_send, sem) = rest[:-5], rest[-5:]
     chip, core = split_index()
     ib = 1 - inner_index()
-    pairs = []
+    run_copies(
+        [
+            (lists, send),
+            (partner_lists, partner_send),
+            (feats.at[ib], held),
+            (partner_feats.at[ib], partner_held),
+        ],
+        sem,
+    )
     for offset in range(chips):
         target = 2 * jnp.bitwise_xor(chip, offset) + core
-        pairs.append((wanted(send, feats, ib, target, block), outs[offset].at[0]))
-        pairs.append((wanted(partner_send, partner_feats, ib, target, block), outs[offset].at[1]))
-    run_copies(pairs, sem)
+        outs[offset][0] = wanted(send, held, ib, target, block)[...]
+        outs[offset][1] = wanted(partner_send, partner_held, ib, target, block)[...]
 
 
 def collect_body(picks, *refs):
@@ -92,19 +107,9 @@
     run_copies([(sources[i].at[j], out.at[n]) for n, (i, j) in enumerate(picks)], sem)
 
 
-def prep_body(slots, per_step, adj, tw, sw, rows_out, twt, wide):
-    block = adj.shape[2]
-
-    @pl.when(pl.program_id(0) == 0)
-    def _():
-        for tap in range(tw.shape[0]):
-            twt[tap] = tw[tap].astype(F32).T.astype(BF16)
-
-    wide[...] = adj[0].astype(F32)
-    for n in range(per_step):
-        for slot in range(slots):
-            tile = wide[pl.ds(n * slots * block + slot, block, stride=slots), :]
-            rows_out[0, n, :, slot * block : (slot + 1) * block] = tile.astype(BF16)
+def turn_body(tw, twt):
+    for tap in range(tw.shape[0]):
+        twt[tap] = tw[tap].astype(F32).T.astype(BF16)
 
 
 def position(column, chips, blocks_here, plain):
@@ -116,34 +121,47 @@
     return which * chips + jnp.bitwise_xor(part // 2, chip)
 
 
-def aggregate(plain, snap, chips, blocks_here, slots, cols, own, adj, halo, agg, sw, hidden):
-    block = halo.shape[1]
+def side_by_side(snap, slots, adj, wide, tiles):
+    blocks_here, block = tiles.shape[:2]
+    rows = slots * block
+    for j in range(blocks_here):
+        wide[j % 2] = adj[snap, j * rows : (j + 1) * rows, :].astype(F32)
+        for slot in range(slots):
+            tile = wide[j % 2, pl.ds(slot, block, stride=slots), :]
+            tiles[j, :, slot * block : (slot + 1) * block] = tile.astype(BF16)
+
+
+def aggregate(plain, snap, chips, slots, cols, own, tiles, halo, agg, sw, hidden):
+    blocks_here, block = tiles.shape[:2]
     for j in range(blocks_here):
         rows = slice(j * block, (j + 1) * block)
         pieces = [own[rows, :]]
         for slot in range(1, slots):
             pieces.append(halo[position(cols[snap, slot, j], chips, blocks_here, plain)])
-        agg[rows, :] = dot(adj[j], jnp.concatenate(pieces, axis=0)).astype(BF16)
+        agg[rows, :] = dot(tiles[j], jnp.concatenate(pieces, axis=0)).astype(BF16)
     hidden[...] = dot(agg[...], sw[...]).astype(BF16)
 
 
-def hidden_inner_body(chips, blocks_here, slots, cols, feats, tiles, sw, arrived, *rest):
-    hidden, own, adj, halo, agg, sem = rest
-    ia = inner_index()
-    run_copies([(feats.at[ia], own), (tiles.at[ia], adj), (arrived, halo)], sem)
-    aggregate(True, ia, chips, blocks_here, slots, cols, own, adj, halo, agg, sw, hidden)
-
-
-def hidden_outer_body(chips, blocks_here, slots, cols, feats, tiles, sw, *rest):
-    arrived = rest[:chips]
-    hidden, own, adj, halo, agg, sem = rest[chips:]
-    ib = 1 - inner_index()
-    pairs = [(feats.at[ib], own), (tiles.at[ib], adj)]
-    for offset in range(chips):
-        for which in range(2):
-            pairs.append((arrived[offset].at[which], halo.at[which * chips + offset]))
-    run_copies(pairs, sem)
-    aggregate(False, ib, chips, blocks_here, slots, cols, own, adj, halo, agg, sw, hidden)
+def hidden_body(inner, chips, slots, cols, feats, adj, sw, *rest):
+    arrived, rest = rest[:-7], rest[-7:]
+    hidden, own, wide, tiles, halo, agg, sem = rest
+    snap = inner_index() if inner else 1 - inner_index()
+    pairs = [(feats.at[snap], own)]
+    if inner:
+        pairs.append((arrived[0], halo))
+    else:
+        for offset, source in zip((0,) + FORWARD, arrived):
+            for which in range(2):
+                pairs.append((source.at[which], halo.at[which * chips + offset]))
+    copies = [
+        pltpu.make_async_copy(source, target, sem.at[i]) for i, (source, target) in enumerate(pairs)
+    ]
+    for copy in copies:
+        copy.start()
+    side_by_side(snap, slots, adj, wide, tiles)
+    for copy in copies:
+        copy.wait()
+    aggregate(inner, snap, chips, slots, cols, own, tiles, halo, agg, sw, hidden)
 
 
 def spread(plain, snap, chips, blocks_here, slots, cols, grad, sw, adj, local, acc):
@@ -159,13 +177,11 @@
 
 
 def temporal_body(
-    chips, blocks_here, slots, tile, cols, ha, hb, hn, cot, tw, twt, bias, sw, tiles, *rest
+    chips, blocks_here, slots, tile, cols, ha, hb, hn, cot, tw, twt, bias, sw, raw, *rest
 ):
-    shares, out, partial, rest_a, local, grad, acc, adj, sem = rest
+    shares, out, partial, rest_a, local, grad, acc, adj, wide, sem, held, held_shares = rest
     ia = inner_index()
     ib = 1 - ia
-    fetch = pltpu.make_async_copy(tiles.at[ib], adj, sem)
-    fetch.start()
     flip = lax.axis_index("snap")
     lo, hi = 2 * flip, 2 - 2 * flip
     items, channels = ha.shape
@@ -189,7 +205,7 @@
             gate = jax.nn.sigmoid(mix[:, channels:])
             up = cot[index, rows, :].astype(F32)
             gated = linear * gate
-            out[index, rows, :] = gated.astype(BF16)
+            held[index, rows, :] = gated.astype(BF16)
             first = up * gate
             second = up * gated * (1.0 - gate)
             grads.append(jnp.concatenate([first.astype(BF16), second.astype(BF16)], axis=1))
@@ -199,19 +215,27 @@
         partial[rows, :] = from_a[:, :channels].astype(BF16)
         rest_a[rows, :] = from_a[:, channels:] + from_b[:, :channels]
         grad[rows, :] = (dot(ga, twt[lo]) + from_b[:, channels:]).astype(BF16)
-    fetch.wait()
+    emit = pltpu.make_async_copy(held, out, sem.at[2])
+    emit.start()
+    side_by_side(ib, slots, raw, wide, adj)
     spread(True, ib, chips, blocks_here, slots, cols, grad, sw, adj, local, acc)
-    shares[...] = acc[...].astype(BF16)
-
-
-def inner_body(chips, blocks_here, slots, cols, rest_a, partial, sw, tiles, *rest):
+    half = acc.shape[0] // 2
+    copies = [emit]
+    for n in range(2):
+        some = pl.ds(n * half, half)
+        held_shares[some] = acc[some].astype(BF16)
+        copies.append(pltpu.make_async_copy(held_shares.at[some], shares.at[some], sem.at[n]))
+        copies[-1].start()
+    for copy in copies:
+        copy.wait()
+
+
+def inner_body(chips, blocks_here, slots, cols, rest_a, partial, sw, raw, *rest):
     outs = rest[:chips]
-    local, grad, acc, adj, sem = rest[chips:]
+    local, grad, acc, adj, wide = rest[chips:]
     ia = inner_index()
-    fetch = pltpu.make_async_copy(tiles.at[ia], adj, sem)
-    fetch.start()
+    side_by_side(ia, slots, raw, wide, adj)
     grad[...] = (rest_a[...] + partial[...].astype(F32)).astype(BF16)
-    fetch.wait()
     spread(False, ia, chips, blocks_here, slots, cols, grad, sw, adj, local, acc)
     for offset in range(chips):
         for which in range(2):
@@ -247,20 +271,24 @@
 
 def final_inner_body(chips, send, local, *rest):
     arrived, acc = rest[: chips - 1], rest[chips - 1]
-    terms = [(source_of(offset, 0), arrived[offset - 1].at[0]) for offset in range(1, chips)]
+    terms = [(source_of(offset, 0), value.at[0]) for offset, value in zip(BACKWARD, arrived)]
     add_shares(inner_index(), send, local, terms, acc)
 
 
-def last_body(chips, send, part, swapped, outer, out, acc, sem):
+def last_body(chips, send, part, swapped, outer, out, acc, held, sem):
     ia = inner_index()
-    move = pltpu.make_async_copy(outer, out.at[1 - ia], sem.at[0])
-    move.start()
-    terms = [(source_of(offset, 1), swapped.at[offset]) for offset in range(chips)]
+    copies = [pltpu.make_async_copy(outer, out.at[1 - ia], sem.at[0])]
+    copies[0].start()
+    terms = [(source_of(o, 1), swapped.at[n]) for n, o in enumerate((0,) + BACKWARD)]
     add_shares(ia, send, part, terms, acc)
     block = acc.shape[1]
     for n in range(acc.shape[0]):
-        out[ia, n * block : (n + 1) * block, :] = finish_rows(acc, n)
-    move.wait()
+        rows = pl.ds(n * block, block)
+        held[rows, :] = finish_rows(acc, n)
+        copies.append(pltpu.make_async_copy(held.at[rows], out.at[ia, rows], sem.at[n + 1]))
+        copies[-1].start()
+    for copy in copies:
+        copy.wait()
 
 
 def local_pair(
@@ -297,7 +325,7 @@
         for offset in order:
             pairs = [(i, i ^ (2 * offset)) for i in range(domains)]
             done[offset] = lax.ppermute(payloads[offset], "dom", pairs)
-        return [done[offset] for offset in sorted(done)]
+        return [done[offset] for offset in order]
 
     cols = jnp.swapaxes(block_cols, 1, 2)
     partner_send = swap_cores(send_lists)
@@ -305,12 +333,16 @@
 
     packed_a = call(
         functools.partial(pack_inner_body, domains, block),
-        shape((domains, block, channels)),
+        shape_hbm((domains, block, channels)),
         [HBM] * 2,
         HBM,
-        [pltpu.SMEM(send_lists.shape, jnp.int32), DMA((domains,))],
+        [
+            pltpu.VMEM((items_here, channels), BF16),
+            pltpu.SMEM(send_lists.shape, jnp.int32),
+            DMA((domains,)),
+        ],
         moved=2 * domains * block_bytes,
-    )(send_lists, features)
+    )(in_hbm(send_lists), in_hbm(features))
     packed_a, partner_send, partner_feats = lax.optimization_barrier(
         (packed_a, partner_send, partner_feats)
     )
@@ -319,81 +351,74 @@
         functools.partial(pack_outer_body, chips, block),
         [two] * chips,
         [HBM] * 4,
-        [HBM] * chips,
-        [pltpu.SMEM((2, *send_lists.shape), jnp.int32), DMA((domains,))],
+        [VMEM] * chips,
+        [
+            pltpu.VMEM((items_here, channels), BF16),
+            pltpu.VMEM((items_here, channels), BF16),
+            pltpu.SMEM(send_lists.shape, jnp.int32),
+            pltpu.SMEM(send_lists.shape, jnp.int32),
+            DMA((4,)),
+        ],
         moved=2 * domains * block_bytes,
-    )(send_lists, partner_send, features, partner_feats)
+    )(*(in_hbm(v) for v in (send_lists, partner_send, features, partner_feats)))
     got_b = [packed[0]] + to_chips(packed, FORWARD)
 
-    per_step = 3 if blocks_here % 3 == 0 else 1
-    groups = blocks_here // per_step
     tile_rows = block * slots
     adj_flat = adjacency.reshape(snaps_here, items_here * slots, block)
-    tiles, twt = pl.pallas_call(
-        functools.partial(prep_body, slots, per_step),
-        grid=(snaps_here * groups,),
-        in_specs=[
-            pl.BlockSpec((1, per_step * tile_rows, block), lambda i: (i // groups, i % groups, 0)),
-            pl.BlockSpec((taps, channels, doubled), lambda i: (0, 0, 0)),
-            pl.BlockSpec((channels, channels), lambda i: (0, 0)),
-        ],
-        out_specs=[
-            pl.BlockSpec(
-                (1, per_step, block, tile_rows), lambda i: (i // groups, i % groups, 0, 0)
-            ),
-            pl.BlockSpec((taps, doubled, channels), lambda i: (0, 0, 0)),
-        ],
-        out_shape=[
-            shape((snaps_here, blocks_here, block, tile_rows)),
-            shape((taps, doubled, channels)),
-        ],
-        scratch_shapes=[pltpu.VMEM((per_step * tile_rows, block), F32)],
-        compiler_params=pltpu.CompilerParams(vmem_limit_bytes=VMEM_LIMIT),
-        cost_estimate=pl.CostEstimate(
-            flops=0, bytes_accessed=2 * adj_flat.size * 2, transcendentals=0
-        ),
-    )(adj_flat, temporal_weight, spatial_weight)
-
-    def hidden_of(body, arrived):
+    twt = call(
+        turn_body,
+        shape((taps, doubled, channels)),
+        [VMEM],
+        VMEM,
+        moved=4 * taps * channels * doubled,
+    )(temporal_weight)
+
+    def hidden_of(inner, arrived):
         return call(
-            functools.partial(body, chips, blocks_here, slots),
+            functools.partial(hidden_body, inner, chips, slots),
             shape((items_here, channels)),
-            [SMEM, HBM, HBM, VMEM] + [HBM] * len(arrived),
+            [SMEM, HBM, VMEM, VMEM] + [HBM] * len(arrived),
             VMEM,
             [
                 pltpu.VMEM((items_here, channels), BF16),
+                pltpu.VMEM((2, tile_rows, block), F32),
                 pltpu.VMEM((blocks_here, block, tile_rows), BF16),
                 pltpu.VMEM((domains, block, channels), BF16),
                 pltpu.VMEM((items_here, channels), BF16),
-                DMA((domains + 2,)),
+                DMA((domains + 1,)),
             ],
             flops=(slots + 1) * item_flops,
             moved=(slots + 4) * items_here * channels * 2,
-        )(cols, features, tiles, spatial_weight, *arrived)
-
-    hidden_a = hidden_of(hidden_inner_body, [got_a])
+        )(cols, features, adj_flat, spatial_weight, *(in_hbm(v) for v in arrived))
+
+    hidden_a = hidden_of(True, [got_a])
     hidden_n = lax.ppermute(hidden_a, "snap", other_snap)
-    hidden_b = hidden_of(hidden_outer_body, got_b)
+    hidden_b = hidden_of(False, got_b)
 
     back_scratch = [
         pltpu.VMEM((items_here, channels), BF16),
         pltpu.VMEM((domains, block, channels), F32),
         pltpu.VMEM((blocks_here, block, tile_rows), BF16),
-        DMA,
+        pltpu.VMEM((2, tile_rows, block), F32),
     ]
     local_shape = shape((blocks_here, block, channels), F32)
     shares_b, output, partial, rest_a, local_b = call(
-        functools.partial(temporal_body, chips, blocks_here, slots, per_step * block),
+        functools.partial(temporal_body, chips, blocks_here, slots, TILE),
         [
-            shape((domains, block, channels)),
-            shape((snaps_here, items_here, channels)),
+            shape_hbm((domains, block, channels)),
+            shape_hbm((snaps_here, items_here, channels)),
             shape((items_here, channels)),
             shape((items_here, channels), F32),
             local_shape,
         ],
-        [SMEM] + [VMEM] * 8 + [HBM],
-        [VMEM] * 5,
-        back_scratch,
+        [SMEM] + [VMEM] * 9,
+        [HBM] * 2 + [VMEM] * 3,
+        back_scratch
+        + [
+            DMA((3,)),
+            pltpu.VMEM((snaps_here, items_here, channels), BF16),
+            pltpu.VMEM((domains, block, channels), BF16),
+        ],
         flops=26 * item_flops,
         moved=20 * items_here * channels * 2,
     )(
@@ -406,7 +431,7 @@
         twt,
         temporal_bias.reshape(1, doubled),
         spatial_weight,
-        tiles,
+        adj_flat,
     )
     partial_n = lax.ppermute(partial, "snap", other_snap)
     back_b = exchange(shares_b)
@@ -414,12 +439,12 @@
     results = call(
         functools.partial(inner_body, chips, blocks_here, slots),
         [two] * chips + [local_shape],
-        [SMEM] + [VMEM] * 3 + [HBM],
+        [SMEM] + [VMEM] * 4,
         [VMEM] * (chips + 1),
         back_scratch,
         flops=(slots + 1) * item_flops,
         moved=12 * items_here * channels * 2,
-    )(cols, rest_a, partial_n, spatial_weight, tiles)
+    )(cols, rest_a, partial_n, spatial_weight, adj_flat)
     shares_a, local_a = results[:chips], results[chips]
     back_a = to_chips(shares_a, BACKWARD)
     swapped = swap_cores(
@@ -452,10 +477,10 @@
     )(send_lists, local_a, *back_a)
     input_grad = call(
         functools.partial(last_body, chips),
-        shape((snaps_here, items_here, channels)),
+        shape_hbm((snaps_here, items_here, channels)),
         [SMEM] + [VMEM] * 3,
-        VMEM,
-        [acc, DMA((1,))],
+        HBM,
+        [acc, pltpu.VMEM((items_here, channels), BF16), DMA((blocks_here + 1,))],
         **cost,
     )(send_lists, part, swapped, grad_b)
     return output, input_grad

time: 83.4 us -> 79.5 us (0.953)
  local copies, waits for them, and re-layouts: 9.51 us -> 3.71 us
  starting transfers between devices: 40.6 us -> 42.8 us
  Pallas kernels: 19.1 us -> 18.2 us
    unnamed x38 -> x30, local copies, waits for them, and re-layouts: 9.51 us -> 3.71 us
    ppermute x14, waiting for transfers between devices: 10.5 us -> 12.7 us  [to_chips(): done[offset] = lax.ppermute(payloads[offset], 'dom', pairs)]
    ppermute x1, waiting for transfers between devices: 1.52 us -> 0.01 us  [local_pair(): hidden_n = lax.ppermute(hidden_a, 'snap', other_snap)]
    all_to_all x2, starting transfers between devices: 13.2 us -> 14.7 us  [exchange(): lax.all_to_all(values, 'dom', split_axis=0, concat_axis=0, tiled=True)]
    pallas_call x6, Pallas kernels: 13.8 us -> 12.8 us  [the longest x2 5.18 us: hidden_of(): call(functools.partial(hidden_body, inner, chips, slots), shape((items_he...]
  transfers between devices with their start and end apart: 21 -> 21, of which waited for: 4 -> 4; matrix products, arithmetic and copies ran while one was open for 0% -> 0% of each run, Pallas kernels for 16% -> 17%
where the time goes in v3:
time: 79.5 us; the launch traced here: 78.4 us
  starting transfers between devices  42.8 us (54%)
  Pallas kernels  18.2 us (23%)
  waiting for transfers between devices  12.7 us (16%)
  local copies, waits for them, and re-layouts  3.71 us (5%)
  between operations  0.94 us (1%)
    ppermute x14, starting transfers between devices, to_chips(): done[offset] = lax.ppermute(payloads[offset], 'dom', pairs)  24.4 us
    all_to_all x2, starting transfers between devices, exchange(): lax.all_to_all(values, 'dom', split_axis=0, concat_axis=0, tiled=True)  14.7 us
    ppermute x14, waiting for transfers between devices, to_chips(): done[offset] = lax.ppermute(payloads[offset], 'dom', pairs)  12.7 us
    pallas_call x2, Pallas kernels, hidden_of(): call(functools.partial(hidden_body, inner, chips, slots), shape((items_he...  5.18 us
    unnamed x30, local copies, waits for them, and re-layouts  3.71 us
    pallas_call x1, Pallas kernels, local_pair(): call(functools.partial(temporal_body, chips, blocks_here, slots, TILE), [...  3.63 us
    pallas_call x1, Pallas kernels, local_pair(): call(functools.partial(pack_inner_body, domains, block), shape_hbm((domai...  2.29 us
    pallas_call x1, Pallas kernels, local_pair(): call(functools.partial(pack_outer_body, chips, block), [two] * chips, [HB...  1.78 us
  transfers between devices with their start and end apart: 21, of which 4 were waited for; matrix products, arithmetic and copies ran while one was open for 0% of the time, Pallas kernels for 17%

profile of v3, /device:TPU:0, one launch (start us, length us, event | category | flops | bytes accessed | tf_op | source)
XLA Modules:
  0.0 78.4 jit_solution(10831584373070843696)
XLA Ops:
  0.6 0.0 copy-start
  0.7 0.0 copy-start.3
  0.7 0.5 collective-permute-start.1
  1.2 0.1 collective-permute-start
  1.3 2.3 %shard_map.95 = bf16[16,128,128]{2,1,0:T(8,128)(2,1)} custom-call(s32[2,1,16]{2,1,0:T(1,128)} %send.5, bf16[2,1152,128]{2,1,0:T(8,128)(2,1)} %feats.7), custom_call_target="tpu_custom_call" | custom-call | bytes 104857600 | tf_op jit(solution)/shard_map/pallas_call | solution.py:334
  3.6 0.0 collective-permute-done.partner_lists
  3.6 0.0 collective-permute-done.1.partner_feats
  3.6 7.4 %all-to-all-start = ((bf16[16,128,128]{2,1,0:T(8,128)(2,1)}), bf16[16,128,128]{2,1,0:T(8,128)(2,1)}, u32[]{:S(2)}, u32[]{:S(2)}) async-start(bf16[16,128,128]{2,1,0:T(8,128)(2,1)} %shard_map.95), calls=%async_computation | async-start | bytes 1048576 | tf_op jit(solution)/shard_map/all_to_all | solution.py:321
  11.0 1.8 %shard_map.97 = (bf16[2,128,128]{2,1,0:T(8,128)(2,1)S(1)}, bf16[2,128,128]{2,1,0:T(8,128)(2,1)S(1)}, bf16[2,128,128]{2,1,0:T(8,128)(2,1)S(1)}, bf16[2,128,128]{2...) custom-call(s32[2,1,16]{2,1,0:T(1,128)} %send.5, ...), custom_call_target="tpu_custom_call" | custom-call | bytes 104857600 | tf_op jit(solution)/shard_map/pallas_call | solution.py:350
  12.8 0.6 copy-done.7
  13.4 1.9 %collective-permute-start.2 = (bf16[2,128,128]{2,1,0:T(8,128)(2,1)S(1)}, bf16[2,128,128]{2,1,0:T(8,128)(2,1)S(1)}, u32[]{:S(2)}, u32[]{:S(2)}) collective-permute-start(bf16[2,128,128]{2,1,0:T(8,128)(2,1)S(1)} %get-tuple-element.31), channel_id=1, source_target_pairs={{0,2},{1,3},{2,0},{3,1},{4,6},{5,7},{6,4},{7,5},{8,10},{9,11},{10,... | collective-permute-start | bytes 196616 | tf_op jit(solution)/shard_map/ppermute | solution.py:327
  15.3 1.5 %collective-permute-start.3 = (bf16[2,128,128]{2,1,0:T(8,128)(2,1)S(1)}, bf16[2,128,128]{2,1,0:T(8,128)(2,1)S(1)}, u32[]{:S(2)}, u32[]{:S(2)}) collective-permute-start(bf16[2,128,128]{2,1,0:T(8,128)(2,1)S(1)} %get-tuple-element.32), channel_id=1, source_target_pairs={{0,4},{1,5},{2,6},{3,7},{4,0},{5,1},{6,2},{7,3},{8,12},{9,13},{10,... | collective-permute-start | bytes 196616 | tf_op jit(solution)/shard_map/ppermute | solution.py:327
  16.8 0.1 shard_map.99.twt
  16.9 0.2 collective-permute-start.4
  17.1 3.7 %collective-permute-start.5 = (bf16[2,128,128]{2,1,0:T(8,128)(2,1)}, bf16[2,128,128]{2,1,0:T(8,128)(2,1)}, u32[]{:S(2)}, u32[]{:S(2)}) collective-permute-start(bf16[2,128,128]{2,1,0:T(8,128)(2,1)} %get-tuple-element.34), channel_id=1, source_target_pairs={{0,10},{1,11},{2,8},{3,9},{4,14},{5,15},{6,12},{7,13},{8,2},{9,3},... | collective-permute-start | bytes 196616 | tf_op jit(solution)/shard_map/ppermute | solution.py:327
  20.8 0.6 collective-permute-start.6
  21.4 0.0 collective-permute-done.2.rest_1_
  21.4 3.3 %collective-permute-start.7 = (bf16[2,128,128]{2,1,0:T(8,128)(2,1)S(1)}, bf16[2,128,128]{2,1,0:T(8,128)(2,1)}, u32[]{:S(2)}, u32[]{:S(2)}) collective-permute-start(bf16[2,128,128]{2,1,0:T(8,128)(2,1)S(1)} %get-tuple-element.36), channel_id=1, source_target_pairs={{0,14},{1,15},{2,12},{3,13},{4,10},{5,11},{6,8},{7,9},{8,6},{9,7},... | collective-permute-start | bytes 196616 | tf_op jit(solution)/shard_map/ppermute | solution.py:327
  24.6 0.0 collective-permute-done.3.rest_2_
  24.6 0.6 copy-done.14
  25.3 1.2 %collective-permute-start.8 = (bf16[2,128,128]{2,1,0:T(8,128)(2,1)S(1)}, bf16[2,128,128]{2,1,0:T(8,128)(2,1)}, u32[]{:S(2)}, u32[]{:S(2)}) collective-permute-start(bf16[2,128,128]{2,1,0:T(8,128)(2,1)S(1)} %get-tuple-element.37), channel_id=1, source_target_pairs={{0,12},{1,13},{2,14},{3,15},{4,8},{5,9},{6,10},{7,11},{8,4},{9,5},... | collective-permute-start | bytes 196616 | tf_op jit(solution)/shard_map/ppermute | solution.py:327
  26.5 0.0 all-to-all-done.rest_0_
  26.5 0.0 copy-start.8
  26.5 0.7 copy-done.8
  27.3 2.5 %shard_map.96.ha = bf16[1152,128]{1,0:T(8,128)(2,1)S(1)} custom-call(s32[2,4,9]{2,1,0:T(4,128)S(1)} %bitcast.7, bf16[2,1152,128]{2,1,0:T(8,128)(2,1)S(1)} %copy-done, bf16[2,4608,128]{2,1,0:T(8,128)(2,1)S(1)} %bitcast.3, bf16[128,128]{1,0:T(8,128)(2,1)S(1)} %copy-done.8, bf16[16,128,128]{2,1,0:T(8,128)(2,1)} %all-to-all-done.rest_0_), custom_call_target="tpu_custom_call" | custom-call | flops 18874368000 | bytes 235929600 | tf_op jit(solution)/shard_map/pallas_call | solution.py:377
  29.8 0.0 collective-permute-done.4.rest_3_
  29.8 1.6 %collective-permute-start.9 = (bf16[1152,128]{1,0:T(8,128)(2,1)S(1)}, bf16[1152,128]{1,0:T(8,128)(2,1)S(1)}, u32[]{:S(2)}, u32[]{:S(2)}) collective-permute-start(bf16[1152,128]{1,0:T(8,128)(2,1)S(1)} %shard_map.96.ha), channel_id=1, source_target_pairs={{0,16},{16,0},{1,17},{17,1},{2,18},{18,2},{3,19},{19,3},{4,20},{20... | collective-permute-start | bytes 884744 | tf_op jit(solution)/shard_map/ppermute | solution.py:395
  31.4 3.4 %collective-permute-done.5.rest_4_ = bf16[2,128,128]{2,1,0:T(8,128)(2,1)} collective-permute-done((bf16[2,128,128]{2,1,0:T(8,128)(2,1)}, bf16[2,128,128]{2,1,0:T(8,128)(2,1)}, u32[]{:S(2)}, u32[]{:S(2)}) %collective-permute-start.5) | collective-permute-done | bytes 65568 | tf_op jit(solution)/shard_map/ppermute | solution.py:327
  34.8 0.5 collective-permute-done.6.rest_5_
  35.3 0.0 collective-permute-done.7.rest_6_
  35.3 0.0 collective-permute-done.8.rest_7_
  35.3 0.0 copy-start.6
  35.3 0.0 copy-start.11
  35.3 2.7 %shard_map.98.hb = bf16[1152,128]{1,0:T(8,128)(2,1)S(1)} custom-call(s32[2,4,9]{2,1,0:T(4,128)S(1)} %bitcast.8, bf16[2,1152,128]{2,1,0:T(8,128)(2,1)S(1)} %copy-done, bf16[2,4608,128]{2,1,0:T(8,128)(2,1)S(1)} %bitcast.4, bf16[128,128]{1,0:T(8,128)(2,1)S(1)} %copy-done.8, bf16[2,128,128]{2,1,0:T(8,128)(2,1)} %copy-done.7, bf16[2,128,128]{2,1,0:T(8,128)(2,1)} %copy-done.13, ...), custom_call_target="tpu_custom_call" | custom-call | flops 18874368000 | bytes 235929600 | tf_op jit(solution)/shard_map/pallas_call | solution.py:377
  38.0 0.0 collective-permute-done.9.hn
  38.0 0.0 copy-start.9
  38.0 3.6 %shard_map.100 = (bf16[16,128,128]{2,1,0:T(8,128)(2,1)}, bf16[2,1152,128]{2,1,0:T(8,128)(2,1)}, bf16[1152,128]{1,0:T(8,128)(2,1)S(1)}, f32[1152,128]{1,0:T(8,128)S(1)}, f32[9,128,128]{2,1,0:T(8,128)S(1)}) custom-call(s32[2,4,9]{2,1,0:T(4,128)S(1)} %bitcast.9, bf16[1152,128]{1,0:T(8,128)(2,1)S(1)} %shard_map.96.ha, bf16[1152,128]{1,0:T(8,128)(2,1)S(1)} %shard_map.98.hb, ...), custom_call_target="tpu_custom_call" | custom-call | flops 98146713600 | bytes 589824000 | tf_op jit(solution)/shard_map/pallas_call | solution.py:405
  41.7 1.6 %collective-permute-start.10 = (bf16[1152,128]{1,0:T(8,128)(2,1)S(1)}, bf16[1152,128]{1,0:T(8,128)(2,1)S(1)}, u32[]{:S(2)}, u32[]{:S(2)}) collective-permute-start(bf16[1152,128]{1,0:T(8,128)(2,1)S(1)} %get-tuple-element.40), channel_id=1, source_target_pairs={{0,16},{16,0},{1,17},{17,1},{2,18},{18,2},{3,19},{19,3},{4,20},{20... | collective-permute-start | bytes 884744 | tf_op jit(solution)/shard_map/ppermute | solution.py:436
  43.2 7.3 %all-to-all-start.1 = ((bf16[16,128,128]{2,1,0:T(8,128)(2,1)}), bf16[16,128,128]{2,1,0:T(8,128)(2,1)S(1)}, u32[]{:S(2)}, u32[]{:S(2)}) async-start(bf16[16,128,128]{2,1,0:T(8,128)(2,1)} %get-tuple-element.51), calls=%async_computation.1 | async-start | bytes 1048576 | tf_op jit(solution)/shard_map/all_to_all | solution.py:321
  50.5 0.0 collective-permute-done.10.partial
  50.5 0.0 copy-start.5
  50.5 1.7 %copy-done.5 = bf16[2,1152,4,128]{3,2,1,0:T(4,128)(2,1)S(1)} copy-done((bf16[2,1152,4,128]{3,2,1,0:T(4,128)(2,1)S(1)}, bf16[2,1152,4,128]{3,2,1,0:T(4,128)(2,1)}, u32[]{:S(2)}) %copy-start.5) | copy-done | bytes 2359320
  52.2 1.6 %shard_map.101 = (bf16[2,128,128]{2,1,0:T(8,128)(2,1)S(1)}, bf16[2,128,128]{2,1,0:T(8,128)(2,1)S(1)}, bf16[2,128,128]{2,1,0:T(8,128)(2,1)S(1)}, bf16[2,128,128]{...) custom-call(s32[2,4,9]{2,1,0:T(4,128)S(1)} %bitcast.10, ...), custom_call_target="tpu_custom_call" | custom-call | flops 18874368000 | bytes 353894400 | tf_op jit(solution)/shard_map/pallas_call | solution.py:439
  53.8 2.0 %collective-permute-start.11 = (bf16[2,128,128]{2,1,0:T(8,128)(2,1)S(1)}, bf16[2,128,128]{2,1,0:T(8,128)(2,1)S(1)}, u32[]{:S(2)}, u32[]{:S(2)}) collective-permute-start(bf16[2,128,128]{2,1,0:T(8,128)(2,1)S(1)} %get-tuple-element.42), channel_id=1, source_target_pairs={{0,2},{1,3},{2,0},{3,1},{4,6},{5,7},{6,4},{7,5},{8,10},{9,11},{10,... | collective-permute-start | bytes 196616 | tf_op jit(solution)/shard_map/ppermute | solution.py:327
  55.8 2.2 %collective-permute-start.12 = (bf16[2,128,128]{2,1,0:T(8,128)(2,1)S(1)}, bf16[2,128,128]{2,1,0:T(8,128)(2,1)S(1)}, u32[]{:S(2)}, u32[]{:S(2)}) collective-permute-start(bf16[2,128,128]{2,1,0:T(8,128)(2,1)S(1)} %get-tuple-element.43), channel_id=1, source_target_pairs={{0,4},{1,5},{2,6},{3,7},{4,0},{5,1},{6,2},{7,3},{8,12},{9,13},{10,... | collective-permute-start | bytes 196616 | tf_op jit(solution)/shard_map/ppermute | solution.py:327
  57.9 0.0 collective-permute-start.13
  57.9 3.1 %collective-permute-start.14 = (bf16[2,128,128]{2,1,0:T(8,128)(2,1)S(1)}, bf16[2,128,128]{2,1,0:T(8,128)(2,1)S(1)}, u32[]{:S(2)}, u32[]{:S(2)}) collective-permute-start(bf16[2,128,128]{2,1,0:T(8,128)(2,1)S(1)} %get-tuple-element.45), channel_id=1, source_target_pairs={{0,10},{1,11},{2,8},{3,9},{4,14},{5,15},{6,12},{7,13},{8,2},{9,3},... | collective-permute-start | bytes 196616 | tf_op jit(solution)/shard_map/ppermute | solution.py:327
  61.0 0.7 collective-permute-start.15
  61.8 0.0 collective-permute-done.11.rest_0_.refs_1_
  61.8 3.1 %collective-permute-start.16 = (bf16[2,128,128]{2,1,0:T(8,128)(2,1)S(1)}, bf16[2,128,128]{2,1,0:T(8,128)(2,1)S(1)}, u32[]{:S(2)}, u32[]{:S(2)}) collective-permute-start(bf16[2,128,128]{2,1,0:T(8,128)(2,1)S(1)} %get-tuple-element.47), channel_id=1, source_target_pairs={{0,14},{1,15},{2,12},{3,13},{4,10},{5,11},{6,8},{7,9},{8,6},{9,7},... | collective-permute-start | bytes 196616 | tf_op jit(solution)/shard_map/ppermute | solution.py:327
  64.9 0.0 collective-permute-done.12.rest_1_.refs_2_
  64.9 1.0 %collective-permute-start.17 = (bf16[2,128,128]{2,1,0:T(8,128)(2,1)S(1)}, bf16[2,128,128]{2,1,0:T(8,128)(2,1)S(1)}, u32[]{:S(2)}, u32[]{:S(2)}) collective-permute-start(bf16[2,128,128]{2,1,0:T(8,128)(2,1)S(1)} %get-tuple-element.48), channel_id=1, source_target_pairs={{0,12},{1,13},{2,14},{3,15},{4,8},{5,9},{6,10},{7,11},{8,4},{9,5},... | collective-permute-start | bytes 196616 | tf_op jit(solution)/shard_map/ppermute | solution.py:327
  65.9 0.0 collective-permute-done.13.rest_2_.refs_3_
  65.9 8.3 %collective-permute-done.14.rest_3_.refs_4_ = bf16[2,128,128]{2,1,0:T(8,128)(2,1)S(1)} collective-permute-done((bf16[2,128,128]{2,1,0:T(8,128)(2,1)S(1)}, bf16[2,128,128]{2,1,0:T(8,128)(2,1)S(1)}, u32[]{:S(2)}, u32[]{:S(2)}) %collective-permute-start.14) | collective-permute-done | bytes 65568 | tf_op jit(solution)/shard_map/ppermute | solution.py:327
  74.2 0.5 collective-permute-done.15.rest_4_.refs_5_
  74.7 0.0 collective-permute-done.16.rest_5_.refs_6_
  74.7 0.0 collective-permute-done.17.rest_6_.refs_7_
  74.7 0.4 shard_map.103
  75.1 0.1 collective-permute-start.18
  75.2 0.7 shard_map.102.part
  75.9 0.0 all-to-all-done.1.arrived
  75.9 0.9 %shard_map.104.outer = bf16[1152,128]{1,0:T(8,128)(2,1)S(1)} custom-call(s32[2,1,16]{2,1,0:T(1,128)S(1)} %copy-done.2, f32[9,128,128]{2,1,0:T(8,128)S(1)} %get-tuple-element.50.local, bf16[16,128,128]{2,1,0:T(8,128)(2,1)S(1)} %all-to-all-done.1.arrived), custom_call_target="tpu_custom_call" | custom-call | flops 26214400 | bytes 235929600 | tf_op jit(solution)/shard_map/pallas_call | solution.py:463
  76.8 0.0 collective-permute-done.18.swapped
  76.8 1.6 %shard_map.105 = bf16[2,1152,128]{2,1,0:T(8,128)(2,1)} custom-call(s32[2,1,16]{2,1,0:T(1,128)S(1)} %copy-done.2, f32[9,128,128]{2,1,0:T(8,128)S(1)} %shard_map.102.part, bf16[8,128,128]{2,1,0:T(8,128)(2,1)S(1)} %collective-permute-done.18.swapped, bf16[1152,128]{1,0:T(8,128)(2,1)S(1)} %shard_map.104.outer), custom_call_target="tpu_custom_call" | custom-call | flops 26214400 | bytes 235929600 | tf_op jit(solution)/shard_map/pallas_call | solution.py:478
  (19 shorter events, 0.0 us)
Async XLA Ops:
  0.6 25.9 %copy-start = (bf16[2,1152,128]{2,1,0:T(8,128)(2,1)S(1)}, bf16[2,1152,128]{2,1,0:T(8,128)(2,1)}, u32[]{:S(2)}) copy-start(bf16[2,1152,128]{2,1,0:T(8,128)(2,1)} %feats.7) | copy-start | bytes 1769476
  0.6 16.1 %copy-start.1 = (bf16[3,128,256]{2,1,0:T(8,128)(2,1)S(1)}, bf16[3,128,256]{2,1,0:T(8,128)(2,1)}, u32[]{:S(2)}) copy-start(bf16[3,128,256]{2,1,0:T(8,128)(2,1)} %tw.3) | copy-start | bytes 589828
  0.7 25.8 %copy-start.10 = (s32[2,9,4]{1,2,0:T(4,128)S(1)}, s32[2,9,4]{1,2,0:T(4,128)}, u32[]{:S(2)}) copy-start(s32[2,9,4]{1,2,0:T(4,128)} %param.11) | copy-start | bytes 868
  0.7 25.8 %copy-start.3 = (bf16[2,1152,4,128]{3,2,1,0:T(4,128)(2,1)S(1)}, bf16[2,1152,4,128]{3,2,1,0:T(4,128)(2,1)}, u32[]{:S(2)}) copy-start(bf16[2,1152,4,128]{3,2,1,0:T(4,128)(2,1)} %param.10) | copy-start | bytes 7077892
  0.7 2.9 %collective-permute-start.1 = (bf16[2,1152,128]{2,1,0:T(8,128)(2,1)}, bf16[2,1152,128]{2,1,0:T(8,128)(2,1)}, u32[]{:S(2)}, u32[]{:S(2)}) collective-permute-start(bf16[2,1152,128]{2,1,0:T(8,128)(2,1)} %feats.7), channel_id=1, source_target_pairs={{0,1},{1,0},{2,3},{3,2},{4,5},{5,4},{6,7},{7,6},{8,9},{9,8},{10,11... | collective-permute-start | bytes 1769480 | tf_op jit(solution)/shard_map/ppermute | solution.py:318
  1.2 2.4 %collective-permute-start = (s32[2,1,16]{2,1,0:T(1,128)}, s32[2,1,16]{2,1,0:T(1,128)S(1)}, u32[]{:S(2)}, u32[]{:S(2)}) collective-permute-start(s32[2,1,16]{2,1,0:T(1,128)} %send.5), channel_id=1, source_target_pairs={{0,1},{1,0},{2,3},{3,2},{4,5},{5,4},{6,7},{7,6},{8,9},{9,8},{10,11... | collective-permute-start | bytes 392 | tf_op jit(solution)/shard_map/ppermute | solution.py:318
  3.6 7.4 %copy-start.12 = (s32[2,1,16]{2,1,0:T(1,128)}, s32[2,1,16]{2,1,0:T(1,128)S(1)}, u32[]{:S(2)}) copy-start(s32[2,1,16]{2,1,0:T(1,128)S(1)} %collective-permute-done.partner_lists) | copy-start | bytes 388
  3.6 22.9 %all-to-all-start = ((bf16[16,128,128]{2,1,0:T(8,128)(2,1)}), bf16[16,128,128]{2,1,0:T(8,128)(2,1)}, u32[]{:S(2)}, u32[]{:S(2)}) async-start(bf16[16,128,128]{2,1,0:T(8,128)(2,1)} %shard_map.95), calls=%async_computation | async-start | bytes 1048576 | tf_op jit(solution)/shard_map/all_to_all | solution.py:321
  12.8 0.6 copy-start.7
  13.4 7.9 %collective-permute-start.2 = (bf16[2,128,128]{2,1,0:T(8,128)(2,1)S(1)}, bf16[2,128,128]{2,1,0:T(8,128)(2,1)S(1)}, u32[]{:S(2)}, u32[]{:S(2)}) collective-permute-start(bf16[2,128,128]{2,1,0:T(8,128)(2,1)S(1)} %get-tuple-element.31), channel_id=1, source_target_pairs={{0,2},{1,3},{2,0},{3,1},{4,6},{5,7},{6,4},{7,5},{8,10},{9,11},{10,... | collective-permute-start | bytes 196616 | tf_op jit(solution)/shard_map/ppermute | solution.py:327
  15.3 9.3 %collective-permute-start.3 = (bf16[2,128,128]{2,1,0:T(8,128)(2,1)S(1)}, bf16[2,128,128]{2,1,0:T(8,128)(2,1)S(1)}, u32[]{:S(2)}, u32[]{:S(2)}) collective-permute-start(bf16[2,128,128]{2,1,0:T(8,128)(2,1)S(1)} %get-tuple-element.32), channel_id=1, source_target_pairs={{0,4},{1,5},{2,6},{3,7},{4,0},{5,1},{6,2},{7,3},{8,12},{9,13},{10,... | collective-permute-start | bytes 196616 | tf_op jit(solution)/shard_map/ppermute | solution.py:327
  16.9 12.9 %collective-permute-start.4 = (bf16[2,128,128]{2,1,0:T(8,128)(2,1)}, bf16[2,128,128]{2,1,0:T(8,128)(2,1)}, u32[]{:S(2)}, u32[]{:S(2)}) collective-permute-start(bf16[2,128,128]{2,1,0:T(8,128)(2,1)} %get-tuple-element.33), channel_id=1, source_target_pairs={{0,6},{1,7},{2,4},{3,5},{4,2},{5,3},{6,0},{7,1},{8,14},{9,15},{10,... | collective-permute-start | bytes 196616 | tf_op jit(solution)/shard_map/ppermute | solution.py:327
  17.1 17.6 %collective-permute-start.5 = (bf16[2,128,128]{2,1,0:T(8,128)(2,1)}, bf16[2,128,128]{2,1,0:T(8,128)(2,1)}, u32[]{:S(2)}, u32[]{:S(2)}) collective-permute-start(bf16[2,128,128]{2,1,0:T(8,128)(2,1)} %get-tuple-element.34), channel_id=1, source_target_pairs={{0,10},{1,11},{2,8},{3,9},{4,14},{5,15},{6,12},{7,13},{8,2},{9,3},... | collective-permute-start | bytes 196616 | tf_op jit(solution)/shard_map/ppermute | solution.py:327
  20.8 14.5 %collective-permute-start.6 = (bf16[2,128,128]{2,1,0:T(8,128)(2,1)S(1)}, bf16[2,128,128]{2,1,0:T(8,128)(2,1)}, u32[]{:S(2)}, u32[]{:S(2)}) collective-permute-start(bf16[2,128,128]{2,1,0:T(8,128)(2,1)S(1)} %get-tuple-element.35), channel_id=1, source_target_pairs={{0,8},{1,9},{2,10},{3,11},{4,12},{5,13},{6,14},{7,15},{8,0},{9,1},... | collective-permute-start | bytes 196616 | tf_op jit(solution)/shard_map/ppermute | solution.py:327
  21.4 3.3 %copy-start.13 = (bf16[2,128,128]{2,1,0:T(8,128)(2,1)}, bf16[2,128,128]{2,1,0:T(8,128)(2,1)S(1)}, u32[]{:S(2)}) copy-start(bf16[2,128,128]{2,1,0:T(8,128)(2,1)S(1)} %collective-permute-done.2.rest_1_) | copy-start | bytes 196612
  21.4 13.9 %collective-permute-start.7 = (bf16[2,128,128]{2,1,0:T(8,128)(2,1)S(1)}, bf16[2,128,128]{2,1,0:T(8,128)(2,1)}, u32[]{:S(2)}, u32[]{:S(2)}) collective-permute-start(bf16[2,128,128]{2,1,0:T(8,128)(2,1)S(1)} %get-tuple-element.36), channel_id=1, source_target_pairs={{0,14},{1,15},{2,12},{3,13},{4,10},{5,11},{6,8},{7,9},{8,6},{9,7},... | collective-permute-start | bytes 196616 | tf_op jit(solution)/shard_map/ppermute | solution.py:327
  24.6 0.6 copy-start.14
  25.3 10.0 %collective-permute-start.8 = (bf16[2,128,128]{2,1,0:T(8,128)(2,1)S(1)}, bf16[2,128,128]{2,1,0:T(8,128)(2,1)}, u32[]{:S(2)}, u32[]{:S(2)}) collective-permute-start(bf16[2,128,128]{2,1,0:T(8,128)(2,1)S(1)} %get-tuple-element.37), channel_id=1, source_target_pairs={{0,12},{1,13},{2,14},{3,15},{4,8},{5,9},{6,10},{7,11},{8,4},{9,5},... | collective-permute-start | bytes 196616 | tf_op jit(solution)/shard_map/ppermute | solution.py:327
  26.5 0.8 copy-start.8
  29.8 8.2 %collective-permute-start.9 = (bf16[1152,128]{1,0:T(8,128)(2,1)S(1)}, bf16[1152,128]{1,0:T(8,128)(2,1)S(1)}, u32[]{:S(2)}, u32[]{:S(2)}) collective-permute-start(bf16[1152,128]{1,0:T(8,128)(2,1)S(1)} %shard_map.96.ha), channel_id=1, source_target_pairs={{0,16},{16,0},{1,17},{17,1},{2,18},{18,2},{3,19},{19,3},{4,20},{20... | collective-permute-start | bytes 884744 | tf_op jit(solution)/shard_map/ppermute | solution.py:395
  35.3 2.7 %copy-start.4 = (bf16[2,1152,4,128]{3,2,1,0:T(4,128)(2,1)S(1)}, bf16[2,1152,4,128]{3,2,1,0:T(4,128)(2,1)}, u32[]{:S(2)}) copy-start(bf16[2,1152,4,128]{3,2,1,0:T(4,128)(2,1)} %param.10) | copy-start | bytes 7077892
  35.3 2.7 %copy-start.6 = (bf16[2,1152,128]{2,1,0:T(8,128)(2,1)S(1)}, bf16[2,1152,128]{2,1,0:T(8,128)(2,1)}, u32[]{:S(2)}) copy-start(bf16[2,1152,128]{2,1,0:T(8,128)(2,1)} %cot.1) | copy-start | bytes 1769476
  35.3 2.7 %copy-start.11 = (f32[256]{0:T(256)S(1)}, f32[256]{0:T(256)}, u32[]{:S(2)}) copy-start(f32[256]{0:T(256)} %param.15) | copy-start | bytes 3076
  38.0 12.5 %copy-start.9 = (bf16[128,128]{1,0:T(8,128)(2,1)S(1)}, bf16[128,128]{1,0:T(8,128)(2,1)}, u32[]{:S(2)}) copy-start(bf16[128,128]{1,0:T(8,128)(2,1)} %sw.7) | copy-start | bytes 98308
  41.7 8.8 %collective-permute-start.10 = (bf16[1152,128]{1,0:T(8,128)(2,1)S(1)}, bf16[1152,128]{1,0:T(8,128)(2,1)S(1)}, u32[]{:S(2)}, u32[]{:S(2)}) collective-permute-start(bf16[1152,128]{1,0:T(8,128)(2,1)S(1)} %get-tuple-element.40), channel_id=1, source_target_pairs={{0,16},{16,0},{1,17},{17,1},{2,18},{18,2},{3,19},{19,3},{4,20},{20... | collective-permute-start | bytes 884744 | tf_op jit(solution)/shard_map/ppermute | solution.py:436
  43.2 32.7 %all-to-all-start.1 = ((bf16[16,128,128]{2,1,0:T(8,128)(2,1)}), bf16[16,128,128]{2,1,0:T(8,128)(2,1)S(1)}, u32[]{:S(2)}, u32[]{:S(2)}) async-start(bf16[16,128,128]{2,1,0:T(8,128)(2,1)} %get-tuple-element.51), calls=%async_computation.1 | async-start | bytes 1048576 | tf_op jit(solution)/shard_map/all_to_all | solution.py:321
  50.5 1.7 %copy-start.5 = (bf16[2,1152,4,128]{3,2,1,0:T(4,128)(2,1)S(1)}, bf16[2,1152,4,128]{3,2,1,0:T(4,128)(2,1)}, u32[]{:S(2)}) copy-start(bf16[2,1152,4,128]{3,2,1,0:T(4,128)(2,1)} %param.10) | copy-start | bytes 7077892
  52.2 23.0 %copy-start.2 = (s32[2,1,16]{2,1,0:T(1,128)S(1)}, s32[2,1,16]{2,1,0:T(1,128)}, u32[]{:S(2)}) copy-start(s32[2,1,16]{2,1,0:T(1,128)} %send.5) | copy-start | bytes 388
  53.8 8.0 %collective-permute-start.11 = (bf16[2,128,128]{2,1,0:T(8,128)(2,1)S(1)}, bf16[2,128,128]{2,1,0:T(8,128)(2,1)S(1)}, u32[]{:S(2)}, u32[]{:S(2)}) collective-permute-start(bf16[2,128,128]{2,1,0:T(8,128)(2,1)S(1)} %get-tuple-element.42), channel_id=1, source_target_pairs={{0,2},{1,3},{2,0},{3,1},{4,6},{5,7},{6,4},{7,5},{8,10},{9,11},{10,... | collective-permute-start | bytes 196616 | tf_op jit(solution)/shard_map/ppermute | solution.py:327
  55.8 9.1 %collective-permute-start.12 = (bf16[2,128,128]{2,1,0:T(8,128)(2,1)S(1)}, bf16[2,128,128]{2,1,0:T(8,128)(2,1)S(1)}, u32[]{:S(2)}, u32[]{:S(2)}) collective-permute-start(bf16[2,128,128]{2,1,0:T(8,128)(2,1)S(1)} %get-tuple-element.43), channel_id=1, source_target_pairs={{0,4},{1,5},{2,6},{3,7},{4,0},{5,1},{6,2},{7,3},{8,12},{9,13},{10,... | collective-permute-start | bytes 196616 | tf_op jit(solution)/shard_map/ppermute | solution.py:327
  57.9 7.9 %collective-permute-start.13 = (bf16[2,128,128]{2,1,0:T(8,128)(2,1)S(1)}, bf16[2,128,128]{2,1,0:T(8,128)(2,1)S(1)}, u32[]{:S(2)}, u32[]{:S(2)}) collective-permute-start(bf16[2,128,128]{2,1,0:T(8,128)(2,1)S(1)} %get-tuple-element.44), channel_id=1, source_target_pairs={{0,6},{1,7},{2,4},{3,5},{4,2},{5,3},{6,0},{7,1},{8,14},{9,15},{10,... | collective-permute-start | bytes 196616 | tf_op jit(solution)/shard_map/ppermute | solution.py:327
  57.9 16.2 %collective-permute-start.14 = (bf16[2,128,128]{2,1,0:T(8,128)(2,1)S(1)}, bf16[2,128,128]{2,1,0:T(8,128)(2,1)S(1)}, u32[]{:S(2)}, u32[]{:S(2)}) collective-permute-start(bf16[2,128,128]{2,1,0:T(8,128)(2,1)S(1)} %get-tuple-element.45), channel_id=1, source_target_pairs={{0,10},{1,11},{2,8},{3,9},{4,14},{5,15},{6,12},{7,13},{8,2},{9,3},... | collective-permute-start | bytes 196616 | tf_op jit(solution)/shard_map/ppermute | solution.py:327
  61.0 13.6 %collective-permute-start.15 = (bf16[2,128,128]{2,1,0:T(8,128)(2,1)S(1)}, bf16[2,128,128]{2,1,0:T(8,128)(2,1)S(1)}, u32[]{:S(2)}, u32[]{:S(2)}) collective-permute-start(bf16[2,128,128]{2,1,0:T(8,128)(2,1)S(1)} %get-tuple-element.46), channel_id=1, source_target_pairs={{0,8},{1,9},{2,10},{3,11},{4,12},{5,13},{6,14},{7,15},{8,0},{9,1},... | collective-permute-start | bytes 196616 | tf_op jit(solution)/shard_map/ppermute | solution.py:327
  61.8 12.9 %collective-permute-start.16 = (bf16[2,128,128]{2,1,0:T(8,128)(2,1)S(1)}, bf16[2,128,128]{2,1,0:T(8,128)(2,1)S(1)}, u32[]{:S(2)}, u32[]{:S(2)}) collective-permute-start(bf16[2,128,128]{2,1,0:T(8,128)(2,1)S(1)} %get-tuple-element.47), channel_id=1, source_target_pairs={{0,14},{1,15},{2,12},{3,13},{4,10},{5,11},{6,8},{7,9},{8,6},{9,7},... | collective-permute-start | bytes 196616 | tf_op jit(solution)/shard_map/ppermute | solution.py:327
  64.9 9.8 %collective-permute-start.17 = (bf16[2,128,128]{2,1,0:T(8,128)(2,1)S(1)}, bf16[2,128,128]{2,1,0:T(8,128)(2,1)S(1)}, u32[]{:S(2)}, u32[]{:S(2)}) collective-permute-start(bf16[2,128,128]{2,1,0:T(8,128)(2,1)S(1)} %get-tuple-element.48), channel_id=1, source_target_pairs={{0,12},{1,13},{2,14},{3,15},{4,8},{5,9},{6,10},{7,11},{8,4},{9,5},... | collective-permute-start | bytes 196616 | tf_op jit(solution)/shard_map/ppermute | solution.py:327
  75.1 1.7 %collective-permute-start.18 = (bf16[8,128,128]{2,1,0:T(8,128)(2,1)S(1)}, bf16[8,128,128]{2,1,0:T(8,128)(2,1)S(1)}, u32[]{:S(2)}, u32[]{:S(2)}) collective-permute-start(bf16[8,128,128]{2,1,0:T(8,128)(2,1)S(1)} %shard_map.103), channel_id=1, source_target_pairs={{0,1},{1,0},{2,3},{3,2},{4,5},{5,4},{6,7},{7,6},{8,9},{9,8},{10,11... | collective-permute-start | bytes 786440 | tf_op jit(solution)/shard_map/ppermute | solution.py:318

commit v4 on v3

--- a/solution.py
+++ b/solution.py
@@ -121,10 +121,12 @@
     return which * chips + jnp.bitwise_xor(part // 2, chip)
 
 
-def side_by_side(snap, slots, adj, wide, tiles):
+def side_by_side(snap, slots, adj, wide, tiles, fetches=()):
     blocks_here, block = tiles.shape[:2]
     rows = slots * block
     for j in range(blocks_here):
+        if fetches and j % 3 == 0:
+            fetches[j // 3].wait()
         wide[j % 2] = adj[snap, j * rows : (j + 1) * rows, :].astype(F32)
         for slot in range(slots):
             tile = wide[j % 2, pl.ds(slot, block, stride=slots), :]
@@ -142,11 +144,11 @@
     hidden[...] = dot(agg[...], sw[...]).astype(BF16)
 
 
-def hidden_body(inner, chips, slots, cols, feats, adj, sw, *rest):
-    arrived, rest = rest[:-7], rest[-7:]
-    hidden, own, wide, tiles, halo, agg, sem = rest
+def hidden_body(inner, chips, slots, cols, feats, adj, weight, *rest):
+    arrived, rest = rest[:-8], rest[-8:]
+    hidden, own, sw, wide, tiles, halo, agg, sem = rest
     snap = inner_index() if inner else 1 - inner_index()
-    pairs = [(feats.at[snap], own)]
+    pairs = [(feats.at[snap], own), (weight, sw)]
     if inner:
         pairs.append((arrived[0], halo))
     else:
@@ -232,10 +234,18 @@
 
 def inner_body(chips, blocks_here, slots, cols, rest_a, partial, sw, raw, *rest):
     outs = rest[:chips]
-    local, grad, acc, adj, wide = rest[chips:]
+    local, grad, acc, adj, wide, held, sem = rest[chips:]
     ia = inner_index()
-    side_by_side(ia, slots, raw, wide, adj)
+    rows = held.shape[1] // blocks_here
+    fetches = []
+    for j in range(0, blocks_here, 3):
+        some = pl.ds(j * rows, min(3, blocks_here - j) * rows)
+        fetches.append(
+            pltpu.make_async_copy(raw.at[ia, some], held.at[0, some], sem.at[len(fetches)])
+        )
+        fetches[-1].start()
     grad[...] = (rest_a[...] + partial[...].astype(F32)).astype(BF16)
+    side_by_side(0, slots, held, wide, adj, fetches)
     spread(False, ia, chips, blocks_here, slots, cols, grad, sw, adj, local, acc)
     for offset in range(chips):
         for which in range(2):
@@ -377,19 +387,20 @@
         return call(
             functools.partial(hidden_body, inner, chips, slots),
             shape((items_here, channels)),
-            [SMEM, HBM, VMEM, VMEM] + [HBM] * len(arrived),
+            [SMEM, HBM, VMEM, HBM] + [HBM] * len(arrived),
             VMEM,
             [
                 pltpu.VMEM((items_here, channels), BF16),
+                pltpu.VMEM((channels, channels), BF16),
                 pltpu.VMEM((2, tile_rows, block), F32),
                 pltpu.VMEM((blocks_here, block, tile_rows), BF16),
                 pltpu.VMEM((domains, block, channels), BF16),
                 pltpu.VMEM((items_here, channels), BF16),
-                DMA((domains + 1,)),
+                DMA((domains + 2,)),
             ],
             flops=(slots + 1) * item_flops,
             moved=(slots + 4) * items_here * channels * 2,
-        )(cols, features, adj_flat, spatial_weight, *(in_hbm(v) for v in arrived))
+        )(cols, features, adj_flat, in_hbm(spatial_weight), *(in_hbm(v) for v in arrived))
 
     hidden_a = hidden_of(True, [got_a])
     hidden_n = lax.ppermute(hidden_a, "snap", other_snap)
@@ -439,12 +450,13 @@
     results = call(
         functools.partial(inner_body, chips, blocks_here, slots),
         [two] * chips + [local_shape],
-        [SMEM] + [VMEM] * 4,
+        [SMEM] + [VMEM] * 3 + [HBM],
         [VMEM] * (chips + 1),
-        back_scratch,
+        back_scratch
+        + [pltpu.VMEM((1, items_here * slots, block), BF16), DMA((pl.cdiv(blocks_here, 3),))],
         flops=(slots + 1) * item_flops,
         moved=12 * items_here * channels * 2,
-    )(cols, rest_a, partial_n, spatial_weight, adj_flat)
+    )(cols, rest_a, partial_n, spatial_weight, in_hbm(adj_flat))
     shares_a, local_a = results[:chips], results[chips]
     back_a = to_chips(shares_a, BACKWARD)
     swapped = swap_cores(

time: 79.5 us -> 78.6 us (0.989)
  local copies, waits for them, and re-layouts: 3.71 us -> 1.29 us
  Pallas kernels: 18.2 us -> 19.3 us
  waiting for transfers between devices: 12.7 us -> 13.6 us
    unnamed x30 -> x26, local copies, waits for them, and re-layouts: 3.71 us -> 1.29 us
    pallas_call x1, Pallas kernels: 1.57 us -> 2.66 us  [local_pair(): call(functools.partial(inner_body, chips, blocks_here, slots), [two] * ch...]
    ppermute x14, waiting for transfers between devices: 12.7 us -> 13.5 us  [to_chips(): done[offset] = lax.ppermute(payloads[offset], 'dom', pairs)]
  transfers between devices with their start and end apart: 21 -> 21, of which waited for: 4 -> 5; matrix products, arithmetic and copies ran while one was open for 0% -> 0% of each run, Pallas kernels for 17% -> 18%
where the time goes in v4:
time: 78.6 us; the launch traced here: 77.7 us
  starting transfers between devices  42.5 us (54%)
  Pallas kernels  19.3 us (25%)
  waiting for transfers between devices  13.6 us (17%)
  local copies, waits for them, and re-layouts  1.29 us (2%)
  between operations  0.92 us (1%)
    ppermute x14, starting transfers between devices, to_chips(): done[offset] = lax.ppermute(payloads[offset], 'dom', pairs)  24.8 us
    all_to_all x2, starting transfers between devices, exchange(): lax.all_to_all(values, 'dom', split_axis=0, concat_axis=0, tiled=True)  13.9 us
    ppermute x14, waiting for transfers between devices, to_chips(): done[offset] = lax.ppermute(payloads[offset], 'dom', pairs)  13.5 us
    pallas_call x2, Pallas kernels, hidden_of(): call(functools.partial(hidden_body, inner, chips, slots), shape((items_he...  5.23 us
    pallas_call x1, Pallas kernels, local_pair(): call(functools.partial(temporal_body, chips, blocks_here, slots, TILE), [...  3.63 us
    pallas_call x1, Pallas kernels, local_pair(): call(functools.partial(inner_body, chips, blocks_here, slots), [two] * ch...  2.66 us
    pallas_call x1, Pallas kernels, local_pair(): call(functools.partial(pack_inner_body, domains, block), shape_hbm((domai...  2.29 us
    pallas_call x1, Pallas kernels, local_pair(): call(functools.partial(pack_outer_body, chips, block), [two] * chips, [HB...  1.78 us
  transfers between devices with their start and end apart: 21, of which 5 were waited for; matrix products, arithmetic and copies ran while one was open for 0% of the time, Pallas kernels for 18%

profile of v4, /device:TPU:0, one launch (start us, length us, event | category | flops | bytes accessed | tf_op | source)
XLA Modules:
  0.0 77.7 jit_solution(15152621734029260308)
XLA Ops:
  0.6 0.0 copy-start
  0.7 0.0 copy-start.3
  0.7 0.5 collective-permute-start.1
  1.2 0.1 collective-permute-start
  1.3 2.3 %shard_map.95 = bf16[16,128,128]{2,1,0:T(8,128)(2,1)} custom-call(s32[2,1,16]{2,1,0:T(1,128)} %send.5, bf16[2,1152,128]{2,1,0:T(8,128)(2,1)} %feats.7), custom_call_target="tpu_custom_call" | custom-call | bytes 104857600 | tf_op jit(solution)/shard_map/pallas_call | solution.py:344
  3.6 0.0 collective-permute-done.partner_lists
  3.6 0.0 collective-permute-done.1.partner_feats
  3.6 7.4 %all-to-all-start = ((bf16[16,128,128]{2,1,0:T(8,128)(2,1)}), bf16[16,128,128]{2,1,0:T(8,128)(2,1)}, u32[]{:S(2)}, u32[]{:S(2)}) async-start(bf16[16,128,128]{2,1,0:T(8,128)(2,1)} %shard_map.95), calls=%async_computation | async-start | bytes 1048576 | tf_op jit(solution)/shard_map/all_to_all | solution.py:331
  11.0 0.0 copy-done.10
  11.0 1.8 %shard_map.97 = (bf16[2,128,128]{2,1,0:T(8,128)(2,1)S(1)}, bf16[2,128,128]{2,1,0:T(8,128)(2,1)S(1)}, bf16[2,128,128]{2,1,0:T(8,128)(2,1)S(1)}, bf16[2,128,128]{2...) custom-call(s32[2,1,16]{2,1,0:T(1,128)} %send.5, ...), custom_call_target="tpu_custom_call" | custom-call | bytes 104857600 | tf_op jit(solution)/shard_map/pallas_call | solution.py:360
  12.8 0.6 copy-done.6
  13.4 1.9 %collective-permute-start.2 = (bf16[2,128,128]{2,1,0:T(8,128)(2,1)S(1)}, bf16[2,128,128]{2,1,0:T(8,128)(2,1)S(1)}, u32[]{:S(2)}, u32[]{:S(2)}) collective-permute-start(bf16[2,128,128]{2,1,0:T(8,128)(2,1)S(1)} %get-tuple-element.31), channel_id=1, source_target_pairs={{0,2},{1,3},{2,0},{3,1},{4,6},{5,7},{6,4},{7,5},{8,10},{9,11},{10,... | collective-permute-start | bytes 196616 | tf_op jit(solution)/shard_map/ppermute | solution.py:337
  15.3 1.5 %collective-permute-start.3 = (bf16[2,128,128]{2,1,0:T(8,128)(2,1)S(1)}, bf16[2,128,128]{2,1,0:T(8,128)(2,1)S(1)}, u32[]{:S(2)}, u32[]{:S(2)}) collective-permute-start(bf16[2,128,128]{2,1,0:T(8,128)(2,1)S(1)} %get-tuple-element.32), channel_id=1, source_target_pairs={{0,4},{1,5},{2,6},{3,7},{4,0},{5,1},{6,2},{7,3},{8,12},{9,13},{10,... | collective-permute-start | bytes 196616 | tf_op jit(solution)/shard_map/ppermute | solution.py:337
  16.8 0.1 shard_map.99.twt
  16.9 0.2 collective-permute-start.4
  17.1 3.7 %collective-permute-start.5 = (bf16[2,128,128]{2,1,0:T(8,128)(2,1)}, bf16[2,128,128]{2,1,0:T(8,128)(2,1)}, u32[]{:S(2)}, u32[]{:S(2)}) collective-permute-start(bf16[2,128,128]{2,1,0:T(8,128)(2,1)} %get-tuple-element.34), channel_id=1, source_target_pairs={{0,10},{1,11},{2,8},{3,9},{4,14},{5,15},{6,12},{7,13},{8,2},{9,3},... | collective-permute-start | bytes 196616 | tf_op jit(solution)/shard_map/ppermute | solution.py:337
  20.8 0.6 collective-permute-start.6
  21.4 0.0 collective-permute-done.2.rest_1_
  21.4 3.3 %collective-permute-start.7 = (bf16[2,128,128]{2,1,0:T(8,128)(2,1)S(1)}, bf16[2,128,128]{2,1,0:T(8,128)(2,1)}, u32[]{:S(2)}, u32[]{:S(2)}) collective-permute-start(bf16[2,128,128]{2,1,0:T(8,128)(2,1)S(1)} %get-tuple-element.36), channel_id=1, source_target_pairs={{0,14},{1,15},{2,12},{3,13},{4,10},{5,11},{6,8},{7,9},{8,6},{9,7},... | collective-permute-start | bytes 196616 | tf_op jit(solution)/shard_map/ppermute | solution.py:337
  24.6 0.0 collective-permute-done.3.rest_2_
  24.7 0.6 copy-done.12
  25.3 1.2 %collective-permute-start.8 = (bf16[2,128,128]{2,1,0:T(8,128)(2,1)S(1)}, bf16[2,128,128]{2,1,0:T(8,128)(2,1)}, u32[]{:S(2)}, u32[]{:S(2)}) collective-permute-start(bf16[2,128,128]{2,1,0:T(8,128)(2,1)S(1)} %get-tuple-element.37), channel_id=1, source_target_pairs={{0,12},{1,13},{2,14},{3,15},{4,8},{5,9},{6,10},{7,11},{8,4},{9,5},... | collective-permute-start | bytes 196616 | tf_op jit(solution)/shard_map/ppermute | solution.py:337
  26.5 0.0 all-to-all-done.rest_0_
  26.5 0.0 copy-done.3
  26.5 2.5 %shard_map.96.ha = bf16[1152,128]{1,0:T(8,128)(2,1)S(1)} custom-call(s32[2,4,9]{2,1,0:T(4,128)S(1)} %bitcast.7, bf16[2,1152,128]{2,1,0:T(8,128)(2,1)S(1)} %copy-done, bf16[2,4608,128]{2,1,0:T(8,128)(2,1)S(1)} %bitcast.4, bf16[128,128]{1,0:T(8,128)(2,1)} %sw.3, bf16[16,128,128]{2,1,0:T(8,128)(2,1)} %all-to-all-done.rest_0_), custom_call_target="tpu_custom_call" | custom-call | flops 18874368000 | bytes 235929600 | tf_op jit(solution)/shard_map/pallas_call | solution.py:387
  29.1 0.0 collective-permute-done.4.rest_3_
  29.1 1.6 %collective-permute-start.9 = (bf16[1152,128]{1,0:T(8,128)(2,1)S(1)}, bf16[1152,128]{1,0:T(8,128)(2,1)S(1)}, u32[]{:S(2)}, u32[]{:S(2)}) collective-permute-start(bf16[1152,128]{1,0:T(8,128)(2,1)S(1)} %shard_map.96.ha), channel_id=1, source_target_pairs={{0,16},{16,0},{1,17},{17,1},{2,18},{18,2},{3,19},{19,3},{4,20},{20... | collective-permute-start | bytes 884744 | tf_op jit(solution)/shard_map/ppermute | solution.py:406
  30.6 4.1 %collective-permute-done.5.rest_4_ = bf16[2,128,128]{2,1,0:T(8,128)(2,1)} collective-permute-done((bf16[2,128,128]{2,1,0:T(8,128)(2,1)}, bf16[2,128,128]{2,1,0:T(8,128)(2,1)}, u32[]{:S(2)}, u32[]{:S(2)}) %collective-permute-start.5) | collective-permute-done | bytes 65568 | tf_op jit(solution)/shard_map/ppermute | solution.py:337
  34.8 0.5 collective-permute-done.6.rest_5_
  35.3 0.0 collective-permute-done.7.rest_6_
  35.3 0.0 collective-permute-done.8.rest_7_
  35.3 0.0 copy-start.5
  35.3 0.0 copy-start.7
  35.3 0.0 copy-start.9
  35.3 2.7 %shard_map.98.hb = bf16[1152,128]{1,0:T(8,128)(2,1)S(1)} custom-call(s32[2,4,9]{2,1,0:T(4,128)S(1)} %bitcast.8, bf16[2,1152,128]{2,1,0:T(8,128)(2,1)S(1)} %copy-done, bf16[2,4608,128]{2,1,0:T(8,128)(2,1)S(1)} %bitcast.5, bf16[128,128]{1,0:T(8,128)(2,1)} %sw.3, bf16[2,128,128]{2,1,0:T(8,128)(2,1)} %copy-done.6, bf16[2,128,128]{2,1,0:T(8,128)(2,1)} %copy-done.11, ...), custom_call_target="tpu_custom_call" | custom-call | flops 18874368000 | bytes 235929600 | tf_op jit(solution)/shard_map/pallas_call | solution.py:387
  38.0 0.0 collective-permute-done.9.hn
  38.0 0.0 copy-done.4
  38.0 0.0 copy-done.5
  38.1 3.6 %shard_map.100 = (bf16[16,128,128]{2,1,0:T(8,128)(2,1)}, bf16[2,1152,128]{2,1,0:T(8,128)(2,1)}, bf16[1152,128]{1,0:T(8,128)(2,1)S(1)}, f32[1152,128]{1,0:T(8,128)S(1)}, f32[9,128,128]{2,1,0:T(8,128)S(1)}) custom-call(s32[2,4,9]{2,1,0:T(4,128)S(1)} %bitcast.9, bf16[1152,128]{1,0:T(8,128)(2,1)S(1)} %shard_map.96.ha, bf16[1152,128]{1,0:T(8,128)(2,1)S(1)} %shard_map.98.hb, ...), custom_call_target="tpu_custom_call" | custom-call | flops 98146713600 | bytes 589824000 | tf_op jit(solution)/shard_map/pallas_call | solution.py:416
  41.7 1.6 %collective-permute-start.10 = (bf16[1152,128]{1,0:T(8,128)(2,1)S(1)}, bf16[1152,128]{1,0:T(8,128)(2,1)S(1)}, u32[]{:S(2)}, u32[]{:S(2)}) collective-permute-start(bf16[1152,128]{1,0:T(8,128)(2,1)S(1)} %get-tuple-element.40), channel_id=1, source_target_pairs={{0,16},{16,0},{1,17},{17,1},{2,18},{18,2},{3,19},{19,3},{4,20},{20... | collective-permute-start | bytes 884744 | tf_op jit(solution)/shard_map/ppermute | solution.py:447
  43.3 6.5 %all-to-all-start.1 = ((bf16[16,128,128]{2,1,0:T(8,128)(2,1)}), bf16[16,128,128]{2,1,0:T(8,128)(2,1)S(1)}, u32[]{:S(2)}, u32[]{:S(2)}) async-start(bf16[16,128,128]{2,1,0:T(8,128)(2,1)} %get-tuple-element.51), calls=%async_computation.1 | async-start | bytes 1048576 | tf_op jit(solution)/shard_map/all_to_all | solution.py:331
  49.8 0.1 collective-permute-done.10.partial
  49.8 2.7 %shard_map.101 = (bf16[2,128,128]{2,1,0:T(8,128)(2,1)S(1)}, bf16[2,128,128]{2,1,0:T(8,128)(2,1)S(1)}, bf16[2,128,128]{2,1,0:T(8,128)(2,1)S(1)}, bf16[2,128,128]{...) custom-call(s32[2,4,9]{2,1,0:T(4,128)S(1)} %bitcast.10, ...), custom_call_target="tpu_custom_call" | custom-call | flops 18874368000 | bytes 353894400 | tf_op jit(solution)/shard_map/pallas_call | solution.py:450
  52.5 1.9 %collective-permute-start.11 = (bf16[2,128,128]{2,1,0:T(8,128)(2,1)S(1)}, bf16[2,128,128]{2,1,0:T(8,128)(2,1)S(1)}, u32[]{:S(2)}, u32[]{:S(2)}) collective-permute-start(bf16[2,128,128]{2,1,0:T(8,128)(2,1)S(1)} %get-tuple-element.42), channel_id=1, source_target_pairs={{0,2},{1,3},{2,0},{3,1},{4,6},{5,7},{6,4},{7,5},{8,10},{9,11},{10,... | collective-permute-start | bytes 196616 | tf_op jit(solution)/shard_map/ppermute | solution.py:337
  54.4 3.0 %collective-permute-start.12 = (bf16[2,128,128]{2,1,0:T(8,128)(2,1)S(1)}, bf16[2,128,128]{2,1,0:T(8,128)(2,1)S(1)}, u32[]{:S(2)}, u32[]{:S(2)}) collective-permute-start(bf16[2,128,128]{2,1,0:T(8,128)(2,1)S(1)} %get-tuple-element.43), channel_id=1, source_target_pairs={{0,4},{1,5},{2,6},{3,7},{4,0},{5,1},{6,2},{7,3},{8,12},{9,13},{10,... | collective-permute-start | bytes 196616 | tf_op jit(solution)/shard_map/ppermute | solution.py:337
  57.4 0.0 collective-permute-start.13
  57.4 3.0 %collective-permute-start.14 = (bf16[2,128,128]{2,1,0:T(8,128)(2,1)S(1)}, bf16[2,128,128]{2,1,0:T(8,128)(2,1)S(1)}, u32[]{:S(2)}, u32[]{:S(2)}) collective-permute-start(bf16[2,128,128]{2,1,0:T(8,128)(2,1)S(1)} %get-tuple-element.45), channel_id=1, source_target_pairs={{0,10},{1,11},{2,8},{3,9},{4,14},{5,15},{6,12},{7,13},{8,2},{9,3},... | collective-permute-start | bytes 196616 | tf_op jit(solution)/shard_map/ppermute | solution.py:337
  60.4 0.8 %collective-permute-start.15 = (bf16[2,128,128]{2,1,0:T(8,128)(2,1)S(1)}, bf16[2,128,128]{2,1,0:T(8,128)(2,1)S(1)}, u32[]{:S(2)}, u32[]{:S(2)}) collective-permute-start(bf16[2,128,128]{2,1,0:T(8,128)(2,1)S(1)} %get-tuple-element.46), channel_id=1, source_target_pairs={{0,8},{1,9},{2,10},{3,11},{4,12},{5,13},{6,14},{7,15},{8,0},{9,1},... | collective-permute-start | bytes 196616 | tf_op jit(solution)/shard_map/ppermute | solution.py:337
  61.2 0.0 collective-permute-done.11.rest_0_.refs_1_
  61.2 2.3 %collective-permute-start.16 = (bf16[2,128,128]{2,1,0:T(8,128)(2,1)S(1)}, bf16[2,128,128]{2,1,0:T(8,128)(2,1)S(1)}, u32[]{:S(2)}, u32[]{:S(2)}) collective-permute-start(bf16[2,128,128]{2,1,0:T(8,128)(2,1)S(1)} %get-tuple-element.47), channel_id=1, source_target_pairs={{0,14},{1,15},{2,12},{3,13},{4,10},{5,11},{6,8},{7,9},{8,6},{9,7},... | collective-permute-start | bytes 196616 | tf_op jit(solution)/shard_map/ppermute | solution.py:337
  63.6 0.0 collective-permute-done.12.rest_1_.refs_2_
  63.6 1.5 %collective-permute-start.17 = (bf16[2,128,128]{2,1,0:T(8,128)(2,1)S(1)}, bf16[2,128,128]{2,1,0:T(8,128)(2,1)S(1)}, u32[]{:S(2)}, u32[]{:S(2)}) collective-permute-start(bf16[2,128,128]{2,1,0:T(8,128)(2,1)S(1)} %get-tuple-element.48), channel_id=1, source_target_pairs={{0,12},{1,13},{2,14},{3,15},{4,8},{5,9},{6,10},{7,11},{8,4},{9,5},... | collective-permute-start | bytes 196616 | tf_op jit(solution)/shard_map/ppermute | solution.py:337
  65.1 0.0 collective-permute-done.13.rest_2_.refs_3_
  65.1 8.4 %collective-permute-done.14.rest_3_.refs_4_ = bf16[2,128,128]{2,1,0:T(8,128)(2,1)S(1)} collective-permute-done((bf16[2,128,128]{2,1,0:T(8,128)(2,1)S(1)}, bf16[2,128,128]{2,1,0:T(8,128)(2,1)S(1)}, u32[]{:S(2)}, u32[]{:S(2)}) %collective-permute-start.14) | collective-permute-done | bytes 65568 | tf_op jit(solution)/shard_map/ppermute | solution.py:337
  73.4 0.5 collective-permute-done.15.rest_4_.refs_5_
  73.9 0.0 collective-permute-done.16.rest_5_.refs_6_
  73.9 0.0 collective-permute-done.17.rest_6_.refs_7_
  74.0 0.4 shard_map.103
  74.4 0.1 collective-permute-start.18
  74.5 0.7 shard_map.102.part
  75.2 0.0 all-to-all-done.1.arrived
  75.2 0.9 %shard_map.104.outer = bf16[1152,128]{1,0:T(8,128)(2,1)S(1)} custom-call(s32[2,1,16]{2,1,0:T(1,128)S(1)} %copy-done.2, f32[9,128,128]{2,1,0:T(8,128)S(1)} %get-tuple-element.50.local, bf16[16,128,128]{2,1,0:T(8,128)(2,1)S(1)} %all-to-all-done.1.arrived), custom_call_target="tpu_custom_call" | custom-call | flops 26214400 | bytes 235929600 | tf_op jit(solution)/shard_map/pallas_call | solution.py:475
  76.1 0.0 collective-permute-done.18.swapped
  76.1 1.6 %shard_map.105 = bf16[2,1152,128]{2,1,0:T(8,128)(2,1)} custom-call(s32[2,1,16]{2,1,0:T(1,128)S(1)} %copy-done.2, f32[9,128,128]{2,1,0:T(8,128)S(1)} %shard_map.102.part, bf16[8,128,128]{2,1,0:T(8,128)(2,1)S(1)} %collective-permute-done.18.swapped, bf16[1152,128]{1,0:T(8,128)(2,1)S(1)} %shard_map.104.outer), custom_call_target="tpu_custom_call" | custom-call | flops 26214400 | bytes 235929600 | tf_op jit(solution)/shard_map/pallas_call | solution.py:490
  (15 shorter events, 0.0 us)
Async XLA Ops:
  0.6 25.9 %copy-start = (bf16[2,1152,128]{2,1,0:T(8,128)(2,1)S(1)}, bf16[2,1152,128]{2,1,0:T(8,128)(2,1)}, u32[]{:S(2)}) copy-start(bf16[2,1152,128]{2,1,0:T(8,128)(2,1)} %feats.7) | copy-start | bytes 1769476
  0.6 16.1 %copy-start.1 = (bf16[3,128,256]{2,1,0:T(8,128)(2,1)S(1)}, bf16[3,128,256]{2,1,0:T(8,128)(2,1)}, u32[]{:S(2)}) copy-start(bf16[3,128,256]{2,1,0:T(8,128)(2,1)} %tw.3) | copy-start | bytes 589828
  0.7 25.8 %copy-start.8 = (s32[2,9,4]{1,2,0:T(4,128)S(1)}, s32[2,9,4]{1,2,0:T(4,128)}, u32[]{:S(2)}) copy-start(s32[2,9,4]{1,2,0:T(4,128)} %param.11) | copy-start | bytes 868
  0.7 25.8 %copy-start.3 = (bf16[2,1152,4,128]{3,2,1,0:T(4,128)(2,1)S(1)}, bf16[2,1152,4,128]{3,2,1,0:T(4,128)(2,1)}, u32[]{:S(2)}) copy-start(bf16[2,1152,4,128]{3,2,1,0:T(4,128)(2,1)} %param.10) | copy-start | bytes 7077892
  0.7 2.9 %collective-permute-start.1 = (bf16[2,1152,128]{2,1,0:T(8,128)(2,1)}, bf16[2,1152,128]{2,1,0:T(8,128)(2,1)}, u32[]{:S(2)}, u32[]{:S(2)}) collective-permute-start(bf16[2,1152,128]{2,1,0:T(8,128)(2,1)} %feats.7), channel_id=1, source_target_pairs={{0,1},{1,0},{2,3},{3,2},{4,5},{5,4},{6,7},{7,6},{8,9},{9,8},{10,11... | collective-permute-start | bytes 1769480 | tf_op jit(solution)/shard_map/ppermute | solution.py:328
  1.2 2.4 %collective-permute-start = (s32[2,1,16]{2,1,0:T(1,128)}, s32[2,1,16]{2,1,0:T(1,128)S(1)}, u32[]{:S(2)}, u32[]{:S(2)}) collective-permute-start(s32[2,1,16]{2,1,0:T(1,128)} %send.5), channel_id=1, source_target_pairs={{0,1},{1,0},{2,3},{3,2},{4,5},{5,4},{6,7},{7,6},{8,9},{9,8},{10,11... | collective-permute-start | bytes 392 | tf_op jit(solution)/shard_map/ppermute | solution.py:328
  3.6 7.4 %copy-start.10 = (s32[2,1,16]{2,1,0:T(1,128)}, s32[2,1,16]{2,1,0:T(1,128)S(1)}, u32[]{:S(2)}) copy-start(s32[2,1,16]{2,1,0:T(1,128)S(1)} %collective-permute-done.partner_lists) | copy-start | bytes 388
  3.6 22.9 %all-to-all-start = ((bf16[16,128,128]{2,1,0:T(8,128)(2,1)}), bf16[16,128,128]{2,1,0:T(8,128)(2,1)}, u32[]{:S(2)}, u32[]{:S(2)}) async-start(bf16[16,128,128]{2,1,0:T(8,128)(2,1)} %shard_map.95), calls=%async_computation | async-start | bytes 1048576 | tf_op jit(solution)/shard_map/all_to_all | solution.py:331
  12.8 0.6 copy-start.6
  13.4 7.9 %collective-permute-start.2 = (bf16[2,128,128]{2,1,0:T(8,128)(2,1)S(1)}, bf16[2,128,128]{2,1,0:T(8,128)(2,1)S(1)}, u32[]{:S(2)}, u32[]{:S(2)}) collective-permute-start(bf16[2,128,128]{2,1,0:T(8,128)(2,1)S(1)} %get-tuple-element.31), channel_id=1, source_target_pairs={{0,2},{1,3},{2,0},{3,1},{4,6},{5,7},{6,4},{7,5},{8,10},{9,11},{10,... | collective-permute-start | bytes 196616 | tf_op jit(solution)/shard_map/ppermute | solution.py:337
  15.3 9.3 %collective-permute-start.3 = (bf16[2,128,128]{2,1,0:T(8,128)(2,1)S(1)}, bf16[2,128,128]{2,1,0:T(8,128)(2,1)S(1)}, u32[]{:S(2)}, u32[]{:S(2)}) collective-permute-start(bf16[2,128,128]{2,1,0:T(8,128)(2,1)S(1)} %get-tuple-element.32), channel_id=1, source_target_pairs={{0,4},{1,5},{2,6},{3,7},{4,0},{5,1},{6,2},{7,3},{8,12},{9,13},{10,... | collective-permute-start | bytes 196616 | tf_op jit(solution)/shard_map/ppermute | solution.py:337
  16.9 12.1 %collective-permute-start.4 = (bf16[2,128,128]{2,1,0:T(8,128)(2,1)}, bf16[2,128,128]{2,1,0:T(8,128)(2,1)}, u32[]{:S(2)}, u32[]{:S(2)}) collective-permute-start(bf16[2,128,128]{2,1,0:T(8,128)(2,1)} %get-tuple-element.33), channel_id=1, source_target_pairs={{0,6},{1,7},{2,4},{3,5},{4,2},{5,3},{6,0},{7,1},{8,14},{9,15},{10,... | collective-permute-start | bytes 196616 | tf_op jit(solution)/shard_map/ppermute | solution.py:337
  17.1 17.6 %collective-permute-start.5 = (bf16[2,128,128]{2,1,0:T(8,128)(2,1)}, bf16[2,128,128]{2,1,0:T(8,128)(2,1)}, u32[]{:S(2)}, u32[]{:S(2)}) collective-permute-start(bf16[2,128,128]{2,1,0:T(8,128)(2,1)} %get-tuple-element.34), channel_id=1, source_target_pairs={{0,10},{1,11},{2,8},{3,9},{4,14},{5,15},{6,12},{7,13},{8,2},{9,3},... | collective-permute-start | bytes 196616 | tf_op jit(solution)/shard_map/ppermute | solution.py:337
  20.8 14.4 %collective-permute-start.6 = (bf16[2,128,128]{2,1,0:T(8,128)(2,1)S(1)}, bf16[2,128,128]{2,1,0:T(8,128)(2,1)}, u32[]{:S(2)}, u32[]{:S(2)}) collective-permute-start(bf16[2,128,128]{2,1,0:T(8,128)(2,1)S(1)} %get-tuple-element.35), channel_id=1, source_target_pairs={{0,8},{1,9},{2,10},{3,11},{4,12},{5,13},{6,14},{7,15},{8,0},{9,1},... | collective-permute-start | bytes 196616 | tf_op jit(solution)/shard_map/ppermute | solution.py:337
  21.4 3.3 %copy-start.11 = (bf16[2,128,128]{2,1,0:T(8,128)(2,1)}, bf16[2,128,128]{2,1,0:T(8,128)(2,1)S(1)}, u32[]{:S(2)}) copy-start(bf16[2,128,128]{2,1,0:T(8,128)(2,1)S(1)} %collective-permute-done.2.rest_1_) | copy-start | bytes 196612
  21.4 13.9 %collective-permute-start.7 = (bf16[2,128,128]{2,1,0:T(8,128)(2,1)S(1)}, bf16[2,128,128]{2,1,0:T(8,128)(2,1)}, u32[]{:S(2)}, u32[]{:S(2)}) collective-permute-start(bf16[2,128,128]{2,1,0:T(8,128)(2,1)S(1)} %get-tuple-element.36), channel_id=1, source_target_pairs={{0,14},{1,15},{2,12},{3,13},{4,10},{5,11},{6,8},{7,9},{8,6},{9,7},... | collective-permute-start | bytes 196616 | tf_op jit(solution)/shard_map/ppermute | solution.py:337
  24.7 0.6 copy-start.12
  25.3 10.0 %collective-permute-start.8 = (bf16[2,128,128]{2,1,0:T(8,128)(2,1)S(1)}, bf16[2,128,128]{2,1,0:T(8,128)(2,1)}, u32[]{:S(2)}, u32[]{:S(2)}) collective-permute-start(bf16[2,128,128]{2,1,0:T(8,128)(2,1)S(1)} %get-tuple-element.37), channel_id=1, source_target_pairs={{0,12},{1,13},{2,14},{3,15},{4,8},{5,9},{6,10},{7,11},{8,4},{9,5},... | collective-permute-start | bytes 196616 | tf_op jit(solution)/shard_map/ppermute | solution.py:337
  29.1 8.9 %collective-permute-start.9 = (bf16[1152,128]{1,0:T(8,128)(2,1)S(1)}, bf16[1152,128]{1,0:T(8,128)(2,1)S(1)}, u32[]{:S(2)}, u32[]{:S(2)}) collective-permute-start(bf16[1152,128]{1,0:T(8,128)(2,1)S(1)} %shard_map.96.ha), channel_id=1, source_target_pairs={{0,16},{16,0},{1,17},{17,1},{2,18},{18,2},{3,19},{19,3},{4,20},{20... | collective-permute-start | bytes 884744 | tf_op jit(solution)/shard_map/ppermute | solution.py:406
  35.3 2.7 %copy-start.4 = (bf16[2,1152,4,128]{3,2,1,0:T(4,128)(2,1)S(1)}, bf16[2,1152,4,128]{3,2,1,0:T(4,128)(2,1)}, u32[]{:S(2)}) copy-start(bf16[2,1152,4,128]{3,2,1,0:T(4,128)(2,1)} %param.10) | copy-start | bytes 7077892
  35.3 2.8 %copy-start.5 = (bf16[2,1152,128]{2,1,0:T(8,128)(2,1)S(1)}, bf16[2,1152,128]{2,1,0:T(8,128)(2,1)}, u32[]{:S(2)}) copy-start(bf16[2,1152,128]{2,1,0:T(8,128)(2,1)} %cot.1) | copy-start | bytes 1769476
  35.3 2.8 %copy-start.7 = (bf16[128,128]{1,0:T(8,128)(2,1)S(1)}, bf16[128,128]{1,0:T(8,128)(2,1)}, u32[]{:S(2)}) copy-start(bf16[128,128]{1,0:T(8,128)(2,1)} %sw.3) | copy-start | bytes 98308
  35.3 2.8 %copy-start.9 = (f32[256]{0:T(256)S(1)}, f32[256]{0:T(256)}, u32[]{:S(2)}) copy-start(f32[256]{0:T(256)} %param.15) | copy-start | bytes 3076
  41.7 8.1 %collective-permute-start.10 = (bf16[1152,128]{1,0:T(8,128)(2,1)S(1)}, bf16[1152,128]{1,0:T(8,128)(2,1)S(1)}, u32[]{:S(2)}, u32[]{:S(2)}) collective-permute-start(bf16[1152,128]{1,0:T(8,128)(2,1)S(1)} %get-tuple-element.40), channel_id=1, source_target_pairs={{0,16},{16,0},{1,17},{17,1},{2,18},{18,2},{3,19},{19,3},{4,20},{20... | collective-permute-start | bytes 884744 | tf_op jit(solution)/shard_map/ppermute | solution.py:447
  43.3 31.9 %all-to-all-start.1 = ((bf16[16,128,128]{2,1,0:T(8,128)(2,1)}), bf16[16,128,128]{2,1,0:T(8,128)(2,1)S(1)}, u32[]{:S(2)}, u32[]{:S(2)}) async-start(bf16[16,128,128]{2,1,0:T(8,128)(2,1)} %get-tuple-element.51), calls=%async_computation.1 | async-start | bytes 1048576 | tf_op jit(solution)/shard_map/all_to_all | solution.py:331
  49.8 24.6 %copy-start.2 = (s32[2,1,16]{2,1,0:T(1,128)S(1)}, s32[2,1,16]{2,1,0:T(1,128)}, u32[]{:S(2)}) copy-start(s32[2,1,16]{2,1,0:T(1,128)} %send.5) | copy-start | bytes 388
  52.5 8.7 %collective-permute-start.11 = (bf16[2,128,128]{2,1,0:T(8,128)(2,1)S(1)}, bf16[2,128,128]{2,1,0:T(8,128)(2,1)S(1)}, u32[]{:S(2)}, u32[]{:S(2)}) collective-permute-start(bf16[2,128,128]{2,1,0:T(8,128)(2,1)S(1)} %get-tuple-element.42), channel_id=1, source_target_pairs={{0,2},{1,3},{2,0},{3,1},{4,6},{5,7},{6,4},{7,5},{8,10},{9,11},{10,... | collective-permute-start | bytes 196616 | tf_op jit(solution)/shard_map/ppermute | solution.py:337
  54.4 9.1 %collective-permute-start.12 = (bf16[2,128,128]{2,1,0:T(8,128)(2,1)S(1)}, bf16[2,128,128]{2,1,0:T(8,128)(2,1)S(1)}, u32[]{:S(2)}, u32[]{:S(2)}) collective-permute-start(bf16[2,128,128]{2,1,0:T(8,128)(2,1)S(1)} %get-tuple-element.43), channel_id=1, source_target_pairs={{0,4},{1,5},{2,6},{3,7},{4,0},{5,1},{6,2},{7,3},{8,12},{9,13},{10,... | collective-permute-start | bytes 196616 | tf_op jit(solution)/shard_map/ppermute | solution.py:337
  57.4 7.7 %collective-permute-start.13 = (bf16[2,128,128]{2,1,0:T(8,128)(2,1)S(1)}, bf16[2,128,128]{2,1,0:T(8,128)(2,1)S(1)}, u32[]{:S(2)}, u32[]{:S(2)}) collective-permute-start(bf16[2,128,128]{2,1,0:T(8,128)(2,1)S(1)} %get-tuple-element.44), channel_id=1, source_target_pairs={{0,6},{1,7},{2,4},{3,5},{4,2},{5,3},{6,0},{7,1},{8,14},{9,15},{10,... | collective-permute-start | bytes 196616 | tf_op jit(solution)/shard_map/ppermute | solution.py:337
  57.4 16.0 %collective-permute-start.14 = (bf16[2,128,128]{2,1,0:T(8,128)(2,1)S(1)}, bf16[2,128,128]{2,1,0:T(8,128)(2,1)S(1)}, u32[]{:S(2)}, u32[]{:S(2)}) collective-permute-start(bf16[2,128,128]{2,1,0:T(8,128)(2,1)S(1)} %get-tuple-element.45), channel_id=1, source_target_pairs={{0,10},{1,11},{2,8},{3,9},{4,14},{5,15},{6,12},{7,13},{8,2},{9,3},... | collective-permute-start | bytes 196616 | tf_op jit(solution)/shard_map/ppermute | solution.py:337
  60.4 13.5 %collective-permute-start.15 = (bf16[2,128,128]{2,1,0:T(8,128)(2,1)S(1)}, bf16[2,128,128]{2,1,0:T(8,128)(2,1)S(1)}, u32[]{:S(2)}, u32[]{:S(2)}) collective-permute-start(bf16[2,128,128]{2,1,0:T(8,128)(2,1)S(1)} %get-tuple-element.46), channel_id=1, source_target_pairs={{0,8},{1,9},{2,10},{3,11},{4,12},{5,13},{6,14},{7,15},{8,0},{9,1},... | collective-permute-start | bytes 196616 | tf_op jit(solution)/shard_map/ppermute | solution.py:337
  61.2 12.7 %collective-permute-start.16 = (bf16[2,128,128]{2,1,0:T(8,128)(2,1)S(1)}, bf16[2,128,128]{2,1,0:T(8,128)(2,1)S(1)}, u32[]{:S(2)}, u32[]{:S(2)}) collective-permute-start(bf16[2,128,128]{2,1,0:T(8,128)(2,1)S(1)} %get-tuple-element.47), channel_id=1, source_target_pairs={{0,14},{1,15},{2,12},{3,13},{4,10},{5,11},{6,8},{7,9},{8,6},{9,7},... | collective-permute-start | bytes 196616 | tf_op jit(solution)/shard_map/ppermute | solution.py:337
  63.6 10.4 %collective-permute-start.17 = (bf16[2,128,128]{2,1,0:T(8,128)(2,1)S(1)}, bf16[2,128,128]{2,1,0:T(8,128)(2,1)S(1)}, u32[]{:S(2)}, u32[]{:S(2)}) collective-permute-start(bf16[2,128,128]{2,1,0:T(8,128)(2,1)S(1)} %get-tuple-element.48), channel_id=1, source_target_pairs={{0,12},{1,13},{2,14},{3,15},{4,8},{5,9},{6,10},{7,11},{8,4},{9,5},... | collective-permute-start | bytes 196616 | tf_op jit(solution)/shard_map/ppermute | solution.py:337
  74.4 1.7 %collective-permute-start.18 = (bf16[8,128,128]{2,1,0:T(8,128)(2,1)S(1)}, bf16[8,128,128]{2,1,0:T(8,128)(2,1)S(1)}, u32[]{:S(2)}, u32[]{:S(2)}) collective-permute-start(bf16[8,128,128]{2,1,0:T(8,128)(2,1)S(1)} %shard_map.103), channel_id=1, source_target_pairs={{0,1},{1,0},{2,3},{3,2},{4,5},{5,4},{6,7},{7,6},{8,9},{9,8},{10,11... | collective-permute-start | bytes 786440 | tf_op jit(solution)/shard_map/ppermute | solution.py:328

commit v5 on v4

--- a/solution.py
+++ b/solution.py
@@ -15,7 +15,7 @@
 TILE = 384
 VMEM_LIMIT = 16 * 1024 * 1024
 DMA = pltpu.SemaphoreType.DMA
-FORWARD = (1, 2, 3, 5, 4, 7, 6)
+FORWARD = (1, 3, 2, 5, 4, 7, 6)
 BACKWARD = (1, 2, 3, 5, 4, 7, 6)
 COST = 100
 
@@ -96,10 +96,10 @@
         ],
         sem,
     )
-    for offset in range(chips):
+    for offset in range(1, chips):
         target = 2 * jnp.bitwise_xor(chip, offset) + core
-        outs[offset][0] = wanted(send, held, ib, target, block)[...]
-        outs[offset][1] = wanted(partner_send, partner_held, ib, target, block)[...]
+        outs[offset - 1][0] = wanted(send, held, ib, target, block)[...]
+        outs[offset - 1][1] = wanted(partner_send, partner_held, ib, target, block)[...]
 
 
 def collect_body(picks, *refs):
@@ -152,7 +152,11 @@
     if inner:
         pairs.append((arrived[0], halo))
     else:
-        for offset, source in zip((0,) + FORWARD, arrived):
+        lists, partner_feats, arrived = arrived[0], arrived[1], arrived[2:]
+        me = lax.axis_index("dom")
+        block = halo.shape[1]
+        pairs.append((wanted(lists, partner_feats.at[snap], snap, me, block), halo.at[chips]))
+        for offset, source in zip(FORWARD, arrived):
             for which in range(2):
                 pairs.append((source.at[which], halo.at[which * chips + offset]))
     copies = [
@@ -204,7 +208,7 @@
         grads = []
         for index, mix in ((ia, mix_a), (ib, mix_b)):
             linear = mix[:, :channels]
-            gate = jax.nn.sigmoid(mix[:, channels:])
+            gate = 0.5 * jnp.tanh(0.5 * mix[:, channels:]) + 0.5
             up = cot[index, rows, :].astype(F32)
             gated = linear * gate
             held[index, rows, :] = gated.astype(BF16)
@@ -359,9 +363,9 @@
     got_a = exchange(packed_a)
     packed = call(
         functools.partial(pack_outer_body, chips, block),
-        [two] * chips,
+        [two] * (chips - 1),
         [HBM] * 4,
-        [VMEM] * chips,
+        [VMEM] * (chips - 1),
         [
             pltpu.VMEM((items_here, channels), BF16),
             pltpu.VMEM((items_here, channels), BF16),
@@ -371,7 +375,7 @@
         ],
         moved=2 * domains * block_bytes,
     )(*(in_hbm(v) for v in (send_lists, partner_send, features, partner_feats)))
-    got_b = [packed[0]] + to_chips(packed, FORWARD)
+    got_b = to_chips(dict(zip(range(1, chips), packed)), FORWARD)
 
     tile_rows = block * slots
     adj_flat = adjacency.reshape(snaps_here, items_here * slots, block)
@@ -383,11 +387,11 @@
         moved=4 * taps * channels * doubled,
     )(temporal_weight)
 
-    def hidden_of(inner, arrived):
+    def hidden_of(inner, arrived, extra=()):
         return call(
             functools.partial(hidden_body, inner, chips, slots),
             shape((items_here, channels)),
-            [SMEM, HBM, VMEM, HBM] + [HBM] * len(arrived),
+            [SMEM, HBM, VMEM, HBM] + [SMEM, HBM][: len(extra)] + [HBM] * len(arrived),
             VMEM,
             [
                 pltpu.VMEM((items_here, channels), BF16),
@@ -400,11 +404,11 @@
             ],
             flops=(slots + 1) * item_flops,
             moved=(slots + 4) * items_here * channels * 2,
-        )(cols, features, adj_flat, in_hbm(spatial_weight), *(in_hbm(v) for v in arrived))
+        )(cols, features, adj_flat, in_hbm(spatial_weight), *extra, *(in_hbm(v) for v in arrived))
 
     hidden_a = hidden_of(True, [got_a])
     hidden_n = lax.ppermute(hidden_a, "snap", other_snap)
-    hidden_b = hidden_of(False, got_b)
+    hidden_b = hidden_of(False, got_b, (partner_send, in_hbm(partner_feats)))
 
     back_scratch = [
         pltpu.VMEM((items_here, channels), BF16),

time: 78.6 us -> 78.7 us (level)
  starting transfers between devices: 42.5 us -> 43.6 us
where the time goes in v5:
time: 78.7 us; the launch traced here: 77.7 us
  starting transfers between devices  43.6 us (55%)
  Pallas kernels  19.1 us (24%)
  waiting for transfers between devices  13.4 us (17%)
  between operations  0.96 us (1%)
    ppermute x14, starting transfers between devices, to_chips(): done[offset] = lax.ppermute(payloads[offset], 'dom', pairs)  25.6 us
    all_to_all x2, starting transfers between devices, exchange(): lax.all_to_all(values, 'dom', split_axis=0, concat_axis=0, tiled=True)  14.2 us
    ppermute x14, waiting for transfers between devices, to_chips(): done[offset] = lax.ppermute(payloads[offset], 'dom', pairs)  13.4 us
    pallas_call x2, Pallas kernels, hidden_of(): call(functools.partial(hidden_body, inner, chips, slots), shape((items_he...  5.03 us
    pallas_call x1, Pallas kernels, local_pair(): call(functools.partial(temporal_body, chips, blocks_here, slots, TILE), [...  3.59 us
    pallas_call x1, Pallas kernels, local_pair(): call(functools.partial(inner_body, chips, blocks_here, slots), [two] * ch...  2.67 us
    pallas_call x1, Pallas kernels, local_pair(): call(functools.partial(pack_inner_body, domains, block), shape_hbm((domai...  2.29 us
    pallas_call x1, Pallas kernels, local_pair(): call(functools.partial(pack_outer_body, chips, block), [two] * (chips - 1...  1.77 us
  transfers between devices with their start and end apart: 21, of which 5 were waited for; matrix products, arithmetic and copies ran while one was open for 0% of the time, Pallas kernels for 18%

profile of v5, /device:TPU:0, one launch (start us, length us, event | category | flops | bytes accessed | tf_op | source)
XLA Modules:
  0.0 77.7 jit_solution(17199109952863809831)
XLA Ops:
  0.6 0.0 copy-start
  0.7 0.0 copy-start.5
  0.7 0.5 collective-permute-start.1
  1.2 0.1 collective-permute-start
  1.3 2.3 %shard_map.95 = bf16[16,128,128]{2,1,0:T(8,128)(2,1)} custom-call(s32[2,1,16]{2,1,0:T(1,128)} %send.5, bf16[2,1152,128]{2,1,0:T(8,128)(2,1)} %feats.7), custom_call_target="tpu_custom_call" | custom-call | bytes 104857600 | tf_op jit(solution)/shard_map/pallas_call | solution.py:348
  3.6 0.0 collective-permute-done.partner_lists.rest_0_
  3.6 0.0 collective-permute-done.1.partner_feats.rest_1_
  3.6 7.4 %all-to-all-start = ((bf16[16,128,128]{2,1,0:T(8,128)(2,1)}), bf16[16,128,128]{2,1,0:T(8,128)(2,1)}, u32[]{:S(2)}, u32[]{:S(2)}) async-start(bf16[16,128,128]{2,1,0:T(8,128)(2,1)} %shard_map.95), calls=%async_computation | async-start | bytes 1048576 | tf_op jit(solution)/shard_map/all_to_all | solution.py:335
  11.0 0.0 copy-done.3
  11.0 1.8 %shard_map.97 = (bf16[2,128,128]{2,1,0:T(8,128)(2,1)S(1)}, bf16[2,128,128]{2,1,0:T(8,128)(2,1)}, bf16[2,128,128]{2,1,0:T(8,128)(2,1)S(1)}, bf16[2,128,128]{2,1,0...) custom-call(s32[2,1,16]{2,1,0:T(1,128)} %send.5, ...), custom_call_target="tpu_custom_call" | custom-call | bytes 104857600 | tf_op jit(solution)/shard_map/pallas_call | solution.py:364
  12.8 1.9 %collective-permute-start.2 = (bf16[2,128,128]{2,1,0:T(8,128)(2,1)S(1)}, bf16[2,128,128]{2,1,0:T(8,128)(2,1)S(1)}, u32[]{:S(2)}, u32[]{:S(2)}) collective-permute-start(bf16[2,128,128]{2,1,0:T(8,128)(2,1)S(1)} %get-tuple-element.29), channel_id=1, source_target_pairs={{0,2},{1,3},{2,0},{3,1},{4,6},{5,7},{6,4},{7,5},{8,10},{9,11},{10,... | collective-permute-start | bytes 196616 | tf_op jit(solution)/shard_map/ppermute | solution.py:341
  14.7 1.5 %collective-permute-start.3 = (bf16[2,128,128]{2,1,0:T(8,128)(2,1)S(1)}, bf16[2,128,128]{2,1,0:T(8,128)(2,1)S(1)}, u32[]{:S(2)}, u32[]{:S(2)}) collective-permute-start(bf16[2,128,128]{2,1,0:T(8,128)(2,1)S(1)} %get-tuple-element.30), channel_id=1, source_target_pairs={{0,6},{1,7},{2,4},{3,5},{4,2},{5,3},{6,0},{7,1},{8,14},{9,15},{10,... | collective-permute-start | bytes 196616 | tf_op jit(solution)/shard_map/ppermute | solution.py:341
  16.2 0.0 copy-done.1
  16.2 0.1 shard_map.99.twt
  16.4 0.2 collective-permute-start.4
  16.6 3.7 %collective-permute-start.5 = (bf16[2,128,128]{2,1,0:T(8,128)(2,1)}, bf16[2,128,128]{2,1,0:T(8,128)(2,1)}, u32[]{:S(2)}, u32[]{:S(2)}) collective-permute-start(bf16[2,128,128]{2,1,0:T(8,128)(2,1)} %get-tuple-element.32), channel_id=1, source_target_pairs={{0,10},{1,11},{2,8},{3,9},{4,14},{5,15},{6,12},{7,13},{8,2},{9,3},... | collective-permute-start | bytes 196616 | tf_op jit(solution)/shard_map/ppermute | solution.py:341
  20.2 0.6 collective-permute-start.6
  20.8 0.0 collective-permute-done.2.rest_2_
  20.8 3.6 %collective-permute-start.7 = (bf16[2,128,128]{2,1,0:T(8,128)(2,1)S(1)}, bf16[2,128,128]{2,1,0:T(8,128)(2,1)}, u32[]{:S(2)}, u32[]{:S(2)}) collective-permute-start(bf16[2,128,128]{2,1,0:T(8,128)(2,1)S(1)} %get-tuple-element.34), channel_id=1, source_target_pairs={{0,14},{1,15},{2,12},{3,13},{4,10},{5,11},{6,8},{7,9},{8,6},{9,7},... | collective-permute-start | bytes 196616 | tf_op jit(solution)/shard_map/ppermute | solution.py:341
  24.4 0.0 collective-permute-done.3.rest_3_
  24.5 0.6 copy-done.13
  25.1 1.8 %collective-permute-start.8 = (bf16[2,128,128]{2,1,0:T(8,128)(2,1)S(1)}, bf16[2,128,128]{2,1,0:T(8,128)(2,1)}, u32[]{:S(2)}, u32[]{:S(2)}) collective-permute-start(bf16[2,128,128]{2,1,0:T(8,128)(2,1)S(1)} %get-tuple-element.35), channel_id=1, source_target_pairs={{0,12},{1,13},{2,14},{3,15},{4,8},{5,9},{6,10},{7,11},{8,4},{9,5},... | collective-permute-start | bytes 196616 | tf_op jit(solution)/shard_map/ppermute | solution.py:341
  26.9 0.0 all-to-all-done.rest_0_
  26.9 2.5 %shard_map.96.ha = bf16[1152,128]{1,0:T(8,128)(2,1)S(1)} custom-call(s32[2,4,9]{2,1,0:T(4,128)S(1)} %bitcast.7, bf16[2,1152,128]{2,1,0:T(8,128)(2,1)S(1)} %copy-done, bf16[2,4608,128]{2,1,0:T(8,128)(2,1)S(1)} %bitcast.4, bf16[128,128]{1,0:T(8,128)(2,1)} %sw.3, bf16[16,128,128]{2,1,0:T(8,128)(2,1)} %all-to-all-done.rest_0_), custom_call_target="tpu_custom_call" | custom-call | flops 18874368000 | bytes 235929600 | tf_op jit(solution)/shard_map/pallas_call | solution.py:391
  29.4 0.0 copy-start.6
  29.5 0.0 copy-start.7
  29.5 0.0 copy-start.8
  29.5 0.0 copy-start.11
  29.5 0.0 collective-permute-done.4.rest_4_
  29.5 1.6 %collective-permute-start.9 = (bf16[1152,128]{1,0:T(8,128)(2,1)S(1)}, bf16[1152,128]{1,0:T(8,128)(2,1)S(1)}, u32[]{:S(2)}, u32[]{:S(2)}) collective-permute-start(bf16[1152,128]{1,0:T(8,128)(2,1)S(1)} %shard_map.96.ha), channel_id=1, source_target_pairs={{0,16},{16,0},{1,17},{17,1},{2,18},{18,2},{3,19},{19,3},{4,20},{20... | collective-permute-start | bytes 884744 | tf_op jit(solution)/shard_map/ppermute | solution.py:410
  31.1 3.7 %collective-permute-done.5.rest_5_ = bf16[2,128,128]{2,1,0:T(8,128)(2,1)} collective-permute-done((bf16[2,128,128]{2,1,0:T(8,128)(2,1)}, bf16[2,128,128]{2,1,0:T(8,128)(2,1)}, u32[]{:S(2)}, u32[]{:S(2)}) %collective-permute-start.5) | collective-permute-done | bytes 65568 | tf_op jit(solution)/shard_map/ppermute | solution.py:341
  34.8 0.5 collective-permute-done.6.rest_6_
  35.3 0.0 collective-permute-done.7.rest_7_
  35.3 0.0 collective-permute-done.8.rest_8_
  35.3 2.5 %shard_map.98.hb = bf16[1152,128]{1,0:T(8,128)(2,1)S(1)} custom-call(s32[2,4,9]{2,1,0:T(4,128)S(1)} %bitcast.8, bf16[2,1152,128]{2,1,0:T(8,128)(2,1)S(1)} %copy-done, bf16[2,4608,128]{2,1,0:T(8,128)(2,1)S(1)} %bitcast.5, bf16[128,128]{1,0:T(8,128)(2,1)} %sw.3, s32[2,1,16]{2,1,0:T(1,128)S(1)} %copy-done.4, ...), custom_call_target="tpu_custom_call" | custom-call | flops 18874368000 | bytes 235929600 | tf_op jit(solution)/shard_map/pallas_call | solution.py:391
  37.8 0.0 collective-permute-done.9.hn
  37.8 0.0 copy-start.9
  37.8 3.6 %shard_map.100 = (bf16[16,128,128]{2,1,0:T(8,128)(2,1)}, bf16[2,1152,128]{2,1,0:T(8,128)(2,1)}, bf16[1152,128]{1,0:T(8,128)(2,1)S(1)}, f32[1152,128]{1,0:T(8,128)S(1)}, f32[9,128,128]{2,1,0:T(8,128)S(1)}) custom-call(s32[2,4,9]{2,1,0:T(4,128)S(1)} %bitcast.9, bf16[1152,128]{1,0:T(8,128)(2,1)S(1)} %shard_map.96.ha, bf16[1152,128]{1,0:T(8,128)(2,1)S(1)} %shard_map.98.hb, ...), custom_call_target="tpu_custom_call" | custom-call | flops 98146713600 | bytes 589824000 | tf_op jit(solution)/shard_map/pallas_call | solution.py:420
  41.4 1.6 %collective-permute-start.10 = (bf16[1152,128]{1,0:T(8,128)(2,1)S(1)}, bf16[1152,128]{1,0:T(8,128)(2,1)S(1)}, u32[]{:S(2)}, u32[]{:S(2)}) collective-permute-start(bf16[1152,128]{1,0:T(8,128)(2,1)S(1)} %get-tuple-element.38), channel_id=1, source_target_pairs={{0,16},{16,0},{1,17},{17,1},{2,18},{18,2},{3,19},{19,3},{4,20},{20... | collective-permute-start | bytes 884744 | tf_op jit(solution)/shard_map/ppermute | solution.py:451
  43.0 6.8 %all-to-all-start.1 = ((bf16[16,128,128]{2,1,0:T(8,128)(2,1)}), bf16[16,128,128]{2,1,0:T(8,128)(2,1)S(1)}, u32[]{:S(2)}, u32[]{:S(2)}) async-start(bf16[16,128,128]{2,1,0:T(8,128)(2,1)} %get-tuple-element.49), calls=%async_computation.1 | async-start | bytes 1048576 | tf_op jit(solution)/shard_map/all_to_all | solution.py:335
  49.8 0.0 collective-permute-done.10.partial
  49.8 0.0 copy-start.2
  49.8 2.7 %shard_map.101 = (bf16[2,128,128]{2,1,0:T(8,128)(2,1)S(1)}, bf16[2,128,128]{2,1,0:T(8,128)(2,1)S(1)}, bf16[2,128,128]{2,1,0:T(8,128)(2,1)S(1)}, bf16[2,128,128]{...) custom-call(s32[2,4,9]{2,1,0:T(4,128)S(1)} %bitcast.10, ...), custom_call_target="tpu_custom_call" | custom-call | flops 18874368000 | bytes 353894400 | tf_op jit(solution)/shard_map/pallas_call | solution.py:454
  52.5 2.0 %collective-permute-start.11 = (bf16[2,128,128]{2,1,0:T(8,128)(2,1)S(1)}, bf16[2,128,128]{2,1,0:T(8,128)(2,1)S(1)}, u32[]{:S(2)}, u32[]{:S(2)}) collective-permute-start(bf16[2,128,128]{2,1,0:T(8,128)(2,1)S(1)} %get-tuple-element.40), channel_id=1, source_target_pairs={{0,2},{1,3},{2,0},{3,1},{4,6},{5,7},{6,4},{7,5},{8,10},{9,11},{10,... | collective-permute-start | bytes 196616 | tf_op jit(solution)/shard_map/ppermute | solution.py:341
  54.5 2.7 %collective-permute-start.12 = (bf16[2,128,128]{2,1,0:T(8,128)(2,1)S(1)}, bf16[2,128,128]{2,1,0:T(8,128)(2,1)S(1)}, u32[]{:S(2)}, u32[]{:S(2)}) collective-permute-start(bf16[2,128,128]{2,1,0:T(8,128)(2,1)S(1)} %get-tuple-element.41), channel_id=1, source_target_pairs={{0,4},{1,5},{2,6},{3,7},{4,0},{5,1},{6,2},{7,3},{8,12},{9,13},{10,... | collective-permute-start | bytes 196616 | tf_op jit(solution)/shard_map/ppermute | solution.py:341
  57.1 0.0 collective-permute-start.13
  57.1 3.0 %collective-permute-start.14 = (bf16[2,128,128]{2,1,0:T(8,128)(2,1)S(1)}, bf16[2,128,128]{2,1,0:T(8,128)(2,1)S(1)}, u32[]{:S(2)}, u32[]{:S(2)}) collective-permute-start(bf16[2,128,128]{2,1,0:T(8,128)(2,1)S(1)} %get-tuple-element.43), channel_id=1, source_target_pairs={{0,10},{1,11},{2,8},{3,9},{4,14},{5,15},{6,12},{7,13},{8,2},{9,3},... | collective-permute-start | bytes 196616 | tf_op jit(solution)/shard_map/ppermute | solution.py:341
  60.1 0.8 %collective-permute-start.15 = (bf16[2,128,128]{2,1,0:T(8,128)(2,1)S(1)}, bf16[2,128,128]{2,1,0:T(8,128)(2,1)S(1)}, u32[]{:S(2)}, u32[]{:S(2)}) collective-permute-start(bf16[2,128,128]{2,1,0:T(8,128)(2,1)S(1)} %get-tuple-element.44), channel_id=1, source_target_pairs={{0,8},{1,9},{2,10},{3,11},{4,12},{5,13},{6,14},{7,15},{8,0},{9,1},... | collective-permute-start | bytes 196616 | tf_op jit(solution)/shard_map/ppermute | solution.py:341
  61.0 0.0 collective-permute-done.11.rest_0_.refs_1_
  61.0 2.6 %collective-permute-start.16 = (bf16[2,128,128]{2,1,0:T(8,128)(2,1)S(1)}, bf16[2,128,128]{2,1,0:T(8,128)(2,1)S(1)}, u32[]{:S(2)}, u32[]{:S(2)}) collective-permute-start(bf16[2,128,128]{2,1,0:T(8,128)(2,1)S(1)} %get-tuple-element.45), channel_id=1, source_target_pairs={{0,14},{1,15},{2,12},{3,13},{4,10},{5,11},{6,8},{7,9},{8,6},{9,7},... | collective-permute-start | bytes 196616 | tf_op jit(solution)/shard_map/ppermute | solution.py:341
  63.6 0.0 collective-permute-done.12.rest_1_.refs_2_
  63.6 1.2 %collective-permute-start.17 = (bf16[2,128,128]{2,1,0:T(8,128)(2,1)S(1)}, bf16[2,128,128]{2,1,0:T(8,128)(2,1)S(1)}, u32[]{:S(2)}, u32[]{:S(2)}) collective-permute-start(bf16[2,128,128]{2,1,0:T(8,128)(2,1)S(1)} %get-tuple-element.46), channel_id=1, source_target_pairs={{0,12},{1,13},{2,14},{3,15},{4,8},{5,9},{6,10},{7,11},{8,4},{9,5},... | collective-permute-start | bytes 196616 | tf_op jit(solution)/shard_map/ppermute | solution.py:341
  64.8 0.3 collective-permute-done.13.rest_2_.refs_3_
  65.1 8.4 %collective-permute-done.14.rest_3_.refs_4_ = bf16[2,128,128]{2,1,0:T(8,128)(2,1)S(1)} collective-permute-done((bf16[2,128,128]{2,1,0:T(8,128)(2,1)S(1)}, bf16[2,128,128]{2,1,0:T(8,128)(2,1)S(1)}, u32[]{:S(2)}, u32[]{:S(2)}) %collective-permute-start.14) | collective-permute-done | bytes 65568 | tf_op jit(solution)/shard_map/ppermute | solution.py:341
  73.5 0.5 collective-permute-done.15.rest_4_.refs_5_
  74.0 0.0 collective-permute-done.16.rest_5_.refs_6_
  74.0 0.0 collective-permute-done.17.rest_6_.refs_7_
  74.0 0.4 shard_map.103
  74.4 0.1 collective-permute-start.18
  74.5 0.7 shard_map.102.part
  75.2 0.0 all-to-all-done.1.arrived
  75.2 0.9 %shard_map.104.outer = bf16[1152,128]{1,0:T(8,128)(2,1)S(1)} custom-call(s32[2,1,16]{2,1,0:T(1,128)S(1)} %copy-done.2, f32[9,128,128]{2,1,0:T(8,128)S(1)} %get-tuple-element.48.local, bf16[16,128,128]{2,1,0:T(8,128)(2,1)S(1)} %all-to-all-done.1.arrived), custom_call_target="tpu_custom_call" | custom-call | flops 26214400 | bytes 235929600 | tf_op jit(solution)/shard_map/pallas_call | solution.py:479
  76.1 0.0 collective-permute-done.18.swapped
  76.1 1.6 %shard_map.105 = bf16[2,1152,128]{2,1,0:T(8,128)(2,1)} custom-call(s32[2,1,16]{2,1,0:T(1,128)S(1)} %copy-done.2, f32[9,128,128]{2,1,0:T(8,128)S(1)} %shard_map.102.part, bf16[8,128,128]{2,1,0:T(8,128)(2,1)S(1)} %collective-permute-done.18.swapped, bf16[1152,128]{1,0:T(8,128)(2,1)S(1)} %shard_map.104.outer), custom_call_target="tpu_custom_call" | custom-call | flops 26214400 | bytes 235929600 | tf_op jit(solution)/shard_map/pallas_call | solution.py:494
  (17 shorter events, 0.0 us)
Async XLA Ops:
  0.6 26.2 %copy-start = (bf16[2,1152,128]{2,1,0:T(8,128)(2,1)S(1)}, bf16[2,1152,128]{2,1,0:T(8,128)(2,1)}, u32[]{:S(2)}) copy-start(bf16[2,1152,128]{2,1,0:T(8,128)(2,1)} %feats.7) | copy-start | bytes 1769476
  0.6 15.6 %copy-start.1 = (bf16[3,128,256]{2,1,0:T(8,128)(2,1)S(1)}, bf16[3,128,256]{2,1,0:T(8,128)(2,1)}, u32[]{:S(2)}) copy-start(bf16[3,128,256]{2,1,0:T(8,128)(2,1)} %tw.3) | copy-start | bytes 589828
  0.7 26.2 %copy-start.10 = (s32[2,9,4]{1,2,0:T(4,128)S(1)}, s32[2,9,4]{1,2,0:T(4,128)}, u32[]{:S(2)}) copy-start(s32[2,9,4]{1,2,0:T(4,128)} %param.11) | copy-start | bytes 868
  0.7 26.2 %copy-start.5 = (bf16[2,1152,4,128]{3,2,1,0:T(4,128)(2,1)S(1)}, bf16[2,1152,4,128]{3,2,1,0:T(4,128)(2,1)}, u32[]{:S(2)}) copy-start(bf16[2,1152,4,128]{3,2,1,0:T(4,128)(2,1)} %param.10) | copy-start | bytes 7077892
  0.7 2.9 %collective-permute-start.1 = (bf16[2,1152,128]{2,1,0:T(8,128)(2,1)}, bf16[2,1152,128]{2,1,0:T(8,128)(2,1)}, u32[]{:S(2)}, u32[]{:S(2)}) collective-permute-start(bf16[2,1152,128]{2,1,0:T(8,128)(2,1)} %feats.7), channel_id=1, source_target_pairs={{0,1},{1,0},{2,3},{3,2},{4,5},{5,4},{6,7},{7,6},{8,9},{9,8},{10,11... | collective-permute-start | bytes 1769480 | tf_op jit(solution)/shard_map/ppermute | solution.py:332
  1.2 2.4 %collective-permute-start = (s32[2,1,16]{2,1,0:T(1,128)}, s32[2,1,16]{2,1,0:T(1,128)S(1)}, u32[]{:S(2)}, u32[]{:S(2)}) collective-permute-start(s32[2,1,16]{2,1,0:T(1,128)} %send.5), channel_id=1, source_target_pairs={{0,1},{1,0},{2,3},{3,2},{4,5},{5,4},{6,7},{7,6},{8,9},{9,8},{10,11... | collective-permute-start | bytes 392 | tf_op jit(solution)/shard_map/ppermute | solution.py:332
  3.6 7.4 %copy-start.3 = (s32[2,1,16]{2,1,0:T(1,128)}, s32[2,1,16]{2,1,0:T(1,128)S(1)}, u32[]{:S(2)}) copy-start(s32[2,1,16]{2,1,0:T(1,128)S(1)} %collective-permute-done.partner_lists.rest_0_) | copy-start | bytes 388
  3.6 23.3 %all-to-all-start = ((bf16[16,128,128]{2,1,0:T(8,128)(2,1)}), bf16[16,128,128]{2,1,0:T(8,128)(2,1)}, u32[]{:S(2)}, u32[]{:S(2)}) async-start(bf16[16,128,128]{2,1,0:T(8,128)(2,1)} %shard_map.95), calls=%async_computation | async-start | bytes 1048576 | tf_op jit(solution)/shard_map/all_to_all | solution.py:335
  12.8 8.0 %collective-permute-start.2 = (bf16[2,128,128]{2,1,0:T(8,128)(2,1)S(1)}, bf16[2,128,128]{2,1,0:T(8,128)(2,1)S(1)}, u32[]{:S(2)}, u32[]{:S(2)}) collective-permute-start(bf16[2,128,128]{2,1,0:T(8,128)(2,1)S(1)} %get-tuple-element.29), channel_id=1, source_target_pairs={{0,2},{1,3},{2,0},{3,1},{4,6},{5,7},{6,4},{7,5},{8,10},{9,11},{10,... | collective-permute-start | bytes 196616 | tf_op jit(solution)/shard_map/ppermute | solution.py:341
  14.7 9.7 %collective-permute-start.3 = (bf16[2,128,128]{2,1,0:T(8,128)(2,1)S(1)}, bf16[2,128,128]{2,1,0:T(8,128)(2,1)S(1)}, u32[]{:S(2)}, u32[]{:S(2)}) collective-permute-start(bf16[2,128,128]{2,1,0:T(8,128)(2,1)S(1)} %get-tuple-element.30), channel_id=1, source_target_pairs={{0,6},{1,7},{2,4},{3,5},{4,2},{5,3},{6,0},{7,1},{8,14},{9,15},{10,... | collective-permute-start | bytes 196616 | tf_op jit(solution)/shard_map/ppermute | solution.py:341
  16.4 13.1 %collective-permute-start.4 = (bf16[2,128,128]{2,1,0:T(8,128)(2,1)}, bf16[2,128,128]{2,1,0:T(8,128)(2,1)}, u32[]{:S(2)}, u32[]{:S(2)}) collective-permute-start(bf16[2,128,128]{2,1,0:T(8,128)(2,1)} %get-tuple-element.31), channel_id=1, source_target_pairs={{0,4},{1,5},{2,6},{3,7},{4,0},{5,1},{6,2},{7,3},{8,12},{9,13},{10,... | collective-permute-start | bytes 196616 | tf_op jit(solution)/shard_map/ppermute | solution.py:341
  16.6 18.2 %collective-permute-start.5 = (bf16[2,128,128]{2,1,0:T(8,128)(2,1)}, bf16[2,128,128]{2,1,0:T(8,128)(2,1)}, u32[]{:S(2)}, u32[]{:S(2)}) collective-permute-start(bf16[2,128,128]{2,1,0:T(8,128)(2,1)} %get-tuple-element.32), channel_id=1, source_target_pairs={{0,10},{1,11},{2,8},{3,9},{4,14},{5,15},{6,12},{7,13},{8,2},{9,3},... | collective-permute-start | bytes 196616 | tf_op jit(solution)/shard_map/ppermute | solution.py:341
  20.2 15.0 %collective-permute-start.6 = (bf16[2,128,128]{2,1,0:T(8,128)(2,1)S(1)}, bf16[2,128,128]{2,1,0:T(8,128)(2,1)}, u32[]{:S(2)}, u32[]{:S(2)}) collective-permute-start(bf16[2,128,128]{2,1,0:T(8,128)(2,1)S(1)} %get-tuple-element.33), channel_id=1, source_target_pairs={{0,8},{1,9},{2,10},{3,11},{4,12},{5,13},{6,14},{7,15},{8,0},{9,1},... | collective-permute-start | bytes 196616 | tf_op jit(solution)/shard_map/ppermute | solution.py:341
  20.8 3.6 %copy-start.12 = (bf16[2,128,128]{2,1,0:T(8,128)(2,1)}, bf16[2,128,128]{2,1,0:T(8,128)(2,1)S(1)}, u32[]{:S(2)}) copy-start(bf16[2,128,128]{2,1,0:T(8,128)(2,1)S(1)} %collective-permute-done.2.rest_2_) | copy-start | bytes 196612
  20.8 14.5 %collective-permute-start.7 = (bf16[2,128,128]{2,1,0:T(8,128)(2,1)S(1)}, bf16[2,128,128]{2,1,0:T(8,128)(2,1)}, u32[]{:S(2)}, u32[]{:S(2)}) collective-permute-start(bf16[2,128,128]{2,1,0:T(8,128)(2,1)S(1)} %get-tuple-element.34), channel_id=1, source_target_pairs={{0,14},{1,15},{2,12},{3,13},{4,10},{5,11},{6,8},{7,9},{8,6},{9,7},... | collective-permute-start | bytes 196616 | tf_op jit(solution)/shard_map/ppermute | solution.py:341
  24.4 0.6 copy-start.13
  25.1 10.2 %collective-permute-start.8 = (bf16[2,128,128]{2,1,0:T(8,128)(2,1)S(1)}, bf16[2,128,128]{2,1,0:T(8,128)(2,1)}, u32[]{:S(2)}, u32[]{:S(2)}) collective-permute-start(bf16[2,128,128]{2,1,0:T(8,128)(2,1)S(1)} %get-tuple-element.35), channel_id=1, source_target_pairs={{0,12},{1,13},{2,14},{3,15},{4,8},{5,9},{6,10},{7,11},{8,4},{9,5},... | collective-permute-start | bytes 196616 | tf_op jit(solution)/shard_map/ppermute | solution.py:341
  26.9 8.4 %copy-start.4 = (s32[2,1,16]{2,1,0:T(1,128)S(1)}, s32[2,1,16]{2,1,0:T(1,128)}, u32[]{:S(2)}) copy-start(s32[2,1,16]{2,1,0:T(1,128)} %copy-done.3) | copy-start | bytes 388
  29.4 8.3 %copy-start.6 = (bf16[2,1152,4,128]{3,2,1,0:T(4,128)(2,1)S(1)}, bf16[2,1152,4,128]{3,2,1,0:T(4,128)(2,1)}, u32[]{:S(2)}) copy-start(bf16[2,1152,4,128]{3,2,1,0:T(4,128)(2,1)} %param.10) | copy-start | bytes 7077892
  29.5 8.3 %copy-start.7 = (bf16[2,1152,128]{2,1,0:T(8,128)(2,1)S(1)}, bf16[2,1152,128]{2,1,0:T(8,128)(2,1)}, u32[]{:S(2)}) copy-start(bf16[2,1152,128]{2,1,0:T(8,128)(2,1)} %cot.1) | copy-start | bytes 1769476
  29.5 8.3 %copy-start.8 = (bf16[128,128]{1,0:T(8,128)(2,1)S(1)}, bf16[128,128]{1,0:T(8,128)(2,1)}, u32[]{:S(2)}) copy-start(bf16[128,128]{1,0:T(8,128)(2,1)} %sw.3) | copy-start | bytes 98308
  29.5 8.3 %copy-start.11 = (f32[256]{0:T(256)S(1)}, f32[256]{0:T(256)}, u32[]{:S(2)}) copy-start(f32[256]{0:T(256)} %param.15) | copy-start | bytes 3076
  29.5 8.3 %collective-permute-start.9 = (bf16[1152,128]{1,0:T(8,128)(2,1)S(1)}, bf16[1152,128]{1,0:T(8,128)(2,1)S(1)}, u32[]{:S(2)}, u32[]{:S(2)}) collective-permute-start(bf16[1152,128]{1,0:T(8,128)(2,1)S(1)} %shard_map.96.ha), channel_id=1, source_target_pairs={{0,16},{16,0},{1,17},{17,1},{2,18},{18,2},{3,19},{19,3},{4,20},{20... | collective-permute-start | bytes 884744 | tf_op jit(solution)/shard_map/ppermute | solution.py:410
  37.8 12.0 %copy-start.9 = (bf16[128,128]{1,0:T(8,128)(2,1)S(1)}, bf16[128,128]{1,0:T(8,128)(2,1)}, u32[]{:S(2)}) copy-start(bf16[128,128]{1,0:T(8,128)(2,1)} %sw.3) | copy-start | bytes 98308
  41.4 8.4 %collective-permute-start.10 = (bf16[1152,128]{1,0:T(8,128)(2,1)S(1)}, bf16[1152,128]{1,0:T(8,128)(2,1)S(1)}, u32[]{:S(2)}, u32[]{:S(2)}) collective-permute-start(bf16[1152,128]{1,0:T(8,128)(2,1)S(1)} %get-tuple-element.38), channel_id=1, source_target_pairs={{0,16},{16,0},{1,17},{17,1},{2,18},{18,2},{3,19},{19,3},{4,20},{20... | collective-permute-start | bytes 884744 | tf_op jit(solution)/shard_map/ppermute | solution.py:451
  43.0 32.2 %all-to-all-start.1 = ((bf16[16,128,128]{2,1,0:T(8,128)(2,1)}), bf16[16,128,128]{2,1,0:T(8,128)(2,1)S(1)}, u32[]{:S(2)}, u32[]{:S(2)}) async-start(bf16[16,128,128]{2,1,0:T(8,128)(2,1)} %get-tuple-element.49), calls=%async_computation.1 | async-start | bytes 1048576 | tf_op jit(solution)/shard_map/all_to_all | solution.py:335
  49.8 24.7 %copy-start.2 = (s32[2,1,16]{2,1,0:T(1,128)S(1)}, s32[2,1,16]{2,1,0:T(1,128)}, u32[]{:S(2)}) copy-start(s32[2,1,16]{2,1,0:T(1,128)} %send.5) | copy-start | bytes 388
  52.5 8.5 %collective-permute-start.11 = (bf16[2,128,128]{2,1,0:T(8,128)(2,1)S(1)}, bf16[2,128,128]{2,1,0:T(8,128)(2,1)S(1)}, u32[]{:S(2)}, u32[]{:S(2)}) collective-permute-start(bf16[2,128,128]{2,1,0:T(8,128)(2,1)S(1)} %get-tuple-element.40), channel_id=1, source_target_pairs={{0,2},{1,3},{2,0},{3,1},{4,6},{5,7},{6,4},{7,5},{8,10},{9,11},{10,... | collective-permute-start | bytes 196616 | tf_op jit(solution)/shard_map/ppermute | solution.py:341
  54.5 9.1 %collective-permute-start.12 = (bf16[2,128,128]{2,1,0:T(8,128)(2,1)S(1)}, bf16[2,128,128]{2,1,0:T(8,128)(2,1)S(1)}, u32[]{:S(2)}, u32[]{:S(2)}) collective-permute-start(bf16[2,128,128]{2,1,0:T(8,128)(2,1)S(1)} %get-tuple-element.41), channel_id=1, source_target_pairs={{0,4},{1,5},{2,6},{3,7},{4,0},{5,1},{6,2},{7,3},{8,12},{9,13},{10,... | collective-permute-start | bytes 196616 | tf_op jit(solution)/shard_map/ppermute | solution.py:341
  57.1 7.9 %collective-permute-start.13 = (bf16[2,128,128]{2,1,0:T(8,128)(2,1)S(1)}, bf16[2,128,128]{2,1,0:T(8,128)(2,1)S(1)}, u32[]{:S(2)}, u32[]{:S(2)}) collective-permute-start(bf16[2,128,128]{2,1,0:T(8,128)(2,1)S(1)} %get-tuple-element.42), channel_id=1, source_target_pairs={{0,6},{1,7},{2,4},{3,5},{4,2},{5,3},{6,0},{7,1},{8,14},{9,15},{10,... | collective-permute-start | bytes 196616 | tf_op jit(solution)/shard_map/ppermute | solution.py:341
  57.1 16.3 %collective-permute-start.14 = (bf16[2,128,128]{2,1,0:T(8,128)(2,1)S(1)}, bf16[2,128,128]{2,1,0:T(8,128)(2,1)S(1)}, u32[]{:S(2)}, u32[]{:S(2)}) collective-permute-start(bf16[2,128,128]{2,1,0:T(8,128)(2,1)S(1)} %get-tuple-element.43), channel_id=1, source_target_pairs={{0,10},{1,11},{2,8},{3,9},{4,14},{5,15},{6,12},{7,13},{8,2},{9,3},... | collective-permute-start | bytes 196616 | tf_op jit(solution)/shard_map/ppermute | solution.py:341
  60.1 13.8 %collective-permute-start.15 = (bf16[2,128,128]{2,1,0:T(8,128)(2,1)S(1)}, bf16[2,128,128]{2,1,0:T(8,128)(2,1)S(1)}, u32[]{:S(2)}, u32[]{:S(2)}) collective-permute-start(bf16[2,128,128]{2,1,0:T(8,128)(2,1)S(1)} %get-tuple-element.44), channel_id=1, source_target_pairs={{0,8},{1,9},{2,10},{3,11},{4,12},{5,13},{6,14},{7,15},{8,0},{9,1},... | collective-permute-start | bytes 196616 | tf_op jit(solution)/shard_map/ppermute | solution.py:341
  61.0 13.0 %collective-permute-start.16 = (bf16[2,128,128]{2,1,0:T(8,128)(2,1)S(1)}, bf16[2,128,128]{2,1,0:T(8,128)(2,1)S(1)}, u32[]{:S(2)}, u32[]{:S(2)}) collective-permute-start(bf16[2,128,128]{2,1,0:T(8,128)(2,1)S(1)} %get-tuple-element.45), channel_id=1, source_target_pairs={{0,14},{1,15},{2,12},{3,13},{4,10},{5,11},{6,8},{7,9},{8,6},{9,7},... | collective-permute-start | bytes 196616 | tf_op jit(solution)/shard_map/ppermute | solution.py:341
  63.6 10.4 %collective-permute-start.17 = (bf16[2,128,128]{2,1,0:T(8,128)(2,1)S(1)}, bf16[2,128,128]{2,1,0:T(8,128)(2,1)S(1)}, u32[]{:S(2)}, u32[]{:S(2)}) collective-permute-start(bf16[2,128,128]{2,1,0:T(8,128)(2,1)S(1)} %get-tuple-element.46), channel_id=1, source_target_pairs={{0,12},{1,13},{2,14},{3,15},{4,8},{5,9},{6,10},{7,11},{8,4},{9,5},... | collective-permute-start | bytes 196616 | tf_op jit(solution)/shard_map/ppermute | solution.py:341
  74.4 1.7 %collective-permute-start.18 = (bf16[8,128,128]{2,1,0:T(8,128)(2,1)S(1)}, bf16[8,128,128]{2,1,0:T(8,128)(2,1)S(1)}, u32[]{:S(2)}, u32[]{:S(2)}) collective-permute-start(bf16[8,128,128]{2,1,0:T(8,128)(2,1)S(1)} %shard_map.103), channel_id=1, source_target_pairs={{0,1},{1,0},{2,3},{3,2},{4,5},{5,4},{6,7},{7,6},{8,9},{9,8},{10,11... | collective-permute-start | bytes 786440 | tf_op jit(solution)/shard_map/ppermute | solution.py:332

commit v6 on v4

--- a/solution.py
+++ b/solution.py
@@ -12,10 +12,10 @@
 VMEM = pl.BlockSpec(memory_space=pltpu.VMEM)
 SMEM = pl.BlockSpec(memory_space=pltpu.SMEM)
 HBM = pl.BlockSpec(memory_space=pltpu.MemorySpace.HBM)
-TILE = 384
+TILE = 1152
 VMEM_LIMIT = 16 * 1024 * 1024
 DMA = pltpu.SemaphoreType.DMA
-FORWARD = (1, 2, 3, 5, 4, 7, 6)
+FORWARD = (1, 3, 2, 5, 4, 7, 6)
 BACKWARD = (1, 2, 3, 5, 4, 7, 6)
 COST = 100
 

time: 78.6 us -> 78.5 us (level)
  no operation moved by 1% of the time
where the time goes in v6:
time: 78.5 us; the launch traced here: 77.6 us
  starting transfers between devices  42.9 us (55%)
  Pallas kernels  19.2 us (24%)
  waiting for transfers between devices  13.3 us (17%)
  local copies, waits for them, and re-layouts  1.29 us (2%)
  between operations  0.92 us (1%)
    ppermute x14, starting transfers between devices, to_chips(): done[offset] = lax.ppermute(payloads[offset], 'dom', pairs)  25.2 us
    all_to_all x2, starting transfers between devices, exchange(): lax.all_to_all(values, 'dom', split_axis=0, concat_axis=0, tiled=True)  13.9 us
    ppermute x14, waiting for transfers between devices, to_chips(): done[offset] = lax.ppermute(payloads[offset], 'dom', pairs)  13.2 us
    pallas_call x2, Pallas kernels, hidden_of(): call(functools.partial(hidden_body, inner, chips, slots), shape((items_he...  5.23 us
    pallas_call x1, Pallas kernels, local_pair(): call(functools.partial(temporal_body, chips, blocks_here, slots, TILE), [...  3.53 us
    pallas_call x1, Pallas kernels, local_pair(): call(functools.partial(inner_body, chips, blocks_here, slots), [two] * ch...  2.66 us
    pallas_call x1, Pallas kernels, local_pair(): call(functools.partial(pack_inner_body, domains, block), shape_hbm((domai...  2.29 us
    pallas_call x1, Pallas kernels, local_pair(): call(functools.partial(pack_outer_body, chips, block), [two] * chips, [HB...  1.78 us
  transfers between devices with their start and end apart: 21, of which 5 were waited for; matrix products, arithmetic and copies ran while one was open for 0% of the time, Pallas kernels for 18%

profile of v6, /device:TPU:0, one launch (start us, length us, event | category | flops | bytes accessed | tf_op | source)
XLA Modules:
  0.0 77.6 jit_solution(785938544738874554)
XLA Ops:
  0.6 0.0 copy-start
  0.7 0.0 copy-start.3
  0.7 0.5 collective-permute-start.1
  1.2 0.1 collective-permute-start
  1.3 2.3 %shard_map.95 = bf16[16,128,128]{2,1,0:T(8,128)(2,1)} custom-call(s32[2,1,16]{2,1,0:T(1,128)} %send.5, bf16[2,1152,128]{2,1,0:T(8,128)(2,1)} %feats.7), custom_call_target="tpu_custom_call" | custom-call | bytes 104857600 | tf_op jit(solution)/shard_map/pallas_call | solution.py:344
  3.6 0.0 collective-permute-done.partner_lists
  3.6 0.0 collective-permute-done.1.partner_feats
  3.6 7.4 %all-to-all-start = ((bf16[16,128,128]{2,1,0:T(8,128)(2,1)}), bf16[16,128,128]{2,1,0:T(8,128)(2,1)}, u32[]{:S(2)}, u32[]{:S(2)}) async-start(bf16[16,128,128]{2,1,0:T(8,128)(2,1)} %shard_map.95), calls=%async_computation | async-start | bytes 1048576 | tf_op jit(solution)/shard_map/all_to_all | solution.py:331
  11.0 0.0 copy-done.10
  11.0 1.8 %shard_map.97 = (bf16[2,128,128]{2,1,0:T(8,128)(2,1)S(1)}, bf16[2,128,128]{2,1,0:T(8,128)(2,1)S(1)}, bf16[2,128,128]{2,1,0:T(8,128)(2,1)}, bf16[2,128,128]{2,1,0...) custom-call(s32[2,1,16]{2,1,0:T(1,128)} %send.5, ...), custom_call_target="tpu_custom_call" | custom-call | bytes 104857600 | tf_op jit(solution)/shard_map/pallas_call | solution.py:360
  12.8 0.6 copy-done.6
  13.4 1.9 %collective-permute-start.2 = (bf16[2,128,128]{2,1,0:T(8,128)(2,1)S(1)}, bf16[2,128,128]{2,1,0:T(8,128)(2,1)S(1)}, u32[]{:S(2)}, u32[]{:S(2)}) collective-permute-start(bf16[2,128,128]{2,1,0:T(8,128)(2,1)S(1)} %get-tuple-element.31), channel_id=1, source_target_pairs={{0,2},{1,3},{2,0},{3,1},{4,6},{5,7},{6,4},{7,5},{8,10},{9,11},{10,... | collective-permute-start | bytes 196616 | tf_op jit(solution)/shard_map/ppermute | solution.py:337
  15.3 1.5 %collective-permute-start.3 = (bf16[2,128,128]{2,1,0:T(8,128)(2,1)S(1)}, bf16[2,128,128]{2,1,0:T(8,128)(2,1)S(1)}, u32[]{:S(2)}, u32[]{:S(2)}) collective-permute-start(bf16[2,128,128]{2,1,0:T(8,128)(2,1)S(1)} %get-tuple-element.32), channel_id=1, source_target_pairs={{0,6},{1,7},{2,4},{3,5},{4,2},{5,3},{6,0},{7,1},{8,14},{9,15},{10,... | collective-permute-start | bytes 196616 | tf_op jit(solution)/shard_map/ppermute | solution.py:337
  16.8 0.1 shard_map.99.twt
  16.9 0.2 collective-permute-start.4
  17.1 3.7 %collective-permute-start.5 = (bf16[2,128,128]{2,1,0:T(8,128)(2,1)}, bf16[2,128,128]{2,1,0:T(8,128)(2,1)}, u32[]{:S(2)}, u32[]{:S(2)}) collective-permute-start(bf16[2,128,128]{2,1,0:T(8,128)(2,1)} %get-tuple-element.34), channel_id=1, source_target_pairs={{0,10},{1,11},{2,8},{3,9},{4,14},{5,15},{6,12},{7,13},{8,2},{9,3},... | collective-permute-start | bytes 196616 | tf_op jit(solution)/shard_map/ppermute | solution.py:337
  20.8 0.6 collective-permute-start.6
  21.4 0.0 collective-permute-done.2.rest_1_
  21.4 3.4 %collective-permute-start.7 = (bf16[2,128,128]{2,1,0:T(8,128)(2,1)S(1)}, bf16[2,128,128]{2,1,0:T(8,128)(2,1)}, u32[]{:S(2)}, u32[]{:S(2)}) collective-permute-start(bf16[2,128,128]{2,1,0:T(8,128)(2,1)S(1)} %get-tuple-element.36), channel_id=1, source_target_pairs={{0,14},{1,15},{2,12},{3,13},{4,10},{5,11},{6,8},{7,9},{8,6},{9,7},... | collective-permute-start | bytes 196616 | tf_op jit(solution)/shard_map/ppermute | solution.py:337
  24.8 0.0 collective-permute-done.3.rest_2_
  24.8 0.6 copy-done.12
  25.4 1.4 %collective-permute-start.8 = (bf16[2,128,128]{2,1,0:T(8,128)(2,1)S(1)}, bf16[2,128,128]{2,1,0:T(8,128)(2,1)}, u32[]{:S(2)}, u32[]{:S(2)}) collective-permute-start(bf16[2,128,128]{2,1,0:T(8,128)(2,1)S(1)} %get-tuple-element.37), channel_id=1, source_target_pairs={{0,12},{1,13},{2,14},{3,15},{4,8},{5,9},{6,10},{7,11},{8,4},{9,5},... | collective-permute-start | bytes 196616 | tf_op jit(solution)/shard_map/ppermute | solution.py:337
  26.9 0.0 all-to-all-done.rest_0_
  26.9 2.5 %shard_map.96.ha = bf16[1152,128]{1,0:T(8,128)(2,1)S(1)} custom-call(s32[2,4,9]{2,1,0:T(4,128)S(1)} %bitcast.7, bf16[2,1152,128]{2,1,0:T(8,128)(2,1)S(1)} %copy-done, bf16[2,4608,128]{2,1,0:T(8,128)(2,1)S(1)} %bitcast.4, bf16[128,128]{1,0:T(8,128)(2,1)} %sw.3, bf16[16,128,128]{2,1,0:T(8,128)(2,1)} %all-to-all-done.rest_0_), custom_call_target="tpu_custom_call" | custom-call | flops 18874368000 | bytes 235929600 | tf_op jit(solution)/shard_map/pallas_call | solution.py:387
  29.4 0.0 collective-permute-done.4.rest_3_
  29.4 1.6 %collective-permute-start.9 = (bf16[1152,128]{1,0:T(8,128)(2,1)S(1)}, bf16[1152,128]{1,0:T(8,128)(2,1)S(1)}, u32[]{:S(2)}, u32[]{:S(2)}) collective-permute-start(bf16[1152,128]{1,0:T(8,128)(2,1)S(1)} %shard_map.96.ha), channel_id=1, source_target_pairs={{0,16},{16,0},{1,17},{17,1},{2,18},{18,2},{3,19},{19,3},{4,20},{20... | collective-permute-start | bytes 884744 | tf_op jit(solution)/shard_map/ppermute | solution.py:406
  31.0 3.8 %collective-permute-done.5.rest_4_ = bf16[2,128,128]{2,1,0:T(8,128)(2,1)} collective-permute-done((bf16[2,128,128]{2,1,0:T(8,128)(2,1)}, bf16[2,128,128]{2,1,0:T(8,128)(2,1)}, u32[]{:S(2)}, u32[]{:S(2)}) %collective-permute-start.5) | collective-permute-done | bytes 65568 | tf_op jit(solution)/shard_map/ppermute | solution.py:337
  34.8 0.5 collective-permute-done.6.rest_5_
  35.3 0.0 collective-permute-done.7.rest_6_
  35.3 0.0 collective-permute-done.8.rest_7_
  35.3 0.0 copy-start.5
  35.3 0.0 copy-start.7
  35.3 0.0 copy-start.9
  35.3 2.7 %shard_map.98.hb = bf16[1152,128]{1,0:T(8,128)(2,1)S(1)} custom-call(s32[2,4,9]{2,1,0:T(4,128)S(1)} %bitcast.8, bf16[2,1152,128]{2,1,0:T(8,128)(2,1)S(1)} %copy-done, bf16[2,4608,128]{2,1,0:T(8,128)(2,1)S(1)} %bitcast.5, bf16[128,128]{1,0:T(8,128)(2,1)} %sw.3, bf16[2,128,128]{2,1,0:T(8,128)(2,1)} %copy-done.6, bf16[2,128,128]{2,1,0:T(8,128)(2,1)} %copy-done.11, ...), custom_call_target="tpu_custom_call" | custom-call | flops 18874368000 | bytes 235929600 | tf_op jit(solution)/shard_map/pallas_call | solution.py:387
  38.0 0.0 collective-permute-done.9.hn
  38.0 0.0 copy-done.4
  38.0 0.0 copy-done.5
  38.0 0.0 copy-done.7
  38.1 3.5 %shard_map.100 = (bf16[16,128,128]{2,1,0:T(8,128)(2,1)}, bf16[2,1152,128]{2,1,0:T(8,128)(2,1)}, bf16[1152,128]{1,0:T(8,128)(2,1)S(1)}, f32[1152,128]{1,0:T(8,128)S(1)}, f32[9,128,128]{2,1,0:T(8,128)S(1)}) custom-call(s32[2,4,9]{2,1,0:T(4,128)S(1)} %bitcast.9, bf16[1152,128]{1,0:T(8,128)(2,1)S(1)} %shard_map.96.ha, bf16[1152,128]{1,0:T(8,128)(2,1)S(1)} %shard_map.98.hb, ...), custom_call_target="tpu_custom_call" | custom-call | flops 98146713600 | bytes 589824000 | tf_op jit(solution)/shard_map/pallas_call | solution.py:416
  41.6 1.6 %collective-permute-start.10 = (bf16[1152,128]{1,0:T(8,128)(2,1)S(1)}, bf16[1152,128]{1,0:T(8,128)(2,1)S(1)}, u32[]{:S(2)}, u32[]{:S(2)}) collective-permute-start(bf16[1152,128]{1,0:T(8,128)(2,1)S(1)} %get-tuple-element.40), channel_id=1, source_target_pairs={{0,16},{16,0},{1,17},{17,1},{2,18},{18,2},{3,19},{19,3},{4,20},{20... | collective-permute-start | bytes 884744 | tf_op jit(solution)/shard_map/ppermute | solution.py:447
  43.1 6.5 %all-to-all-start.1 = ((bf16[16,128,128]{2,1,0:T(8,128)(2,1)}), bf16[16,128,128]{2,1,0:T(8,128)(2,1)S(1)}, u32[]{:S(2)}, u32[]{:S(2)}) async-start(bf16[16,128,128]{2,1,0:T(8,128)(2,1)} %get-tuple-element.51), calls=%async_computation.1 | async-start | bytes 1048576 | tf_op jit(solution)/shard_map/all_to_all | solution.py:331
  49.7 0.1 collective-permute-done.10.partial
  49.7 2.7 %shard_map.101 = (bf16[2,128,128]{2,1,0:T(8,128)(2,1)S(1)}, bf16[2,128,128]{2,1,0:T(8,128)(2,1)S(1)}, bf16[2,128,128]{2,1,0:T(8,128)(2,1)S(1)}, bf16[2,128,128]{...) custom-call(s32[2,4,9]{2,1,0:T(4,128)S(1)} %bitcast.10, ...), custom_call_target="tpu_custom_call" | custom-call | flops 18874368000 | bytes 353894400 | tf_op jit(solution)/shard_map/pallas_call | solution.py:450
  52.4 1.9 %collective-permute-start.11 = (bf16[2,128,128]{2,1,0:T(8,128)(2,1)S(1)}, bf16[2,128,128]{2,1,0:T(8,128)(2,1)S(1)}, u32[]{:S(2)}, u32[]{:S(2)}) collective-permute-start(bf16[2,128,128]{2,1,0:T(8,128)(2,1)S(1)} %get-tuple-element.42), channel_id=1, source_target_pairs={{0,2},{1,3},{2,0},{3,1},{4,6},{5,7},{6,4},{7,5},{8,10},{9,11},{10,... | collective-permute-start | bytes 196616 | tf_op jit(solution)/shard_map/ppermute | solution.py:337
  54.3 2.9 %collective-permute-start.12 = (bf16[2,128,128]{2,1,0:T(8,128)(2,1)S(1)}, bf16[2,128,128]{2,1,0:T(8,128)(2,1)S(1)}, u32[]{:S(2)}, u32[]{:S(2)}) collective-permute-start(bf16[2,128,128]{2,1,0:T(8,128)(2,1)S(1)} %get-tuple-element.43), channel_id=1, source_target_pairs={{0,4},{1,5},{2,6},{3,7},{4,0},{5,1},{6,2},{7,3},{8,12},{9,13},{10,... | collective-permute-start | bytes 196616 | tf_op jit(solution)/shard_map/ppermute | solution.py:337
  57.3 0.0 collective-permute-start.13
  57.3 3.0 %collective-permute-start.14 = (bf16[2,128,128]{2,1,0:T(8,128)(2,1)S(1)}, bf16[2,128,128]{2,1,0:T(8,128)(2,1)S(1)}, u32[]{:S(2)}, u32[]{:S(2)}) collective-permute-start(bf16[2,128,128]{2,1,0:T(8,128)(2,1)S(1)} %get-tuple-element.45), channel_id=1, source_target_pairs={{0,10},{1,11},{2,8},{3,9},{4,14},{5,15},{6,12},{7,13},{8,2},{9,3},... | collective-permute-start | bytes 196616 | tf_op jit(solution)/shard_map/ppermute | solution.py:337
  60.3 0.8 %collective-permute-start.15 = (bf16[2,128,128]{2,1,0:T(8,128)(2,1)S(1)}, bf16[2,128,128]{2,1,0:T(8,128)(2,1)S(1)}, u32[]{:S(2)}, u32[]{:S(2)}) collective-permute-start(bf16[2,128,128]{2,1,0:T(8,128)(2,1)S(1)} %get-tuple-element.46), channel_id=1, source_target_pairs={{0,8},{1,9},{2,10},{3,11},{4,12},{5,13},{6,14},{7,15},{8,0},{9,1},... | collective-permute-start | bytes 196616 | tf_op jit(solution)/shard_map/ppermute | solution.py:337
  61.1 0.0 collective-permute-done.11.rest_0_.refs_1_
  61.1 2.3 %collective-permute-start.16 = (bf16[2,128,128]{2,1,0:T(8,128)(2,1)S(1)}, bf16[2,128,128]{2,1,0:T(8,128)(2,1)S(1)}, u32[]{:S(2)}, u32[]{:S(2)}) collective-permute-start(bf16[2,128,128]{2,1,0:T(8,128)(2,1)S(1)} %get-tuple-element.47), channel_id=1, source_target_pairs={{0,14},{1,15},{2,12},{3,13},{4,10},{5,11},{6,8},{7,9},{8,6},{9,7},... | collective-permute-start | bytes 196616 | tf_op jit(solution)/shard_map/ppermute | solution.py:337
  63.5 0.0 collective-permute-done.12.rest_1_.refs_2_
  63.5 1.5 %collective-permute-start.17 = (bf16[2,128,128]{2,1,0:T(8,128)(2,1)S(1)}, bf16[2,128,128]{2,1,0:T(8,128)(2,1)S(1)}, u32[]{:S(2)}, u32[]{:S(2)}) collective-permute-start(bf16[2,128,128]{2,1,0:T(8,128)(2,1)S(1)} %get-tuple-element.48), channel_id=1, source_target_pairs={{0,12},{1,13},{2,14},{3,15},{4,8},{5,9},{6,10},{7,11},{8,4},{9,5},... | collective-permute-start | bytes 196616 | tf_op jit(solution)/shard_map/ppermute | solution.py:337
  65.0 0.0 collective-permute-done.13.rest_2_.refs_3_
  65.0 8.4 %collective-permute-done.14.rest_3_.refs_4_ = bf16[2,128,128]{2,1,0:T(8,128)(2,1)S(1)} collective-permute-done((bf16[2,128,128]{2,1,0:T(8,128)(2,1)S(1)}, bf16[2,128,128]{2,1,0:T(8,128)(2,1)S(1)}, u32[]{:S(2)}, u32[]{:S(2)}) %collective-permute-start.14) | collective-permute-done | bytes 65568 | tf_op jit(solution)/shard_map/ppermute | solution.py:337
  73.3 0.5 collective-permute-done.15.rest_4_.refs_5_
  73.8 0.0 collective-permute-done.16.rest_5_.refs_6_
  73.8 0.0 collective-permute-done.17.rest_6_.refs_7_
  73.8 0.4 shard_map.103
  74.3 0.1 collective-permute-start.18
  74.4 0.7 shard_map.102.part
  75.1 0.0 all-to-all-done.1.arrived
  75.1 0.9 %shard_map.104.outer = bf16[1152,128]{1,0:T(8,128)(2,1)S(1)} custom-call(s32[2,1,16]{2,1,0:T(1,128)S(1)} %copy-done.2, f32[9,128,128]{2,1,0:T(8,128)S(1)} %get-tuple-element.50.local, bf16[16,128,128]{2,1,0:T(8,128)(2,1)S(1)} %all-to-all-done.1.arrived), custom_call_target="tpu_custom_call" | custom-call | flops 26214400 | bytes 235929600 | tf_op jit(solution)/shard_map/pallas_call | solution.py:475
  76.0 0.0 collective-permute-done.18.swapped
  76.0 1.6 %shard_map.105 = bf16[2,1152,128]{2,1,0:T(8,128)(2,1)} custom-call(s32[2,1,16]{2,1,0:T(1,128)S(1)} %copy-done.2, f32[9,128,128]{2,1,0:T(8,128)S(1)} %shard_map.102.part, bf16[8,128,128]{2,1,0:T(8,128)(2,1)S(1)} %collective-permute-done.18.swapped, bf16[1152,128]{1,0:T(8,128)(2,1)S(1)} %shard_map.104.outer), custom_call_target="tpu_custom_call" | custom-call | flops 26214400 | bytes 235929600 | tf_op jit(solution)/shard_map/pallas_call | solution.py:490
  (15 shorter events, 0.0 us)
Async XLA Ops:
  0.6 26.2 %copy-start = (bf16[2,1152,128]{2,1,0:T(8,128)(2,1)S(1)}, bf16[2,1152,128]{2,1,0:T(8,128)(2,1)}, u32[]{:S(2)}) copy-start(bf16[2,1152,128]{2,1,0:T(8,128)(2,1)} %feats.7) | copy-start | bytes 1769476
  0.6 16.1 %copy-start.1 = (bf16[3,128,256]{2,1,0:T(8,128)(2,1)S(1)}, bf16[3,128,256]{2,1,0:T(8,128)(2,1)}, u32[]{:S(2)}) copy-start(bf16[3,128,256]{2,1,0:T(8,128)(2,1)} %tw.3) | copy-start | bytes 589828
  0.7 26.2 %copy-start.8 = (s32[2,9,4]{1,2,0:T(4,128)S(1)}, s32[2,9,4]{1,2,0:T(4,128)}, u32[]{:S(2)}) copy-start(s32[2,9,4]{1,2,0:T(4,128)} %param.11) | copy-start | bytes 868
  0.7 26.2 %copy-start.3 = (bf16[2,1152,4,128]{3,2,1,0:T(4,128)(2,1)S(1)}, bf16[2,1152,4,128]{3,2,1,0:T(4,128)(2,1)}, u32[]{:S(2)}) copy-start(bf16[2,1152,4,128]{3,2,1,0:T(4,128)(2,1)} %param.10) | copy-start | bytes 7077892
  0.7 2.9 %collective-permute-start.1 = (bf16[2,1152,128]{2,1,0:T(8,128)(2,1)}, bf16[2,1152,128]{2,1,0:T(8,128)(2,1)}, u32[]{:S(2)}, u32[]{:S(2)}) collective-permute-start(bf16[2,1152,128]{2,1,0:T(8,128)(2,1)} %feats.7), channel_id=1, source_target_pairs={{0,1},{1,0},{2,3},{3,2},{4,5},{5,4},{6,7},{7,6},{8,9},{9,8},{10,11... | collective-permute-start | bytes 1769480 | tf_op jit(solution)/shard_map/ppermute | solution.py:328
  1.2 2.4 %collective-permute-start = (s32[2,1,16]{2,1,0:T(1,128)}, s32[2,1,16]{2,1,0:T(1,128)S(1)}, u32[]{:S(2)}, u32[]{:S(2)}) collective-permute-start(s32[2,1,16]{2,1,0:T(1,128)} %send.5), channel_id=1, source_target_pairs={{0,1},{1,0},{2,3},{3,2},{4,5},{5,4},{6,7},{7,6},{8,9},{9,8},{10,11... | collective-permute-start | bytes 392 | tf_op jit(solution)/shard_map/ppermute | solution.py:328
  3.6 7.4 %copy-start.10 = (s32[2,1,16]{2,1,0:T(1,128)}, s32[2,1,16]{2,1,0:T(1,128)S(1)}, u32[]{:S(2)}) copy-start(s32[2,1,16]{2,1,0:T(1,128)S(1)} %collective-permute-done.partner_lists) | copy-start | bytes 388
  3.6 23.3 %all-to-all-start = ((bf16[16,128,128]{2,1,0:T(8,128)(2,1)}), bf16[16,128,128]{2,1,0:T(8,128)(2,1)}, u32[]{:S(2)}, u32[]{:S(2)}) async-start(bf16[16,128,128]{2,1,0:T(8,128)(2,1)} %shard_map.95), calls=%async_computation | async-start | bytes 1048576 | tf_op jit(solution)/shard_map/all_to_all | solution.py:331
  12.8 0.6 copy-start.6
  13.4 7.9 %collective-permute-start.2 = (bf16[2,128,128]{2,1,0:T(8,128)(2,1)S(1)}, bf16[2,128,128]{2,1,0:T(8,128)(2,1)S(1)}, u32[]{:S(2)}, u32[]{:S(2)}) collective-permute-start(bf16[2,128,128]{2,1,0:T(8,128)(2,1)S(1)} %get-tuple-element.31), channel_id=1, source_target_pairs={{0,2},{1,3},{2,0},{3,1},{4,6},{5,7},{6,4},{7,5},{8,10},{9,11},{10,... | collective-permute-start | bytes 196616 | tf_op jit(solution)/shard_map/ppermute | solution.py:337
  15.3 9.5 %collective-permute-start.3 = (bf16[2,128,128]{2,1,0:T(8,128)(2,1)S(1)}, bf16[2,128,128]{2,1,0:T(8,128)(2,1)S(1)}, u32[]{:S(2)}, u32[]{:S(2)}) collective-permute-start(bf16[2,128,128]{2,1,0:T(8,128)(2,1)S(1)} %get-tuple-element.32), channel_id=1, source_target_pairs={{0,6},{1,7},{2,4},{3,5},{4,2},{5,3},{6,0},{7,1},{8,14},{9,15},{10,... | collective-permute-start | bytes 196616 | tf_op jit(solution)/shard_map/ppermute | solution.py:337
  16.9 12.5 %collective-permute-start.4 = (bf16[2,128,128]{2,1,0:T(8,128)(2,1)}, bf16[2,128,128]{2,1,0:T(8,128)(2,1)}, u32[]{:S(2)}, u32[]{:S(2)}) collective-permute-start(bf16[2,128,128]{2,1,0:T(8,128)(2,1)} %get-tuple-element.33), channel_id=1, source_target_pairs={{0,4},{1,5},{2,6},{3,7},{4,0},{5,1},{6,2},{7,3},{8,12},{9,13},{10,... | collective-permute-start | bytes 196616 | tf_op jit(solution)/shard_map/ppermute | solution.py:337
  17.1 17.6 %collective-permute-start.5 = (bf16[2,128,128]{2,1,0:T(8,128)(2,1)}, bf16[2,128,128]{2,1,0:T(8,128)(2,1)}, u32[]{:S(2)}, u32[]{:S(2)}) collective-permute-start(bf16[2,128,128]{2,1,0:T(8,128)(2,1)} %get-tuple-element.34), channel_id=1, source_target_pairs={{0,10},{1,11},{2,8},{3,9},{4,14},{5,15},{6,12},{7,13},{8,2},{9,3},... | collective-permute-start | bytes 196616 | tf_op jit(solution)/shard_map/ppermute | solution.py:337
  20.8 14.4 %collective-permute-start.6 = (bf16[2,128,128]{2,1,0:T(8,128)(2,1)S(1)}, bf16[2,128,128]{2,1,0:T(8,128)(2,1)}, u32[]{:S(2)}, u32[]{:S(2)}) collective-permute-start(bf16[2,128,128]{2,1,0:T(8,128)(2,1)S(1)} %get-tuple-element.35), channel_id=1, source_target_pairs={{0,8},{1,9},{2,10},{3,11},{4,12},{5,13},{6,14},{7,15},{8,0},{9,1},... | collective-permute-start | bytes 196616 | tf_op jit(solution)/shard_map/ppermute | solution.py:337
  21.4 3.4 %copy-start.11 = (bf16[2,128,128]{2,1,0:T(8,128)(2,1)}, bf16[2,128,128]{2,1,0:T(8,128)(2,1)S(1)}, u32[]{:S(2)}) copy-start(bf16[2,128,128]{2,1,0:T(8,128)(2,1)S(1)} %collective-permute-done.2.rest_1_) | copy-start | bytes 196612
  21.4 13.9 %collective-permute-start.7 = (bf16[2,128,128]{2,1,0:T(8,128)(2,1)S(1)}, bf16[2,128,128]{2,1,0:T(8,128)(2,1)}, u32[]{:S(2)}, u32[]{:S(2)}) collective-permute-start(bf16[2,128,128]{2,1,0:T(8,128)(2,1)S(1)} %get-tuple-element.36), channel_id=1, source_target_pairs={{0,14},{1,15},{2,12},{3,13},{4,10},{5,11},{6,8},{7,9},{8,6},{9,7},... | collective-permute-start | bytes 196616 | tf_op jit(solution)/shard_map/ppermute | solution.py:337
  24.8 0.6 copy-start.12
  25.4 9.8 %collective-permute-start.8 = (bf16[2,128,128]{2,1,0:T(8,128)(2,1)S(1)}, bf16[2,128,128]{2,1,0:T(8,128)(2,1)}, u32[]{:S(2)}, u32[]{:S(2)}) collective-permute-start(bf16[2,128,128]{2,1,0:T(8,128)(2,1)S(1)} %get-tuple-element.37), channel_id=1, source_target_pairs={{0,12},{1,13},{2,14},{3,15},{4,8},{5,9},{6,10},{7,11},{8,4},{9,5},... | collective-permute-start | bytes 196616 | tf_op jit(solution)/shard_map/ppermute | solution.py:337
  29.4 8.6 %collective-permute-start.9 = (bf16[1152,128]{1,0:T(8,128)(2,1)S(1)}, bf16[1152,128]{1,0:T(8,128)(2,1)S(1)}, u32[]{:S(2)}, u32[]{:S(2)}) collective-permute-start(bf16[1152,128]{1,0:T(8,128)(2,1)S(1)} %shard_map.96.ha), channel_id=1, source_target_pairs={{0,16},{16,0},{1,17},{17,1},{2,18},{18,2},{3,19},{19,3},{4,20},{20... | collective-permute-start | bytes 884744 | tf_op jit(solution)/shard_map/ppermute | solution.py:406
  35.3 2.7 %copy-start.4 = (bf16[2,1152,4,128]{3,2,1,0:T(4,128)(2,1)S(1)}, bf16[2,1152,4,128]{3,2,1,0:T(4,128)(2,1)}, u32[]{:S(2)}) copy-start(bf16[2,1152,4,128]{3,2,1,0:T(4,128)(2,1)} %param.10) | copy-start | bytes 7077892
  35.3 2.8 %copy-start.5 = (bf16[2,1152,128]{2,1,0:T(8,128)(2,1)S(1)}, bf16[2,1152,128]{2,1,0:T(8,128)(2,1)}, u32[]{:S(2)}) copy-start(bf16[2,1152,128]{2,1,0:T(8,128)(2,1)} %cot.1) | copy-start | bytes 1769476
  35.3 2.8 %copy-start.7 = (bf16[128,128]{1,0:T(8,128)(2,1)S(1)}, bf16[128,128]{1,0:T(8,128)(2,1)}, u32[]{:S(2)}) copy-start(bf16[128,128]{1,0:T(8,128)(2,1)} %sw.3) | copy-start | bytes 98308
  35.3 2.8 %copy-start.9 = (f32[256]{0:T(256)S(1)}, f32[256]{0:T(256)}, u32[]{:S(2)}) copy-start(f32[256]{0:T(256)} %param.15) | copy-start | bytes 3076
  41.6 8.1 %collective-permute-start.10 = (bf16[1152,128]{1,0:T(8,128)(2,1)S(1)}, bf16[1152,128]{1,0:T(8,128)(2,1)S(1)}, u32[]{:S(2)}, u32[]{:S(2)}) collective-permute-start(bf16[1152,128]{1,0:T(8,128)(2,1)S(1)} %get-tuple-element.40), channel_id=1, source_target_pairs={{0,16},{16,0},{1,17},{17,1},{2,18},{18,2},{3,19},{19,3},{4,20},{20... | collective-permute-start | bytes 884744 | tf_op jit(solution)/shard_map/ppermute | solution.py:447
  43.1 31.9 %all-to-all-start.1 = ((bf16[16,128,128]{2,1,0:T(8,128)(2,1)}), bf16[16,128,128]{2,1,0:T(8,128)(2,1)S(1)}, u32[]{:S(2)}, u32[]{:S(2)}) async-start(bf16[16,128,128]{2,1,0:T(8,128)(2,1)} %get-tuple-element.51), calls=%async_computation.1 | async-start | bytes 1048576 | tf_op jit(solution)/shard_map/all_to_all | solution.py:331
  49.7 24.6 %copy-start.2 = (s32[2,1,16]{2,1,0:T(1,128)S(1)}, s32[2,1,16]{2,1,0:T(1,128)}, u32[]{:S(2)}) copy-start(s32[2,1,16]{2,1,0:T(1,128)} %send.5) | copy-start | bytes 388
  52.4 8.7 %collective-permute-start.11 = (bf16[2,128,128]{2,1,0:T(8,128)(2,1)S(1)}, bf16[2,128,128]{2,1,0:T(8,128)(2,1)S(1)}, u32[]{:S(2)}, u32[]{:S(2)}) collective-permute-start(bf16[2,128,128]{2,1,0:T(8,128)(2,1)S(1)} %get-tuple-element.42), channel_id=1, source_target_pairs={{0,2},{1,3},{2,0},{3,1},{4,6},{5,7},{6,4},{7,5},{8,10},{9,11},{10,... | collective-permute-start | bytes 196616 | tf_op jit(solution)/shard_map/ppermute | solution.py:337
  54.3 9.1 %collective-permute-start.12 = (bf16[2,128,128]{2,1,0:T(8,128)(2,1)S(1)}, bf16[2,128,128]{2,1,0:T(8,128)(2,1)S(1)}, u32[]{:S(2)}, u32[]{:S(2)}) collective-permute-start(bf16[2,128,128]{2,1,0:T(8,128)(2,1)S(1)} %get-tuple-element.43), channel_id=1, source_target_pairs={{0,4},{1,5},{2,6},{3,7},{4,0},{5,1},{6,2},{7,3},{8,12},{9,13},{10,... | collective-permute-start | bytes 196616 | tf_op jit(solution)/shard_map/ppermute | solution.py:337
  57.3 7.7 %collective-permute-start.13 = (bf16[2,128,128]{2,1,0:T(8,128)(2,1)S(1)}, bf16[2,128,128]{2,1,0:T(8,128)(2,1)S(1)}, u32[]{:S(2)}, u32[]{:S(2)}) collective-permute-start(bf16[2,128,128]{2,1,0:T(8,128)(2,1)S(1)} %get-tuple-element.44), channel_id=1, source_target_pairs={{0,6},{1,7},{2,4},{3,5},{4,2},{5,3},{6,0},{7,1},{8,14},{9,15},{10,... | collective-permute-start | bytes 196616 | tf_op jit(solution)/shard_map/ppermute | solution.py:337
  57.3 16.0 %collective-permute-start.14 = (bf16[2,128,128]{2,1,0:T(8,128)(2,1)S(1)}, bf16[2,128,128]{2,1,0:T(8,128)(2,1)S(1)}, u32[]{:S(2)}, u32[]{:S(2)}) collective-permute-start(bf16[2,128,128]{2,1,0:T(8,128)(2,1)S(1)} %get-tuple-element.45), channel_id=1, source_target_pairs={{0,10},{1,11},{2,8},{3,9},{4,14},{5,15},{6,12},{7,13},{8,2},{9,3},... | collective-permute-start | bytes 196616 | tf_op jit(solution)/shard_map/ppermute | solution.py:337
  60.3 13.5 %collective-permute-start.15 = (bf16[2,128,128]{2,1,0:T(8,128)(2,1)S(1)}, bf16[2,128,128]{2,1,0:T(8,128)(2,1)S(1)}, u32[]{:S(2)}, u32[]{:S(2)}) collective-permute-start(bf16[2,128,128]{2,1,0:T(8,128)(2,1)S(1)} %get-tuple-element.46), channel_id=1, source_target_pairs={{0,8},{1,9},{2,10},{3,11},{4,12},{5,13},{6,14},{7,15},{8,0},{9,1},... | collective-permute-start | bytes 196616 | tf_op jit(solution)/shard_map/ppermute | solution.py:337
  61.1 12.7 %collective-permute-start.16 = (bf16[2,128,128]{2,1,0:T(8,128)(2,1)S(1)}, bf16[2,128,128]{2,1,0:T(8,128)(2,1)S(1)}, u32[]{:S(2)}, u32[]{:S(2)}) collective-permute-start(bf16[2,128,128]{2,1,0:T(8,128)(2,1)S(1)} %get-tuple-element.47), channel_id=1, source_target_pairs={{0,14},{1,15},{2,12},{3,13},{4,10},{5,11},{6,8},{7,9},{8,6},{9,7},... | collective-permute-start | bytes 196616 | tf_op jit(solution)/shard_map/ppermute | solution.py:337
  63.5 10.4 %collective-permute-start.17 = (bf16[2,128,128]{2,1,0:T(8,128)(2,1)S(1)}, bf16[2,128,128]{2,1,0:T(8,128)(2,1)S(1)}, u32[]{:S(2)}, u32[]{:S(2)}) collective-permute-start(bf16[2,128,128]{2,1,0:T(8,128)(2,1)S(1)} %get-tuple-element.48), channel_id=1, source_target_pairs={{0,12},{1,13},{2,14},{3,15},{4,8},{5,9},{6,10},{7,11},{8,4},{9,5},... | collective-permute-start | bytes 196616 | tf_op jit(solution)/shard_map/ppermute | solution.py:337
  74.3 1.7 %collective-permute-start.18 = (bf16[8,128,128]{2,1,0:T(8,128)(2,1)S(1)}, bf16[8,128,128]{2,1,0:T(8,128)(2,1)S(1)}, u32[]{:S(2)}, u32[]{:S(2)}) collective-permute-start(bf16[8,128,128]{2,1,0:T(8,128)(2,1)S(1)} %shard_map.103), channel_id=1, source_target_pairs={{0,1},{1,0},{2,3},{3,2},{4,5},{5,4},{6,7},{7,6},{8,9},{9,8},{10,11... | collective-permute-start | bytes 786440 | tf_op jit(solution)/shard_map/ppermute | solution.py:328
